TPU v7x, 256 devices: a whole 4x4x8 slice. The times are simulated.
256 devices in a mesh: col: 8 (over z), row: 32 (over y, x, core).
Axes of the slice: x: 4, y: 4, z: 8, core: 2. Of those that a mesh axis runs over, the one named last changes fastest.
Arguments:
- queries: bfloat16 [262144, 256], P(('col', 'row')), may hold values from -6 to 6
- keys: bfloat16 [262144, 256], P(('col', 'row')), may hold values from -6 to 6
- values: bfloat16 [262144, 256], P(('col', 'row')), may hold values from -6 to 6
- out_grad: bfloat16 [262144, 256], P(('col', 'row')), may hold values from -6 to 6
- weight_table: float32 [64, 2, 21], replicated, may hold values from 0.25 to 2
- profile: int32 [262144], P(('col', 'row')), may hold values from 0 to 63
Outputs:
- output: float32 [262144, 256], P(('col', 'row'))
- query_grad: float32 [262144, 256], P(('col', 'row'))
- key_grad: float32 [262144, 256], P(('col', 'row'))
- value_grad: float32 [262144, 256], P(('col', 'row'))
All inputs are finite; a program needn't handle non-finite values.
Results may differ from a plain program's by a relative error of at most 0.0034.
Values sent between devices are 32-bit elements; how exact they have to be, the bound alone decides.
No kernel may reach another device: no remote copies, remote signals or barrier semaphores. Data moves between devices by JAX's collectives and lax.ppermute only.
A program may use at most 128 MiB of HBM per device.

v0:
```python
import functools
import math

import jax
import jax.numpy as jnp
from jax import lax
from jax.experimental import pallas as pl
from jax.experimental.pallas import tpu as pltpu
from jax.sharding import PartitionSpec as P


F32 = jnp.float32
BF16 = jnp.bfloat16
AXES = ("col", "row")
BLOCK = 256
SMALL = 128
STRIDE = 64
ROOM = 16 << 20
VMEM = pl.BlockSpec(memory_space=pltpu.VMEM)
HBM = pl.BlockSpec(memory_space=pltpu.HBM)


def contract(a, b, dim_a, dim_b):
    return lax.dot_general(
        a, b, (((dim_a,), (dim_b,)), ((), ())), preferred_element_type=F32
    )


def outside(*arrays):
    return [pltpu.with_memory_space_constraint(x, pltpu.HBM) for x in arrays]


def call(kernel, out_shape, flops, moved, **rest):
    return pl.pallas_call(
        kernel,
        out_shape=out_shape,
        cost_estimate=pl.CostEstimate(flops=flops, bytes_accessed=moved, transcendentals=0),
        compiler_params=pltpu.CompilerParams(vmem_limit_bytes=ROOM),
        **rest,
    )


def level_weights(table, profile_row, width):
    levels, heads, profiles = table.shape
    places = lax.broadcasted_iota(jnp.int32, (profiles, profile_row.shape[1]), 0)
    onehot = jnp.where(places == profile_row, 1.0, 0.0).astype(BF16)
    blank = jnp.zeros((STRIDE - levels, profiles), F32)
    rows = []
    for h in range(heads):
        rows += [table[:, h, :], blank]
    rows = jnp.concatenate(rows, axis=0)
    high = rows.astype(BF16)
    rest = rows - high.astype(F32)
    middle = rest.astype(BF16)
    low = (rest - middle.astype(F32)).astype(BF16)
    picked = (contract(onehot, high, 0, 1) + contract(onehot, middle, 0, 1)) + contract(
        onehot, low, 0, 1
    )
    depth = (lax.broadcasted_iota(jnp.int32, (1, heads * STRIDE), 1) & (STRIDE - 1)).astype(F32)
    return picked * (jnp.exp2(-0.5 * depth) / math.sqrt(width))


def weighted(x, w, h, level):
    at = h * STRIDE + level
    return (x.astype(F32) * w[:, at : at + 1]).astype(BF16)


def first_kernel(
    top, width, heads, profile_in, table_in, q_in, k_in, v_in, g_in, w_out, ends_out,
    profile, table, q, k, v, g, arrived,
):
    fetches = [
        pltpu.make_async_copy(source, target, arrived.at[n])
        for n, (source, target) in enumerate(
            (
                (profile_in, profile),
                (table_in, table),
                (k_in, k),
                (v_in, v),
                (q_in, q),
                (g_in, g),
            )
        )
    ]
    for fetch in fetches:
        fetch.start()
    fetches[0].wait()
    fetches[1].wait()
    w = level_weights(table, profile[...], width)
    w_out[...] = w
    fetches[2].wait()
    fetches[3].wait()
    for h in range(heads):
        lanes = slice(h * width, (h + 1) * width)
        ends_out[0, h] = contract(k[:, lanes], v[:, lanes], 0, 0)
    fetches[4].wait()
    fetches[5].wait()
    for h in range(heads):
        lanes = slice(h * width, (h + 1) * width)
        ends_out[1, h] = contract(g[:, lanes], weighted(q[:, lanes], w, h, top), 0, 0)


def second_kernel(first_far, width, heads, far, w, q, g, low_out, middle_out):
    for h in range(heads):
        lanes = slice(h * width, (h + 1) * width)
        stack = [weighted(q[:, lanes], w, h, first_far + j) for j in range(far - 1)]
        states = contract(g[:, lanes], jnp.concatenate(stack, axis=1), 0, 0)
        low_out[h] = states[:, :width]
        for j in range(1, far - 1):
            middle_out[j - 1, h] = states[:, j * width : (j + 1) * width]


def block_mask(w, levels, causal):
    parts = []
    for i in range(BLOCK // SMALL):
        rows = w[i * SMALL : (i + 1) * SMALL]
        tri = jnp.broadcast_to(rows[:, 0:1], (SMALL, SMALL))
        for l in range(1, SMALL.bit_length()):
            tri = jnp.where(levels >= l, rows[:, l : l + 1], tri)
        line = []
        for j in range(BLOCK // SMALL):
            if j > i:
                line.append(jnp.zeros((SMALL, SMALL), F32))
            elif j == i:
                line.append(jnp.where(causal, tri, 0.0))
            else:
                l = SMALL.bit_length() - 1 + (i ^ j).bit_length()
                line.append(jnp.broadcast_to(rows[:, l : l + 1], (SMALL, SMALL)))
        parts.append(jnp.concatenate(line, axis=1))
    return jnp.concatenate(parts, axis=0)


def merge_kernel(count, place, own_part, from_other, *sums):
    own = place[0]
    for l in range(count):
        taken = ((own & 1) == 1) & ((own >> l + 1 & 1) == 1)
        sums[l][...] = jnp.where(taken, own_part[l] + from_other[l], 0.0)


def tile_kernel(i, width, heads, depth, first_far, place, w, q, k, v, g, ends, out, dq, dk, dv):
    tokens = q.shape[0]
    on_first = (place[0] & 1) == 0
    places_t = lax.broadcasted_iota(jnp.int32, (SMALL, SMALL), 0)
    places_s = lax.broadcasted_iota(jnp.int32, (SMALL, SMALL), 1)
    differ = places_t ^ places_s
    levels = jnp.zeros((SMALL, SMALL), jnp.int32)
    for p in range(SMALL.bit_length() - 1):
        levels = levels + jnp.where(differ >= 1 << p, 1, 0)
    causal = places_s <= places_t
    rows = slice(i * BLOCK, (i + 1) * BLOCK)
    for h in range(heads):
        lanes = slice(h * width, (h + 1) * width)
        first = h * STRIDE
        qb, kb, vb, gb = q[rows, lanes], k[rows, lanes], v[rows, lanes], g[rows, lanes]
        mask = block_mask(w[rows, first : first + depth], levels, causal)
        probs = (contract(qb, kb, 1, 1) * mask).astype(BF16)
        grads = (contract(gb, vb, 1, 1) * mask).astype(BF16)
        state = jnp.where(on_first, 0.0, ends[0, h]).astype(BF16)
        scale = w[rows, first + first_far : first + first_far + 1]
        o = contract(probs, vb, 1, 0) + scale * contract(qb, state, 1, 0)
        d = contract(grads, kb, 1, 0) + scale * contract(gb, state, 1, 1)
        s = contract(grads, qb, 0, 0)
        e = contract(probs, gb, 0, 0)
        size = BLOCK
        while size < tokens:
            group = i * BLOCK // size
            sibling = slice((group ^ 1) * size, ((group ^ 1) + 1) * size)
            at = first + size.bit_length()
            if group & 1:
                scale = w[rows, at : at + 1]
                state = contract(k[sibling, lanes], v[sibling, lanes], 0, 0).astype(BF16)
                o = o + scale * contract(qb, state, 1, 0)
                d = d + scale * contract(gb, state, 1, 1)
            else:
                scaled = (q[sibling, lanes].astype(F32) * w[sibling, at : at + 1]).astype(BF16)
                pulled = contract(g[sibling, lanes], scaled, 0, 0).astype(BF16)
                s = s + contract(vb, pulled, 1, 0)
                e = e + contract(kb, pulled, 1, 1)
            size *= 2
        out[:, lanes] = o
        dq[:, lanes] = d
        dk[:, lanes] = s
        dv[:, lanes] = e


def far_kernel(
    width, heads, count, first_far, place, w, q, g, stacked, handed, *refs
):
    own = place[0]
    on_first = (own & 1) == 0
    local, (out, dq, near, arrived) = refs[:-4], refs[-4:]
    fetches = [pltpu.make_async_copy(part, near.at[n], arrived.at[n]) for n, part in enumerate(local)]
    for fetch in fetches:
        fetch.start()
    states = []
    for h in range(heads):
        of_head = []
        for j in range(1, count + 1):
            state = jnp.where(on_first, stacked[j - 1, h], handed[j - 1, h])
            of_head.append(jnp.where((own >> j & 1) == 1, state, 0.0).astype(BF16))
        states.append((jnp.concatenate(of_head, axis=0), jnp.concatenate(of_head, axis=1)))
    for i in range(q.shape[0] // BLOCK):
        rows = slice(i * BLOCK, (i + 1) * BLOCK)
        fetches[2 * i].wait()
        fetches[2 * i + 1].wait()
        for h in range(heads):
            lanes = slice(h * width, (h + 1) * width)
            scaled_q = [weighted(q[rows, lanes], w[rows, :], h, first_far + j) for j in range(1, count + 1)]
            scaled_g = [weighted(g[rows, lanes], w[rows, :], h, first_far + j) for j in range(1, count + 1)]
            tall, broad = states[h]
            o = contract(jnp.concatenate(scaled_q, axis=1), tall, 1, 0)
            d = contract(jnp.concatenate(scaled_g, axis=1), broad, 1, 1)
            out[rows, lanes] = near[2 * i, :, lanes] + o
            dq[rows, lanes] = near[2 * i + 1, :, lanes] + d


def last_kernel(
    width, heads, far, first_far, place, w, q, k, v, g, alone, top, alone_in, final, carried,
    far_out, far_dq, *refs,
):
    own = place[0]
    on_first = (own & 1) == 0
    local, (out, dq, dk, dv, near, arrived) = refs[:-6], refs[-6:]
    step = pl.program_id(0)
    fetches = [pltpu.make_async_copy(part, near.at[n], arrived.at[n]) for n, part in enumerate(local)]

    @pl.when(step == 0)
    def _():
        for fetch in fetches:
            fetch.start()

    for i in range(q.shape[0] // BLOCK):

        @pl.when(step == i)
        def _(i=i):
            rows = slice(i * BLOCK, (i + 1) * BLOCK)
            sums = []
            for h in range(heads):
                lanes = slice(h * width, (h + 1) * width)
                pair = []
                for j, here, there in ((far - 2, alone, alone_in), (far - 1, top, final)):
                    state = jnp.where(on_first, here[h], there[h])
                    pair.append(jnp.where((own >> j & 1) == 1, state, 0.0).astype(BF16))
                pulled = jnp.where(on_first, final[h], carried[h]).astype(BF16)
                scaled_q = [weighted(q[rows, lanes], w[rows, :], h, first_far + j) for j in (far - 2, far - 1)]
                scaled_g = [weighted(g[rows, lanes], w[rows, :], h, first_far + j) for j in (far - 2, far - 1)]
                o = contract(jnp.concatenate(scaled_q, axis=1), jnp.concatenate(pair, axis=0), 1, 0)
                d = contract(jnp.concatenate(scaled_g, axis=1), jnp.concatenate(pair, axis=1), 1, 1)
                out[:, lanes] = far_out[rows, lanes] + o
                dq[:, lanes] = far_dq[rows, lanes] + d
                sums.append((contract(v[rows, lanes], pulled, 1, 0), contract(k[rows, lanes], pulled, 1, 1)))
            fetches[2 * i].wait()
            fetches[2 * i + 1].wait()
            for h in range(heads):
                lanes = slice(h * width, (h + 1) * width)
                dk[:, lanes] = near[2 * i, :, lanes] + sums[h][0]
                dv[:, lanes] = near[2 * i + 1, :, lanes] + sums[h][1]


def links(row_bits, col_bits):
    steps = []
    place = 1
    while place < row_bits:
        steps.append(1 << place)
        if place + 1 < row_bits:
            steps.append(3 << place)
        place += 2
    for bit in range(col_bits):
        if bit == col_bits - 1 and bit > 0:
            steps.append(((1 << col_bits) - 1) << row_bits)
        else:
            steps.append(1 << row_bits + bit)
    return steps


def tie(*trees):
    return lax.optimization_barrier(trees)


def shards(row_size, col_size, queries, keys, values, out_grad, weight_table, profile):
    tokens, columns = queries.shape
    _, heads, depth = weight_table.shape
    width = columns // heads
    row_bits = row_size.bit_length() - 1
    col_bits = col_size.bit_length() - 1
    far = row_bits + col_bits
    first_far = tokens.bit_length()
    devices = row_size * col_size
    own = lax.axis_index("col") * row_size + lax.axis_index("row")
    core = own & 1
    on_first = core == 0
    profile_row = profile.reshape(1, tokens)
    table = jnp.transpose(weight_table, (2, 1, 0))

    def full(shape, kind=F32):
        return jax.ShapeDtypeStruct(shape, kind)

    square = (heads, width, width)
    unit = tokens * width * width * heads * 2
    array = tokens * columns * 2
    exchange = [(i, i ^ 1) for i in range(devices)]

    weights, ends = call(
        functools.partial(first_kernel, first_far + far - 1, width, heads),
        (full((tokens, heads * STRIDE)), full((2,) + square)),
        3 * unit,
        4 * array,
        in_specs=[HBM] * 6,
        out_specs=[VMEM] * 2,
        scratch_shapes=[
            pltpu.VMEM(profile_row.shape, jnp.int32),
            pltpu.VMEM(table.shape, F32),
        ]
        + [pltpu.VMEM((tokens, columns), BF16)] * 4
        + [pltpu.SemaphoreType.DMA((6,))],
    )(*outside(profile_row, table, queries, keys, values, out_grad))
    other = lax.ppermute(ends, AXES, exchange)

    def second(w, q, g):
        return call(
            functools.partial(second_kernel, first_far, width, heads, far),
            (full(square), full((far - 2,) + square)),
            far * unit,
            4 * array,
            in_specs=[VMEM] * 3,
        )(w, q, g)

    smem = pl.BlockSpec(memory_space=pltpu.SMEM)
    place = own.reshape(1).astype(jnp.int32)
    blocks = tokens // BLOCK

    def tile(i, *operands):
        return call(
            functools.partial(tile_kernel, i, width, heads, depth, first_far),
            [full((BLOCK, columns))] * 4,
            20 * BLOCK * BLOCK * columns,
            6 * array,
            in_specs=[smem] + [VMEM] * 5 + [pl.BlockSpec()],
        )(place, *operands)

    low_grads, middle = second(weights, queries, out_grad)
    other_middle = lax.ppermute(middle, AXES, exchange)

    def merge(own_part, from_other):
        return call(
            functools.partial(merge_kernel, far - 2),
            [full(square)] * (far - 2),
            far * width * width,
            array,
            in_specs=[smem] + [pl.BlockSpec()] * 2,
            out_specs=[VMEM] * (far - 2),
        )(place, own_part, from_other)

    steps = links(row_bits, col_bits)
    rounds = len(steps)
    carried = jnp.where(on_first, ends[0] + other[0], 0.0)
    received = []
    local = []
    for r in range(1, rounds + 1):
        if r == 1:
            is_upper = (core == 1) & ((own >> far - 1 & 1) == 1)
            send = carried + jnp.where(is_upper, ends[1] + other[1], 0.0)
            carried, send = tie(carried, send)
        else:
            send = carried + sums[far - r - 1]
        pairs = [
            (i, i ^ (steps[rounds - r] if i & 1 else steps[r - 1])) for i in range(devices)
        ]
        work, operands = None, ()
        if r == 1:
            work, operands = merge, (middle, other_middle)
        elif r - 2 < blocks:
            work = functools.partial(tile, r - 2)
            operands = (weights, queries, keys, values, out_grad, other)
        elif r == rounds - 1:
            work, operands = (lambda *parts: jnp.stack(parts)), tuple(received)
        if r > 1:
            send, operands = tie(send, operands)
        got = lax.ppermute(send, AXES, pairs)
        if r == rounds:
            alone = received[-1]
            alone_in = lax.ppermute(alone, AXES, exchange)
            firsts = outside(*[part for i in range(blocks) for part in local[4 * i : 4 * i + 2]])
            far_out, far_dq = call(
                functools.partial(far_kernel, width, heads, far - 3, first_far),
                [full((tokens, columns))] * 2,
                2 * (far - 3) * unit,
                8 * array,
                in_specs=[smem] + [VMEM] * 3 + [pl.BlockSpec()] * 2 + [HBM] * len(firsts),
                out_specs=[VMEM] * 2,
                scratch_shapes=[
                    pltpu.VMEM((len(firsts), BLOCK, columns), F32),
                    pltpu.SemaphoreType.DMA((len(firsts),)),
                ],
            )(place, weights, queries, out_grad, stacked, handed, *firsts)
            got, alone_in, far_out, far_dq = tie(got, alone_in, far_out, far_dq)
        elif r == 1:
            sums = work(*operands)
            got, sums = tie(got, sums)
        else:
            result = work(*operands)
            if r == rounds - 1:
                handed = lax.ppermute(result, AXES, exchange)
            got, result = tie(got, result)
            if r == rounds - 1:
                stacked = result
            else:
                local += list(result)
        received.append(got)
        carried = carried + got

    top = received[-1]
    final = lax.ppermute(jnp.where(on_first, top, carried + low_grads), AXES, exchange)

    wide = pl.BlockSpec((BLOCK, columns), lambda i: (i, 0))
    seconds = outside(*[part for i in range(blocks) for part in local[4 * i + 2 : 4 * i + 4]])
    return call(
        functools.partial(last_kernel, width, heads, far, first_far),
        [full((tokens, columns))] * 4,
        6 * unit,
        16 * array,
        grid=(blocks,),
        in_specs=[smem] + [VMEM] * 5 + [pl.BlockSpec()] * 5 + [VMEM] * 2 + [HBM] * len(seconds),
        out_specs=[wide] * 4,
        scratch_shapes=[
            pltpu.VMEM((len(seconds), BLOCK, columns), F32),
            pltpu.SemaphoreType.DMA((len(seconds),)),
        ],
    )(
        place, weights, queries, keys, values, out_grad, alone, top, alone_in, final, carried,
        far_out, far_dq, *seconds,
    )


def solution(mesh):
    spread = P(AXES, None)

    def body(*args):
        return shards(mesh.shape["row"], mesh.shape["col"], *args)

    return jax.shard_map(
        body,
        mesh=mesh,
        in_specs=(spread,) * 4 + (P(), P(AXES)),
        out_specs=(spread,) * 4,
        check_vma=False,
    )
```

profile of v0, /device:TPU:1, one launch (start us, length us, event | category | flops | bytes accessed | tf_op | source)
XLA Modules:
  0.0 64.0 jit_solution(16054221394288936831)
XLA Ops:
  0.7 3.2 %shard_map.93 = (f32[1024,128]{1,0:T(8,128)S(1)}, f32[2,2,128,128]{3,2,1,0:T(8,128)}) custom-call(s32[1,1024]{1,0:T(1,128)} %bitcast.21, f32[21,2,64]{2,1,0:T(2,128)} %bitcast.20, bf16[1024,256]{1,0:T(8,128)(2,1)} %q.9, bf16[1024,256]{1,0:T(8,128)(2,1)} %k.5, bf16[1024,256]{1,0:T(8,128)(2,1)} %v.5, bf16[1024,256]{1,0:T(8,128)(2,1)} %g.9), custom_call_target="tpu_custom_call" | custom-call | flops 201326592 | bytes 2097152 | tf_op jit(solution)/shard_map/pallas_call | solution.py:303
  3.9 2.3 %shard_map.94 = (f32[2,128,128]{2,1,0:T(8,128)S(1)}, f32[6,2,128,128]{3,2,1,0:T(8,128)S(1)}) custom-call(f32[1024,128]{1,0:T(8,128)S(1)} %get-tuple-element.154.w, bf16[1024,256]{1,0:T(8,128)(2,1)S(1)} %copy-done, bf16[1024,256]{1,0:T(8,128)(2,1)S(1)} %copy-done.1), custom_call_target="tpu_custom_call" | custom-call | flops 536870912 | bytes 2097152 | tf_op jit(solution)/shard_map/pallas_call | solution.py:320
  6.3 3.3 %collective-permute-start.2 = (f32[6,2,128,128]{3,2,1,0:T(8,128)S(1)}, f32[6,2,128,128]{3,2,1,0:T(8,128)S(1)}, u32[]{:S(2)}, u32[]{:S(2)}) collective-permute-start(f32[6,2,128,128]{3,2,1,0:T(8,128)S(1)} %get-tuple-element.105.own_part), channel_id=1, source_target_pairs={{0,1},{1,0},{2,3},{3,2},{4,5},{5,4},{6,7},{7,6},{8,9},{9,8},{10,11... | collective-permute-start | bytes 2359304 | tf_op jit(solution)/shard_map/ppermute | solution.py:342
  9.5 0.1 collective-permute-start
  9.6 2.2 %collective-permute-done.ends = f32[2,2,128,128]{3,2,1,0:T(8,128)S(1)} collective-permute-done((f32[2,2,128,128]{3,2,1,0:T(8,128)}, f32[2,2,128,128]{3,2,1,0:T(8,128)S(1)}, u32[]{:S(2)}, u32[]{:S(2)}) %collective-permute-start) | collective-permute-done | bytes 262176 | tf_op jit(solution)/shard_map/ppermute | solution.py:317
  11.8 1.0 %fusion.2 = (f32[2,128,128]{2,1,0:T(8,128)S(1)}, f32[2,128,128]{2,1,0:T(8,128)S(1)}) fusion(f32[2,2,128,128]{3,2,1,0:T(8,128)S(1)} %collective-permute-done.ends, f32[2,2,128,128]{3,2,1,0:T(8,128)} %get-tuple-element.102, pred[]{:T(512)S(6)} %and.13, pred[]{:T(512)S(6)} %eq.9), kind=kLoop, calls=%fused_computation.3 | loop fusion | flops 163840 | bytes 786434 | tf_op jit(solution)/shard_map/add | solution.py:362
  12.8 4.0 %collective-permute-start.1 = (f32[2,128,128]{2,1,0:T(8,128)S(1)}, f32[2,128,128]{2,1,0:T(8,128)S(1)}, u32[]{:S(2)}, u32[]{:S(2)}) collective-permute-start(f32[2,128,128]{2,1,0:T(8,128)S(1)} %get-tuple-element.104), channel_id=1, source_target_pairs={{0,2},{1,225},{2,0},{3,227},{4,6},{5,229},{6,4},{7,231},{8,10},{9,... | collective-permute-start | bytes 393224 | tf_op jit(solution)/shard_map/ppermute | solution.py:379
  16.8 0.0 collective-permute-done.2.from_other
  16.8 0.1 shard_map.95
  16.9 0.0 copy-start.2
  16.9 3.7 %collective-permute-done.1 = f32[2,128,128]{2,1,0:T(8,128)S(1)} collective-permute-done((f32[2,128,128]{2,1,0:T(8,128)S(1)}, f32[2,128,128]{2,1,0:T(8,128)S(1)}, u32[]{:S(2)}, u32[]{:S(2)}) %collective-permute-start.1) | collective-permute-done | bytes 131104 | tf_op jit(solution)/shard_map/ppermute | solution.py:379
  20.6 0.9 %collective-permute-start.3 = (f32[2,128,128]{2,1,0:T(8,128)S(1)}, f32[2,128,128]{2,1,0:T(8,128)S(1)}, u32[]{:S(2)}, u32[]{:S(2)}) collective-permute-start(f32[2,128,128]{2,1,0:T(8,128)S(1)} %get-tuple-element.114), channel_id=1, source_target_pairs={{0,6},{1,65},{2,4},{3,67},{4,2},{5,69},{6,0},{7,71},{8,14},{9,73},... | collective-permute-start | bytes 393224 | tf_op jit(solution)/shard_map/ppermute | solution.py:379
  21.4 1.7 %shard_map.96 = (f32[256,256]{1,0:T(8,128)S(1)}, f32[256,256]{1,0:T(8,128)S(1)}, f32[256,256]{1,0:T(8,128)S(1)}, f32[256,256]{1,0:T(8,128)S(1)}) custom-call(s32[1]{0:T(128)} %bitcast.place, f32[1024,128]{1,0:T(8,128)S(1)} %get-tuple-element.154.w, bf16[1024,256]{1,0:T(8,128)(2,1)S(1)} %copy-done, bf16[1024,256]{1,0:T(8,128)(2,1)S(1)} %copy-done.2, ...), custom_call_target="tpu_custom_call" | custom-call | flops 335544320 | bytes 3145728 | tf_op jit(solution)/shard_map/pallas_call | solution.py:333
  23.2 0.7 %copy-done.12 = f32[256,256]{1,0:T(8,128)} copy-done((f32[256,256]{1,0:T(8,128)}, f32[256,256]{1,0:T(8,128)S(1)}, u32[]{:S(2)}) %copy-start.12) | copy-done | bytes 262168
  23.9 0.7 %copy-done.13 = f32[256,256]{1,0:T(8,128)} copy-done((f32[256,256]{1,0:T(8,128)}, f32[256,256]{1,0:T(8,128)S(1)}, u32[]{:S(2)}) %copy-start.13) | copy-done | bytes 262168
  24.6 2.2 %collective-permute-done.3 = f32[2,128,128]{2,1,0:T(8,128)S(1)} collective-permute-done((f32[2,128,128]{2,1,0:T(8,128)S(1)}, f32[2,128,128]{2,1,0:T(8,128)S(1)}, u32[]{:S(2)}, u32[]{:S(2)}) %collective-permute-start.3) | collective-permute-done | bytes 131104 | tf_op jit(solution)/shard_map/ppermute | solution.py:379
  26.8 0.1 collective-permute-start.4
  26.9 1.8 %shard_map.97 = (f32[256,256]{1,0:T(8,128)S(1)}, f32[256,256]{1,0:T(8,128)S(1)}, f32[256,256]{1,0:T(8,128)S(1)}, f32[256,256]{1,0:T(8,128)S(1)}) custom-call(s32[1]{0:T(128)} %bitcast.place, f32[1024,128]{1,0:T(8,128)S(1)} %get-tuple-element.154.w, bf16[1024,256]{1,0:T(8,128)(2,1)S(1)} %copy-done, bf16[1024,256]{1,0:T(8,128)(2,1)S(1)} %copy-done.2, ...), custom_call_target="tpu_custom_call" | custom-call | flops 335544320 | bytes 3145728 | tf_op jit(solution)/shard_map/pallas_call | solution.py:333
  28.7 0.7 %copy-done.14 = f32[256,256]{1,0:T(8,128)} copy-done((f32[256,256]{1,0:T(8,128)}, f32[256,256]{1,0:T(8,128)S(1)}, u32[]{:S(2)}) %copy-start.14) | copy-done | bytes 262168
  29.4 0.7 %copy-done.15 = f32[256,256]{1,0:T(8,128)} copy-done((f32[256,256]{1,0:T(8,128)}, f32[256,256]{1,0:T(8,128)S(1)}, u32[]{:S(2)}) %copy-start.15) | copy-done | bytes 262168
  30.1 0.6 collective-permute-done.4
  30.8 0.1 copy-done.6
  30.8 0.1 copy-done.7
  30.9 2.7 %collective-permute-start.5 = (f32[2,128,128]{2,1,0:T(8,128)S(1)}, f32[2,128,128]{2,1,0:T(8,128)S(1)}, u32[]{:S(2)}, u32[]{:S(2)}) collective-permute-start(f32[2,128,128]{2,1,0:T(8,128)S(1)} %get-tuple-element.140), channel_id=1, source_target_pairs={{0,24},{1,25},{2,26},{3,27},{4,28},{5,29},{6,30},{7,31},{8,16},{9,... | collective-permute-start | bytes 393224 | tf_op jit(solution)/shard_map/ppermute | solution.py:379
  33.7 1.6 %shard_map.98 = (f32[256,256]{1,0:T(8,128)S(1)}, f32[256,256]{1,0:T(8,128)S(1)}, f32[256,256]{1,0:T(8,128)S(1)}, f32[256,256]{1,0:T(8,128)S(1)}) custom-call(s32[1]{0:T(128)} %bitcast.place, f32[1024,128]{1,0:T(8,128)S(1)} %get-tuple-element.154.w, bf16[1024,256]{1,0:T(8,128)(2,1)S(1)} %copy-done, bf16[1024,256]{1,0:T(8,128)(2,1)S(1)} %copy-done.2, ...), custom_call_target="tpu_custom_call" | custom-call | flops 335544320 | bytes 3145728 | tf_op jit(solution)/shard_map/pallas_call | solution.py:333
  35.3 0.7 %copy-done.16 = f32[256,256]{1,0:T(8,128)} copy-done((f32[256,256]{1,0:T(8,128)}, f32[256,256]{1,0:T(8,128)S(1)}, u32[]{:S(2)}) %copy-start.16) | copy-done | bytes 262168
  36.0 0.7 %copy-done.17 = f32[256,256]{1,0:T(8,128)} copy-done((f32[256,256]{1,0:T(8,128)}, f32[256,256]{1,0:T(8,128)S(1)}, u32[]{:S(2)}) %copy-start.17) | copy-done | bytes 262168
  36.7 0.0 collective-permute-done.5
  36.8 0.7 %copy-done.8 = f32[256,256]{1,0:T(8,128)} copy-done((f32[256,256]{1,0:T(8,128)}, f32[256,256]{1,0:T(8,128)S(1)}, u32[]{:S(2)}) %copy-start.8) | copy-done | bytes 262168
  37.5 0.1 copy-done.9
  37.6 0.0 collective-permute-start.6
  37.6 1.8 %shard_map.99 = (f32[256,256]{1,0:T(8,128)S(1)}, f32[256,256]{1,0:T(8,128)S(1)}, f32[256,256]{1,0:T(8,128)S(1)}, f32[256,256]{1,0:T(8,128)S(1)}) custom-call(s32[1]{0:T(128)} %bitcast.place, f32[1024,128]{1,0:T(8,128)S(1)} %get-tuple-element.154.w, bf16[1024,256]{1,0:T(8,128)(2,1)S(1)} %copy-done, bf16[1024,256]{1,0:T(8,128)(2,1)S(1)} %copy-done.2, ...), custom_call_target="tpu_custom_call" | custom-call | flops 335544320 | bytes 3145728 | tf_op jit(solution)/shard_map/pallas_call | solution.py:333
  39.4 0.7 %copy-done.18 = f32[256,256]{1,0:T(8,128)} copy-done((f32[256,256]{1,0:T(8,128)}, f32[256,256]{1,0:T(8,128)S(1)}, u32[]{:S(2)}) %copy-start.18) | copy-done | bytes 262168
  40.1 0.7 %copy-done.19 = f32[256,256]{1,0:T(8,128)} copy-done((f32[256,256]{1,0:T(8,128)}, f32[256,256]{1,0:T(8,128)S(1)}, u32[]{:S(2)}) %copy-start.19) | copy-done | bytes 262168
  40.8 0.7 %collective-permute-done.6 = f32[2,128,128]{2,1,0:T(8,128)S(1)} collective-permute-done((f32[2,128,128]{2,1,0:T(8,128)S(1)}, f32[2,128,128]{2,1,0:T(8,128)S(1)}, u32[]{:S(2)}, u32[]{:S(2)}) %collective-permute-start.6) | collective-permute-done | bytes 131104 | tf_op jit(solution)/shard_map/ppermute | solution.py:379
  41.6 0.0 copy-done.11
  41.7 0.5 collective-permute-start.10
  42.2 2.2 %collective-permute-start.7 = (f32[2,128,128]{2,1,0:T(8,128)S(1)}, f32[2,128,128]{2,1,0:T(8,128)S(1)}, u32[]{:S(2)}, u32[]{:S(2)}) collective-permute-start(f32[2,128,128]{2,1,0:T(8,128)S(1)} %get-tuple-element.166), channel_id=1, source_target_pairs={{0,64},{1,7},{2,66},{3,5},{4,68},{5,3},{6,70},{7,1},{8,72},{9,15},... | collective-permute-start | bytes 393224 | tf_op jit(solution)/shard_map/ppermute | solution.py:379
  44.4 3.0 %collective-permute-done.7.alone = f32[2,128,128]{2,1,0:T(8,128)S(1)} collective-permute-done((f32[2,128,128]{2,1,0:T(8,128)S(1)}, f32[2,128,128]{2,1,0:T(8,128)S(1)}, u32[]{:S(2)}, u32[]{:S(2)}) %collective-permute-start.7) | collective-permute-done | bytes 131104 | tf_op jit(solution)/shard_map/ppermute | solution.py:379
  47.3 0.1 collective-permute-start.8
  47.4 6.7 %collective-permute-start.9 = (f32[2,128,128]{2,1,0:T(8,128)S(1)}, f32[2,128,128]{2,1,0:T(8,128)S(1)}, u32[]{:S(2)}, u32[]{:S(2)}) collective-permute-start(f32[2,128,128]{2,1,0:T(8,128)S(1)} %collective-permute-done.7.alone), channel_id=1, source_target_pairs={{0,1},{1,0},{2,3},{3,2},{4,5},{5,4},{6,7},{7,6},{8,9},{9,8},{10,11... | collective-permute-start | bytes 393224 | tf_op jit(solution)/shard_map/ppermute | solution.py:382
  54.1 0.0 collective-permute-done.10.handed
  54.1 3.8 %shard_map.100 = (f32[1024,256]{1,0:T(8,128)S(1)}, f32[1024,256]{1,0:T(8,128)S(1)}) custom-call(s32[1]{0:T(128)} %bitcast.place, f32[1024,128]{1,0:T(8,128)S(1)} %get-tuple-element.154.w, bf16[1024,256]{1,0:T(8,128)(2,1)S(1)} %copy-done, bf16[1024,256]{1,0:T(8,128)(2,1)S(1)} %copy-done.1, f32[5,2,128,128]{3,2,1,0:T(8,128)S(1)} %bitcast_dynamic-update-slice_fusion.stacked, ...), custom_call_target="tpu_custom_call" | custom-call | flops 671088640 | bytes 4194304 | tf_op jit(solution)/shard_map/pallas_call | solution.py:384
  57.9 0.0 collective-permute-done.8.top
  57.9 0.0 collective-permute-done.9.alone_in
  58.0 0.3 collective-permute-start.11
  58.2 1.2 %collective-permute-done.11.final = f32[2,128,128]{2,1,0:T(8,128)S(1)} collective-permute-done((f32[2,128,128]{2,1,0:T(8,128)S(1)}, f32[2,128,128]{2,1,0:T(8,128)S(1)}, u32[]{:S(2)}, u32[]{:S(2)}) %collective-permute-start.11) | collective-permute-done | bytes 131104 | tf_op jit(solution)/shard_map/ppermute | solution.py:413
  59.4 4.5 %shard_map.101 = (f32[1024,256]{1,0:T(8,128)}, f32[1024,256]{1,0:T(8,128)}, f32[1024,256]{1,0:T(8,128)}, f32[1024,256]{1,0:T(8,128)}) custom-call(s32[1]{0:T(128)} %bitcast.place, f32[1024,128]{1,0:T(8,128)S(1)} %get-tuple-element.154.w, bf16[1024,256]{1,0:T(8,128)(2,1)S(1)} %copy-done, bf16[1024,256]{1,0:T(8,128)(2,1)S(1)} %copy-done.2, ...), custom_call_target="tpu_custom_call" | custom-call | flops 402653184 | bytes 8388608 | tf_op jit(solution)/shard_map/pallas_call | solution.py:417
  (38 shorter events, 0.3 us)
Async XLA Ops:
  0.6 3.3 %copy-start = (bf16[1024,256]{1,0:T(8,128)(2,1)S(1)}, bf16[1024,256]{1,0:T(8,128)(2,1)}, u32[]{:S(2)}) copy-start(bf16[1024,256]{1,0:T(8,128)(2,1)} %q.9) | copy-start | bytes 1572868
  0.6 3.3 %copy-start.1 = (bf16[1024,256]{1,0:T(8,128)(2,1)S(1)}, bf16[1024,256]{1,0:T(8,128)(2,1)}, u32[]{:S(2)}) copy-start(bf16[1024,256]{1,0:T(8,128)(2,1)} %g.9) | copy-start | bytes 1572868
  6.3 10.5 %collective-permute-start.2 = (f32[6,2,128,128]{3,2,1,0:T(8,128)S(1)}, f32[6,2,128,128]{3,2,1,0:T(8,128)S(1)}, u32[]{:S(2)}, u32[]{:S(2)}) collective-permute-start(f32[6,2,128,128]{3,2,1,0:T(8,128)S(1)} %get-tuple-element.105.own_part), channel_id=1, source_target_pairs={{0,1},{1,0},{2,3},{3,2},{4,5},{5,4},{6,7},{7,6},{8,9},{9,8},{10,11... | collective-permute-start | bytes 2359304 | tf_op jit(solution)/shard_map/ppermute | solution.py:342
  9.5 2.3 %collective-permute-start = (f32[2,2,128,128]{3,2,1,0:T(8,128)}, f32[2,2,128,128]{3,2,1,0:T(8,128)S(1)}, u32[]{:S(2)}, u32[]{:S(2)}) collective-permute-start(f32[2,2,128,128]{3,2,1,0:T(8,128)} %get-tuple-element.102), channel_id=1, source_target_pairs={{0,1},{1,0},{2,3},{3,2},{4,5},{5,4},{6,7},{7,6},{8,9},{9,8},{10,11... | collective-permute-start | bytes 786440 | tf_op jit(solution)/shard_map/ppermute | solution.py:317
  12.8 7.7 %collective-permute-start.1 = (f32[2,128,128]{2,1,0:T(8,128)S(1)}, f32[2,128,128]{2,1,0:T(8,128)S(1)}, u32[]{:S(2)}, u32[]{:S(2)}) collective-permute-start(f32[2,128,128]{2,1,0:T(8,128)S(1)} %get-tuple-element.104), channel_id=1, source_target_pairs={{0,2},{1,225},{2,0},{3,227},{4,6},{5,229},{6,4},{7,231},{8,10},{9,... | collective-permute-start | bytes 393224 | tf_op jit(solution)/shard_map/ppermute | solution.py:379
  16.8 4.6 %copy-start.3 = (bf16[1024,256]{1,0:T(8,128)(2,1)S(1)}, bf16[1024,256]{1,0:T(8,128)(2,1)}, u32[]{:S(2)}) copy-start(bf16[1024,256]{1,0:T(8,128)(2,1)} %v.5) | copy-start | bytes 1572868
  16.9 4.6 %copy-start.2 = (bf16[1024,256]{1,0:T(8,128)(2,1)S(1)}, bf16[1024,256]{1,0:T(8,128)(2,1)}, u32[]{:S(2)}) copy-start(bf16[1024,256]{1,0:T(8,128)(2,1)} %k.5) | copy-start | bytes 1572868
  20.6 6.2 %collective-permute-start.3 = (f32[2,128,128]{2,1,0:T(8,128)S(1)}, f32[2,128,128]{2,1,0:T(8,128)S(1)}, u32[]{:S(2)}, u32[]{:S(2)}) collective-permute-start(f32[2,128,128]{2,1,0:T(8,128)S(1)} %get-tuple-element.114), channel_id=1, source_target_pairs={{0,6},{1,65},{2,4},{3,67},{4,2},{5,69},{6,0},{7,71},{8,14},{9,73},... | collective-permute-start | bytes 393224 | tf_op jit(solution)/shard_map/ppermute | solution.py:379
  23.2 0.7 %copy-start.12 = (f32[256,256]{1,0:T(8,128)}, f32[256,256]{1,0:T(8,128)S(1)}, u32[]{:S(2)}) copy-start(f32[256,256]{1,0:T(8,128)S(1)} %get-tuple-element.190.refs_0_) | copy-start | bytes 786436
  23.9 0.7 %copy-start.13 = (f32[256,256]{1,0:T(8,128)}, f32[256,256]{1,0:T(8,128)S(1)}, u32[]{:S(2)}) copy-start(f32[256,256]{1,0:T(8,128)S(1)} %get-tuple-element.191.refs_1_) | copy-start | bytes 786436
  24.6 2.2 %copy-start.4 = (f32[256,256]{1,0:T(8,128)}, f32[256,256]{1,0:T(8,128)S(1)}, u32[]{:S(2)}) copy-start(f32[256,256]{1,0:T(8,128)S(1)} %get-tuple-element.175.refs_0_) | copy-start | bytes 786436
  24.6 2.2 %copy-start.5 = (f32[256,256]{1,0:T(8,128)}, f32[256,256]{1,0:T(8,128)S(1)}, u32[]{:S(2)}) copy-start(f32[256,256]{1,0:T(8,128)S(1)} %get-tuple-element.176.refs_1_) | copy-start | bytes 786436
  26.8 3.9 %collective-permute-start.4 = (f32[2,128,128]{2,1,0:T(8,128)S(1)}, f32[2,128,128]{2,1,0:T(8,128)S(1)}, u32[]{:S(2)}, u32[]{:S(2)}) collective-permute-start(f32[2,128,128]{2,1,0:T(8,128)S(1)} %get-tuple-element.127), channel_id=1, source_target_pairs={{0,8},{1,33},{2,10},{3,35},{4,12},{5,37},{6,14},{7,39},{8,0},{9,41... | collective-permute-start | bytes 393224 | tf_op jit(solution)/shard_map/ppermute | solution.py:379
  28.7 0.7 %copy-start.14 = (f32[256,256]{1,0:T(8,128)}, f32[256,256]{1,0:T(8,128)S(1)}, u32[]{:S(2)}) copy-start(f32[256,256]{1,0:T(8,128)S(1)} %get-tuple-element.192.refs_2_) | copy-start | bytes 786436
  29.4 0.7 %copy-start.15 = (f32[256,256]{1,0:T(8,128)}, f32[256,256]{1,0:T(8,128)S(1)}, u32[]{:S(2)}) copy-start(f32[256,256]{1,0:T(8,128)S(1)} %get-tuple-element.193.refs_3_) | copy-start | bytes 786436
  30.1 0.7 %copy-start.6 = (f32[256,256]{1,0:T(8,128)}, f32[256,256]{1,0:T(8,128)S(1)}, u32[]{:S(2)}) copy-start(f32[256,256]{1,0:T(8,128)S(1)} %get-tuple-element.177.refs_2_) | copy-start | bytes 786436
  30.1 0.8 %copy-start.7 = (f32[256,256]{1,0:T(8,128)}, f32[256,256]{1,0:T(8,128)S(1)}, u32[]{:S(2)}) copy-start(f32[256,256]{1,0:T(8,128)S(1)} %get-tuple-element.178.refs_3_) | copy-start | bytes 786436
  30.9 5.8 %collective-permute-start.5 = (f32[2,128,128]{2,1,0:T(8,128)S(1)}, f32[2,128,128]{2,1,0:T(8,128)S(1)}, u32[]{:S(2)}, u32[]{:S(2)}) collective-permute-start(f32[2,128,128]{2,1,0:T(8,128)S(1)} %get-tuple-element.140), channel_id=1, source_target_pairs={{0,24},{1,25},{2,26},{3,27},{4,28},{5,29},{6,30},{7,31},{8,16},{9,... | collective-permute-start | bytes 393224 | tf_op jit(solution)/shard_map/ppermute | solution.py:379
  35.3 0.7 %copy-start.16 = (f32[256,256]{1,0:T(8,128)}, f32[256,256]{1,0:T(8,128)S(1)}, u32[]{:S(2)}) copy-start(f32[256,256]{1,0:T(8,128)S(1)} %get-tuple-element.194.refs_4_) | copy-start | bytes 786436
  36.0 0.7 %copy-start.17 = (f32[256,256]{1,0:T(8,128)}, f32[256,256]{1,0:T(8,128)S(1)}, u32[]{:S(2)}) copy-start(f32[256,256]{1,0:T(8,128)S(1)} %get-tuple-element.195.refs_5_) | copy-start | bytes 786436
  36.7 0.7 %copy-start.8 = (f32[256,256]{1,0:T(8,128)}, f32[256,256]{1,0:T(8,128)S(1)}, u32[]{:S(2)}) copy-start(f32[256,256]{1,0:T(8,128)S(1)} %get-tuple-element.179.refs_4_) | copy-start | bytes 786436
  36.7 0.8 %copy-start.9 = (f32[256,256]{1,0:T(8,128)}, f32[256,256]{1,0:T(8,128)S(1)}, u32[]{:S(2)}) copy-start(f32[256,256]{1,0:T(8,128)S(1)} %get-tuple-element.180.refs_5_) | copy-start | bytes 786436
  37.6 4.0 %collective-permute-start.6 = (f32[2,128,128]{2,1,0:T(8,128)S(1)}, f32[2,128,128]{2,1,0:T(8,128)S(1)}, u32[]{:S(2)}, u32[]{:S(2)}) collective-permute-start(f32[2,128,128]{2,1,0:T(8,128)S(1)} %get-tuple-element.153), channel_id=1, source_target_pairs={{0,32},{1,9},{2,34},{3,11},{4,36},{5,13},{6,38},{7,15},{8,40},{9,1... | collective-permute-start | bytes 393224 | tf_op jit(solution)/shard_map/ppermute | solution.py:379
  39.4 0.7 %copy-start.18 = (f32[256,256]{1,0:T(8,128)}, f32[256,256]{1,0:T(8,128)S(1)}, u32[]{:S(2)}) copy-start(f32[256,256]{1,0:T(8,128)S(1)} %get-tuple-element.196.refs_6_) | copy-start | bytes 786436
  40.1 0.7 %copy-start.19 = (f32[256,256]{1,0:T(8,128)}, f32[256,256]{1,0:T(8,128)S(1)}, u32[]{:S(2)}) copy-start(f32[256,256]{1,0:T(8,128)S(1)} %get-tuple-element.197.refs_7_) | copy-start | bytes 786436
  40.8 0.7 %copy-start.10 = (f32[256,256]{1,0:T(8,128)}, f32[256,256]{1,0:T(8,128)S(1)}, u32[]{:S(2)}) copy-start(f32[256,256]{1,0:T(8,128)S(1)} %get-tuple-element.181.refs_6_) | copy-start | bytes 786436
  40.8 0.8 %copy-start.11 = (f32[256,256]{1,0:T(8,128)}, f32[256,256]{1,0:T(8,128)S(1)}, u32[]{:S(2)}) copy-start(f32[256,256]{1,0:T(8,128)S(1)} %get-tuple-element.182.refs_7_) | copy-start | bytes 786436
  41.7 12.4 %collective-permute-start.10 = (f32[5,2,128,128]{3,2,1,0:T(8,128)S(1)}, f32[5,2,128,128]{3,2,1,0:T(8,128)S(1)}, u32[]{:S(2)}, u32[]{:S(2)}) collective-permute-start(f32[5,2,128,128]{3,2,1,0:T(8,128)S(1)} %bitcast_dynamic-update-slice_fusion.stacked), channel_id=1, source_target_pairs={{0,1},{1,0},{2,3},{3,2},{4,5},{5,4},{6,7},{7,6},{8,9},{9,8},{10,11... | collective-permute-start | bytes 1966088 | tf_op jit(solution)/shard_map/ppermute | solution.py:403
  42.2 5.2 %collective-permute-start.7 = (f32[2,128,128]{2,1,0:T(8,128)S(1)}, f32[2,128,128]{2,1,0:T(8,128)S(1)}, u32[]{:S(2)}, u32[]{:S(2)}) collective-permute-start(f32[2,128,128]{2,1,0:T(8,128)S(1)} %get-tuple-element.166), channel_id=1, source_target_pairs={{0,64},{1,7},{2,66},{3,5},{4,68},{5,3},{6,70},{7,1},{8,72},{9,15},... | collective-permute-start | bytes 393224 | tf_op jit(solution)/shard_map/ppermute | solution.py:379
  47.3 10.6 %collective-permute-start.8 = (f32[2,128,128]{2,1,0:T(8,128)S(1)}, f32[2,128,128]{2,1,0:T(8,128)S(1)}, u32[]{:S(2)}, u32[]{:S(2)}) collective-permute-start(f32[2,128,128]{2,1,0:T(8,128)S(1)} %get-tuple-element.200), channel_id=1, source_target_pairs={{0,224},{1,3},{2,226},{3,1},{4,228},{5,7},{6,230},{7,5},{8,232},{9... | collective-permute-start | bytes 393224 | tf_op jit(solution)/shard_map/ppermute | solution.py:379
  47.4 10.5 %collective-permute-start.9 = (f32[2,128,128]{2,1,0:T(8,128)S(1)}, f32[2,128,128]{2,1,0:T(8,128)S(1)}, u32[]{:S(2)}, u32[]{:S(2)}) collective-permute-start(f32[2,128,128]{2,1,0:T(8,128)S(1)} %collective-permute-done.7.alone), channel_id=1, source_target_pairs={{0,1},{1,0},{2,3},{3,2},{4,5},{5,4},{6,7},{7,6},{8,9},{9,8},{10,11... | collective-permute-start | bytes 393224 | tf_op jit(solution)/shard_map/ppermute | solution.py:382
  58.0 1.4 %collective-permute-start.11 = (f32[2,128,128]{2,1,0:T(8,128)S(1)}, f32[2,128,128]{2,1,0:T(8,128)S(1)}, u32[]{:S(2)}, u32[]{:S(2)}) collective-permute-start(f32[2,128,128]{2,1,0:T(8,128)S(1)} %get-tuple-element.198), channel_id=1, source_target_pairs={{0,1},{1,0},{2,3},{3,2},{4,5},{5,4},{6,7},{7,6},{8,9},{9,8},{10,11... | collective-permute-start | bytes 393224 | tf_op jit(solution)/shard_map/ppermute | solution.py:413
where the time goes:
time: 64.2 us; the launch traced here: 64 us
  Pallas kernels  20.8 us (32%)
  starting transfers between devices  20.7 us (32%)
  waiting for transfers between devices  13.5 us (21%)
  local copies, waits for them, and re-layouts  6.72 us (10%)
  other arithmetic  1.18 us (2%)
  between operations  1.06 us (2%)
    ppermute x7, waiting for transfers between devices, shards(): got = lax.ppermute(send, AXES, pairs)  10.1 us
    ppermute x7, starting transfers between devices, shards(): got = lax.ppermute(send, AXES, pairs)  9.95 us
    pallas_call x4, Pallas kernels, tile(): call(functools.partial(tile_kernel, i, width, heads, depth, first_far), [...  6.95 us
    unnamed x44, local copies, waits for them, and re-layouts  6.71 us
    ppermute x1, starting transfers between devices, shards(): alone_in = lax.ppermute(alone, AXES, exchange)  6.67 us
    pallas_call x1, Pallas kernels, shards(): call(functools.partial(last_kernel, width, heads, far, first_far), [full(...  4.46 us
    pallas_call x1, Pallas kernels, shards(): call(functools.partial(far_kernel, width, heads, far - 3, first_far), [fu...  3.77 us
    ppermute x1, starting transfers between devices, shards(): other_middle = lax.ppermute(middle, AXES, exchange)  3.29 us
  transfers between devices with their start and end apart: 12, of which 7 were waited for; matrix products, arithmetic and copies ran while one was open for 2% of the time, Pallas kernels for 17%

commit v1 on v0

--- a/solution.py
+++ b/solution.py
@@ -214,6 +214,19 @@
             dq[rows, lanes] = near[2 * i + 1, :, lanes] + d
 
 
+def more_kernel(width, heads, level, first_far, place, w, q, g, here, there, f_out, f_dq, out, dq):
+    own = place[0]
+    on_first = (own & 1) == 0
+    for h in range(heads):
+        lanes = slice(h * width, (h + 1) * width)
+        state = jnp.where(on_first, here[h], there[h])
+        state = jnp.where((own >> level & 1) == 1, state, 0.0).astype(BF16)
+        scaled_q = weighted(q[:, lanes], w, h, first_far + level)
+        scaled_g = weighted(g[:, lanes], w, h, first_far + level)
+        out[:, lanes] = f_out[:, lanes] + contract(scaled_q, state, 1, 0)
+        dq[:, lanes] = f_dq[:, lanes] + contract(scaled_g, state, 1, 1)
+
+
 def last_kernel(
     width, heads, far, first_far, place, w, q, k, v, g, alone, top, alone_in, final, carried,
     far_out, far_dq, *refs,
@@ -267,7 +280,7 @@
         place += 2
     for bit in range(col_bits):
         if bit == col_bits - 1 and bit > 0:
-            steps.append(((1 << col_bits) - 1) << row_bits)
+            steps.append(3 << row_bits + bit - 1)
         else:
             steps.append(1 << row_bits + bit)
     return steps
@@ -366,25 +379,29 @@
         pairs = [
             (i, i ^ (steps[rounds - r] if i & 1 else steps[r - 1])) for i in range(devices)
         ]
-        work, operands = None, ()
+        if r > 1:
+            (send,) = tie(send)
+        got = lax.ppermute(send, AXES, pairs)
+        after = (got,)
         if r == 1:
-            work, operands = merge, (middle, other_middle)
-        elif r - 2 < blocks:
-            work = functools.partial(tile, r - 2)
-            operands = (weights, queries, keys, values, out_grad, other)
+            sums = merge(middle, other_middle)
+            after += (sums,)
+        if r <= blocks:
+            part = tile(r - 1, *tie((weights, queries, keys, values, out_grad, other), send)[0])
+            local += list(part)
+            after += (part,)
+        elif r == rounds - 2:
+            stacked = jnp.stack(received)
+            handed = lax.ppermute(stacked, AXES, exchange)
+            after += (stacked, handed)
         elif r == rounds - 1:
-            work, operands = (lambda *parts: jnp.stack(parts)), tuple(received)
-        if r > 1:
-            send, operands = tie(send, operands)
-        got = lax.ppermute(send, AXES, pairs)
-        if r == rounds:
-            alone = received[-1]
-            alone_in = lax.ppermute(alone, AXES, exchange)
+            fifth = received[-1]
+            fifth_in = lax.ppermute(fifth, AXES, exchange)
             firsts = outside(*[part for i in range(blocks) for part in local[4 * i : 4 * i + 2]])
-            far_out, far_dq = call(
-                functools.partial(far_kernel, width, heads, far - 3, first_far),
+            far_sums = call(
+                functools.partial(far_kernel, width, heads, far - 4, first_far),
                 [full((tokens, columns))] * 2,
-                2 * (far - 3) * unit,
+                2 * (far - 4) * unit,
                 8 * array,
                 in_specs=[smem] + [VMEM] * 3 + [pl.BlockSpec()] * 2 + [HBM] * len(firsts),
                 out_specs=[VMEM] * 2,
@@ -393,19 +410,27 @@
                     pltpu.SemaphoreType.DMA((len(firsts),)),
                 ],
             )(place, weights, queries, out_grad, stacked, handed, *firsts)
-            got, alone_in, far_out, far_dq = tie(got, alone_in, far_out, far_dq)
-        elif r == 1:
-            sums = work(*operands)
-            got, sums = tie(got, sums)
+            after += (fifth_in, far_sums)
         else:
-            result = work(*operands)
-            if r == rounds - 1:
-                handed = lax.ppermute(result, AXES, exchange)
-            got, result = tie(got, result)
-            if r == rounds - 1:
-                stacked = result
-            else:
-                local += list(result)
+            alone = received[-1]
+            alone_in = lax.ppermute(alone, AXES, exchange)
+            far_out, far_dq = call(
+                functools.partial(more_kernel, width, heads, far - 3, first_far),
+                [full((tokens, columns))] * 2,
+                2 * unit,
+                8 * array,
+                in_specs=[smem] + [VMEM] * 7,
+                out_specs=[VMEM] * 2,
+            )(place, weights, queries, out_grad, fifth, fifth_in, *far_sums)
+            after += (alone_in, far_out, far_dq)
+        after = tie(*after)
+        got = after[0]
+        if r == 1:
+            sums = after[1]
+        if r == rounds - 1:
+            far_sums = after[2]
+        if r == rounds:
+            far_out, far_dq = after[2:]
         received.append(got)
         carried = carried + got
 

time: 64.2 us -> 63.7 us (level)
  waiting for transfers between devices: 13.5 us -> 10.5 us
  starting transfers between devices: 20.7 us -> 23.3 us
  Pallas kernels: 20.8 us -> 23.2 us
  local copies, waits for them, and re-layouts: 6.72 us -> 5.21 us
  other arithmetic: 1.18 us -> 0.27 us
    ppermute x1, starting transfers between devices: 6.67 us -> 2.42 us  [shards(): alone_in = lax.ppermute(alone, AXES, exchange)]
    ppermute x1, starting transfers between devices: 0.27 us -> 4.16 us  [shards(): lax.ppermute(jnp.where(on_first, top, carried + low_grads), AXES, exchange)]
    ppermute x7, waiting for transfers between devices: 10.1 us -> 6.57 us  [shards(): got = lax.ppermute(send, AXES, pairs)]
    ppermute x7, starting transfers between devices: 9.95 us -> 12.7 us  [shards(): got = lax.ppermute(send, AXES, pairs)]
    pallas_call x1, Pallas kernels: 0.08 us -> 1.74 us  [merge(): call(functools.partial(merge_kernel, far - 2), [full(square)] * (far - 2)...]
    unnamed x44 -> x40, local copies, waits for them, and re-layouts: 6.71 us -> 5.21 us
    add x1, other arithmetic: 1 us -> 0.03 us  [shards(): send = carried + jnp.where(is_upper, ends[1] + other[1], 0.0)]
    pallas_call x1, Pallas kernels: 2.32 us -> 3.21 us  [second(): call(functools.partial(second_kernel, first_far, width, heads, far), (ful...]
  transfers between devices with their start and end apart: 12 -> 13, of which waited for: 7 -> 6; matrix products, arithmetic and copies ran while one was open for 2% -> 0% of each run, Pallas kernels for 17% -> 20%
where the time goes in v1:
time: 63.7 us; the launch traced here: 63.5 us
  starting transfers between devices  23.3 us (37%)
  Pallas kernels  23.2 us (36%)
  waiting for transfers between devices  10.5 us (16%)
  local copies, waits for them, and re-layouts  5.21 us (8%)
  between operations  1.07 us (2%)
    ppermute x7, starting transfers between devices, shards(): got = lax.ppermute(send, AXES, pairs)  12.7 us
    pallas_call x4, Pallas kernels, tile(): call(functools.partial(tile_kernel, i, width, heads, depth, first_far), [...  6.93 us
    ppermute x7, waiting for transfers between devices, shards(): got = lax.ppermute(send, AXES, pairs)  6.57 us
    unnamed x40, local copies, waits for them, and re-layouts  5.21 us
    pallas_call x1, Pallas kernels, shards(): call(functools.partial(last_kernel, width, heads, far, first_far), [full(...  4.46 us
    ppermute x1, starting transfers between devices, shards(): lax.ppermute(jnp.where(on_first, top, carried + low_grads), AXES, exchange)  4.16 us
    pallas_call x1, Pallas kernels, shards(): call(functools.partial(far_kernel, width, heads, far - 4, first_far), [fu...  3.79 us
    pallas_call x1, Pallas kernels, second(): call(functools.partial(second_kernel, first_far, width, heads, far), (ful...  3.21 us
  transfers between devices with their start and end apart: 13, of which 6 were waited for; matrix products, arithmetic and copies ran while one was open for 0% of the time, Pallas kernels for 20%

profile of v1, /device:TPU:1, one launch (start us, length us, event | category | flops | bytes accessed | tf_op | source)
XLA Modules:
  0.0 63.5 jit_solution(3411001245012579035)
XLA Ops:
  0.7 2.5 %shard_map.93 = (f32[1024,128]{1,0:T(8,128)S(1)}, f32[2,2,128,128]{3,2,1,0:T(8,128)S(1)}) custom-call(s32[1,1024]{1,0:T(1,128)} %bitcast.19, f32[21,2,64]{2,1,0:T(2,128)} %bitcast.18, bf16[1024,256]{1,0:T(8,128)(2,1)} %q.11, bf16[1024,256]{1,0:T(8,128)(2,1)} %k.5, bf16[1024,256]{1,0:T(8,128)(2,1)} %v.5, bf16[1024,256]{1,0:T(8,128)(2,1)} %g.11), custom_call_target="tpu_custom_call" | custom-call | flops 201326592 | bytes 2097152 | tf_op jit(solution)/shard_map/pallas_call | solution.py:316
  3.2 0.0 copy-start.3
  3.2 3.2 %shard_map.94 = (f32[2,128,128]{2,1,0:T(8,128)S(1)}, f32[6,2,128,128]{3,2,1,0:T(8,128)}) custom-call(f32[1024,128]{1,0:T(8,128)S(1)} %get-tuple-element.124.w, bf16[1024,256]{1,0:T(8,128)(2,1)S(1)} %copy-done, bf16[1024,256]{1,0:T(8,128)(2,1)S(1)} %copy-done.1), custom_call_target="tpu_custom_call" | custom-call | flops 536870912 | bytes 2097152 | tf_op jit(solution)/shard_map/pallas_call | solution.py:333
  6.4 3.2 %collective-permute-start.2 = (f32[6,2,128,128]{3,2,1,0:T(8,128)}, f32[6,2,128,128]{3,2,1,0:T(8,128)}, u32[]{:S(2)}, u32[]{:S(2)}) collective-permute-start(f32[6,2,128,128]{3,2,1,0:T(8,128)} %get-tuple-element.81.own_part), channel_id=1, source_target_pairs={{0,1},{1,0},{2,3},{3,2},{4,5},{5,4},{6,7},{7,6},{8,9},{9,8},{10,11... | collective-permute-start | bytes 2359304 | tf_op jit(solution)/shard_map/ppermute | solution.py:355
  9.6 0.0 collective-permute-start
  9.6 2.5 %collective-permute-done.ends = f32[2,2,128,128]{3,2,1,0:T(8,128)S(1)} collective-permute-done((f32[2,2,128,128]{3,2,1,0:T(8,128)S(1)}, f32[2,2,128,128]{3,2,1,0:T(8,128)S(1)}, u32[]{:S(2)}, u32[]{:S(2)}) %collective-permute-start) | collective-permute-done | bytes 262176 | tf_op jit(solution)/shard_map/ppermute | solution.py:330
  12.2 4.4 %collective-permute-start.1 = (f32[2,128,128]{2,1,0:T(8,128)S(1)}, f32[2,128,128]{2,1,0:T(8,128)S(1)}, u32[]{:S(2)}, u32[]{:S(2)}) collective-permute-start(f32[2,128,128]{2,1,0:T(8,128)S(1)} %get-tuple-element.80), channel_id=1, source_target_pairs={{0,2},{1,193},{2,0},{3,195},{4,6},{5,197},{6,4},{7,199},{8,10},{9,... | collective-permute-start | bytes 393224 | tf_op jit(solution)/shard_map/ppermute | solution.py:384
  16.6 1.7 %shard_map.96 = (f32[256,256]{1,0:T(8,128)S(1)}, f32[256,256]{1,0:T(8,128)S(1)}, f32[256,256]{1,0:T(8,128)S(1)}, f32[256,256]{1,0:T(8,128)S(1)}) custom-call(s32[1]{0:T(128)} %bitcast.place, f32[1024,128]{1,0:T(8,128)S(1)} %get-tuple-element.124.w, bf16[1024,256]{1,0:T(8,128)(2,1)S(1)} %copy-done, bf16[1024,256]{1,0:T(8,128)(2,1)S(1)} %copy-done.2, ...), custom_call_target="tpu_custom_call" | custom-call | flops 335544320 | bytes 3145728 | tf_op jit(solution)/shard_map/pallas_call | solution.py:346
  18.3 0.0 copy-start.13
  18.3 0.7 %copy-done.13 = f32[256,256]{1,0:T(8,128)} copy-done((f32[256,256]{1,0:T(8,128)}, f32[256,256]{1,0:T(8,128)S(1)}, u32[]{:S(2)}) %copy-start.13) | copy-done | bytes 262168
  19.0 0.0 collective-permute-done.2.from_other
  19.0 1.7 %shard_map.95 = (f32[2,128,128]{2,1,0:T(8,128)S(1)}, f32[2,128,128]{2,1,0:T(8,128)S(1)}, f32[2,128,128]{2,1,0:T(8,128)S(1)}, f32[2,128,128]{2,1,0:T(8,128)S(1)},...) custom-call(s32[1]{0:T(128)} %bitcast.place, f32[6,2,128,128]{3,2,1,0:T(8,128)} %get-tuple-element.81.own_part, ...), custom_call_target="tpu_custom_call" | custom-call | flops 131072 | bytes 524288 | tf_op jit(solution)/shard_map/pallas_call | solution.py:358
  20.8 0.0 collective-permute-done.1
  20.8 1.3 %collective-permute-start.3 = (f32[2,128,128]{2,1,0:T(8,128)S(1)}, f32[2,128,128]{2,1,0:T(8,128)S(1)}, u32[]{:S(2)}, u32[]{:S(2)}) collective-permute-start(f32[2,128,128]{2,1,0:T(8,128)S(1)} %get-tuple-element.162), channel_id=1, source_target_pairs={{0,6},{1,65},{2,4},{3,67},{4,2},{5,69},{6,0},{7,71},{8,14},{9,73},... | collective-permute-start | bytes 393224 | tf_op jit(solution)/shard_map/ppermute | solution.py:384
  22.1 1.8 %shard_map.97 = (f32[256,256]{1,0:T(8,128)S(1)}, f32[256,256]{1,0:T(8,128)S(1)}, f32[256,256]{1,0:T(8,128)S(1)}, f32[256,256]{1,0:T(8,128)S(1)}) custom-call(s32[1]{0:T(128)} %bitcast.place, f32[1024,128]{1,0:T(8,128)S(1)} %get-tuple-element.124.w, bf16[1024,256]{1,0:T(8,128)(2,1)S(1)} %copy-done, bf16[1024,256]{1,0:T(8,128)(2,1)S(1)} %copy-done.2, ...), custom_call_target="tpu_custom_call" | custom-call | flops 335544320 | bytes 3145728 | tf_op jit(solution)/shard_map/pallas_call | solution.py:346
  23.9 0.7 %copy-done.14 = f32[256,256]{1,0:T(8,128)} copy-done((f32[256,256]{1,0:T(8,128)}, f32[256,256]{1,0:T(8,128)S(1)}, u32[]{:S(2)}) %copy-start.14) | copy-done | bytes 262168
  24.6 0.7 %copy-done.15 = f32[256,256]{1,0:T(8,128)} copy-done((f32[256,256]{1,0:T(8,128)}, f32[256,256]{1,0:T(8,128)S(1)}, u32[]{:S(2)}) %copy-start.15) | copy-done | bytes 262168
  25.3 1.7 %collective-permute-done.3 = f32[2,128,128]{2,1,0:T(8,128)S(1)} collective-permute-done((f32[2,128,128]{2,1,0:T(8,128)S(1)}, f32[2,128,128]{2,1,0:T(8,128)S(1)}, u32[]{:S(2)}, u32[]{:S(2)}) %collective-permute-start.3) | collective-permute-done | bytes 131104 | tf_op jit(solution)/shard_map/ppermute | solution.py:384
  27.1 0.1 collective-permute-start.4
  27.2 1.6 %shard_map.98 = (f32[256,256]{1,0:T(8,128)S(1)}, f32[256,256]{1,0:T(8,128)S(1)}, f32[256,256]{1,0:T(8,128)S(1)}, f32[256,256]{1,0:T(8,128)S(1)}) custom-call(s32[1]{0:T(128)} %bitcast.place, f32[1024,128]{1,0:T(8,128)S(1)} %get-tuple-element.124.w, bf16[1024,256]{1,0:T(8,128)(2,1)S(1)} %copy-done, bf16[1024,256]{1,0:T(8,128)(2,1)S(1)} %copy-done.2, ...), custom_call_target="tpu_custom_call" | custom-call | flops 335544320 | bytes 3145728 | tf_op jit(solution)/shard_map/pallas_call | solution.py:346
  28.8 0.7 %copy-done.16 = f32[256,256]{1,0:T(8,128)} copy-done((f32[256,256]{1,0:T(8,128)}, f32[256,256]{1,0:T(8,128)S(1)}, u32[]{:S(2)}) %copy-start.16) | copy-done | bytes 262168
  29.5 0.7 %copy-done.17 = f32[256,256]{1,0:T(8,128)} copy-done((f32[256,256]{1,0:T(8,128)}, f32[256,256]{1,0:T(8,128)S(1)}, u32[]{:S(2)}) %copy-start.17) | copy-done | bytes 262168
  30.3 0.7 %collective-permute-done.4 = f32[2,128,128]{2,1,0:T(8,128)S(1)} collective-permute-done((f32[2,128,128]{2,1,0:T(8,128)S(1)}, f32[2,128,128]{2,1,0:T(8,128)S(1)}, u32[]{:S(2)}, u32[]{:S(2)}) %collective-permute-start.4) | collective-permute-done | bytes 131104 | tf_op jit(solution)/shard_map/ppermute | solution.py:384
  31.0 0.1 copy-done.9
  31.1 3.0 %collective-permute-start.5 = (f32[2,128,128]{2,1,0:T(8,128)S(1)}, f32[2,128,128]{2,1,0:T(8,128)S(1)}, u32[]{:S(2)}, u32[]{:S(2)}) collective-permute-start(f32[2,128,128]{2,1,0:T(8,128)S(1)} %get-tuple-element.158), channel_id=1, source_target_pairs={{0,24},{1,25},{2,26},{3,27},{4,28},{5,29},{6,30},{7,31},{8,16},{9,... | collective-permute-start | bytes 393224 | tf_op jit(solution)/shard_map/ppermute | solution.py:384
  34.0 1.8 %shard_map.99 = (f32[256,256]{1,0:T(8,128)S(1)}, f32[256,256]{1,0:T(8,128)S(1)}, f32[256,256]{1,0:T(8,128)S(1)}, f32[256,256]{1,0:T(8,128)S(1)}) custom-call(s32[1]{0:T(128)} %bitcast.place, f32[1024,128]{1,0:T(8,128)S(1)} %get-tuple-element.124.w, bf16[1024,256]{1,0:T(8,128)(2,1)S(1)} %copy-done, bf16[1024,256]{1,0:T(8,128)(2,1)S(1)} %copy-done.2, ...), custom_call_target="tpu_custom_call" | custom-call | flops 335544320 | bytes 3145728 | tf_op jit(solution)/shard_map/pallas_call | solution.py:346
  35.9 0.7 %copy-done.19 = f32[256,256]{1,0:T(8,128)} copy-done((f32[256,256]{1,0:T(8,128)}, f32[256,256]{1,0:T(8,128)S(1)}, u32[]{:S(2)}) %copy-start.19) | copy-done | bytes 262168
  36.6 0.0 collective-permute-done.5
  36.7 0.6 %copy-done.10 = f32[256,256]{1,0:T(8,128)} copy-done((f32[256,256]{1,0:T(8,128)}, f32[256,256]{1,0:T(8,128)S(1)}, u32[]{:S(2)}) %copy-start.10) | copy-done | bytes 262168
  37.3 0.1 copy-done.11
  37.4 0.1 copy-done.18
  37.5 0.0 collective-permute-start.7
  37.5 0.1 collective-permute-start.6
  37.6 4.1 %collective-permute-done.6.here = f32[2,128,128]{2,1,0:T(8,128)S(1)} collective-permute-done((f32[2,128,128]{2,1,0:T(8,128)S(1)}, f32[2,128,128]{2,1,0:T(8,128)S(1)}, u32[]{:S(2)}, u32[]{:S(2)}) %collective-permute-start.6) | collective-permute-done | bytes 131104 | tf_op jit(solution)/shard_map/ppermute | solution.py:384
  41.7 0.0 collective-permute-done.7.handed
  41.8 2.6 %collective-permute-start.8 = (f32[2,128,128]{2,1,0:T(8,128)S(1)}, f32[2,128,128]{2,1,0:T(8,128)S(1)}, u32[]{:S(2)}, u32[]{:S(2)}) collective-permute-start(f32[2,128,128]{2,1,0:T(8,128)S(1)} %get-tuple-element.154), channel_id=1, source_target_pairs={{0,64},{1,7},{2,66},{3,5},{4,68},{5,3},{6,70},{7,1},{8,72},{9,15},... | collective-permute-start | bytes 393224 | tf_op jit(solution)/shard_map/ppermute | solution.py:384
  44.3 0.8 %collective-permute-start.9 = (f32[2,128,128]{2,1,0:T(8,128)S(1)}, f32[2,128,128]{2,1,0:T(8,128)S(1)}, u32[]{:S(2)}, u32[]{:S(2)}) collective-permute-start(f32[2,128,128]{2,1,0:T(8,128)S(1)} %collective-permute-done.6.here), channel_id=1, source_target_pairs={{0,1},{1,0},{2,3},{3,2},{4,5},{5,4},{6,7},{7,6},{8,9},{9,8},{10,11... | collective-permute-start | bytes 393224 | tf_op jit(solution)/shard_map/ppermute | solution.py:399
  45.2 3.8 %shard_map.100 = (f32[1024,256]{1,0:T(8,128)S(1)}, f32[1024,256]{1,0:T(8,128)S(1)}) custom-call(s32[1]{0:T(128)} %bitcast.place, f32[1024,128]{1,0:T(8,128)S(1)} %get-tuple-element.124.w, bf16[1024,256]{1,0:T(8,128)(2,1)S(1)} %copy-done, bf16[1024,256]{1,0:T(8,128)(2,1)S(1)} %copy-done.1, f32[4,2,128,128]{3,2,1,0:T(8,128)S(1)} %pad_maximum_fusion.stacked, ...), custom_call_target="tpu_custom_call" | custom-call | flops 536870912 | bytes 4194304 | tf_op jit(solution)/shard_map/pallas_call | solution.py:401
  49.0 0.0 collective-permute-done.8.alone
  49.0 0.0 collective-permute-done.9.there
  49.0 1.3 %collective-permute-start.10 = (f32[2,128,128]{2,1,0:T(8,128)S(1)}, f32[2,128,128]{2,1,0:T(8,128)S(1)}, u32[]{:S(2)}, u32[]{:S(2)}) collective-permute-start(f32[2,128,128]{2,1,0:T(8,128)S(1)} %get-tuple-element.152), channel_id=1, source_target_pairs={{0,192},{1,3},{2,194},{3,1},{4,196},{5,7},{6,198},{7,5},{8,200},{9... | collective-permute-start | bytes 393224 | tf_op jit(solution)/shard_map/ppermute | solution.py:384
  50.3 2.4 %collective-permute-start.11 = (f32[2,128,128]{2,1,0:T(8,128)S(1)}, f32[2,128,128]{2,1,0:T(8,128)S(1)}, u32[]{:S(2)}, u32[]{:S(2)}) collective-permute-start(f32[2,128,128]{2,1,0:T(8,128)S(1)} %collective-permute-done.8.alone), channel_id=1, source_target_pairs={{0,1},{1,0},{2,3},{3,2},{4,5},{5,4},{6,7},{7,6},{8,9},{9,8},{10,11... | collective-permute-start | bytes 393224 | tf_op jit(solution)/shard_map/ppermute | solution.py:416
  52.7 0.5 shard_map.101
  53.2 0.0 collective-permute-done.10.top
  53.3 0.5 collective-permute-done.11.alone_in
  53.8 4.2 %collective-permute-start.12 = (f32[2,128,128]{2,1,0:T(8,128)S(1)}, f32[2,128,128]{2,1,0:T(8,128)S(1)}, u32[]{:S(2)}, u32[]{:S(2)}) collective-permute-start(f32[2,128,128]{2,1,0:T(8,128)S(1)} %get-tuple-element.150), channel_id=1, source_target_pairs={{0,1},{1,0},{2,3},{3,2},{4,5},{5,4},{6,7},{7,6},{8,9},{9,8},{10,11... | collective-permute-start | bytes 393224 | tf_op jit(solution)/shard_map/ppermute | solution.py:438
  57.9 1.0 %collective-permute-done.12.final = f32[2,128,128]{2,1,0:T(8,128)S(1)} collective-permute-done((f32[2,128,128]{2,1,0:T(8,128)S(1)}, f32[2,128,128]{2,1,0:T(8,128)S(1)}, u32[]{:S(2)}, u32[]{:S(2)}) %collective-permute-start.12) | collective-permute-done | bytes 131104 | tf_op jit(solution)/shard_map/ppermute | solution.py:438
  58.9 4.5 %shard_map.102 = (f32[1024,256]{1,0:T(8,128)}, f32[1024,256]{1,0:T(8,128)}, f32[1024,256]{1,0:T(8,128)}, f32[1024,256]{1,0:T(8,128)}) custom-call(s32[1]{0:T(128)} %bitcast.place, f32[1024,128]{1,0:T(8,128)S(1)} %get-tuple-element.124.w, bf16[1024,256]{1,0:T(8,128)(2,1)S(1)} %copy-done, bf16[1024,256]{1,0:T(8,128)(2,1)S(1)} %copy-done.2, ...), custom_call_target="tpu_custom_call" | custom-call | flops 402653184 | bytes 8388608 | tf_op jit(solution)/shard_map/pallas_call | solution.py:442
  (37 shorter events, 0.3 us)
Async XLA Ops:
  0.6 2.6 %copy-start = (bf16[1024,256]{1,0:T(8,128)(2,1)S(1)}, bf16[1024,256]{1,0:T(8,128)(2,1)}, u32[]{:S(2)}) copy-start(bf16[1024,256]{1,0:T(8,128)(2,1)} %q.11) | copy-start | bytes 1572868
  0.6 2.6 %copy-start.1 = (bf16[1024,256]{1,0:T(8,128)(2,1)S(1)}, bf16[1024,256]{1,0:T(8,128)(2,1)}, u32[]{:S(2)}) copy-start(bf16[1024,256]{1,0:T(8,128)(2,1)} %g.11) | copy-start | bytes 1572868
  3.2 13.4 %copy-start.3 = (bf16[1024,256]{1,0:T(8,128)(2,1)S(1)}, bf16[1024,256]{1,0:T(8,128)(2,1)}, u32[]{:S(2)}) copy-start(bf16[1024,256]{1,0:T(8,128)(2,1)} %v.5) | copy-start | bytes 1572868
  6.4 10.1 %copy-start.2 = (bf16[1024,256]{1,0:T(8,128)(2,1)S(1)}, bf16[1024,256]{1,0:T(8,128)(2,1)}, u32[]{:S(2)}) copy-start(bf16[1024,256]{1,0:T(8,128)(2,1)} %k.5) | copy-start | bytes 1572868
  6.4 12.6 %collective-permute-start.2 = (f32[6,2,128,128]{3,2,1,0:T(8,128)}, f32[6,2,128,128]{3,2,1,0:T(8,128)}, u32[]{:S(2)}, u32[]{:S(2)}) collective-permute-start(f32[6,2,128,128]{3,2,1,0:T(8,128)} %get-tuple-element.81.own_part), channel_id=1, source_target_pairs={{0,1},{1,0},{2,3},{3,2},{4,5},{5,4},{6,7},{7,6},{8,9},{9,8},{10,11... | collective-permute-start | bytes 2359304 | tf_op jit(solution)/shard_map/ppermute | solution.py:355
  9.6 2.5 %collective-permute-start = (f32[2,2,128,128]{3,2,1,0:T(8,128)S(1)}, f32[2,2,128,128]{3,2,1,0:T(8,128)S(1)}, u32[]{:S(2)}, u32[]{:S(2)}) collective-permute-start(f32[2,2,128,128]{3,2,1,0:T(8,128)S(1)} %get-tuple-element.78), channel_id=1, source_target_pairs={{0,1},{1,0},{2,3},{3,2},{4,5},{5,4},{6,7},{7,6},{8,9},{9,8},{10,11... | collective-permute-start | bytes 786440 | tf_op jit(solution)/shard_map/ppermute | solution.py:330
  12.2 8.6 %collective-permute-start.1 = (f32[2,128,128]{2,1,0:T(8,128)S(1)}, f32[2,128,128]{2,1,0:T(8,128)S(1)}, u32[]{:S(2)}, u32[]{:S(2)}) collective-permute-start(f32[2,128,128]{2,1,0:T(8,128)S(1)} %get-tuple-element.80), channel_id=1, source_target_pairs={{0,2},{1,193},{2,0},{3,195},{4,6},{5,197},{6,4},{7,199},{8,10},{9,... | collective-permute-start | bytes 393224 | tf_op jit(solution)/shard_map/ppermute | solution.py:384
  18.3 0.7 %copy-start.13 = (f32[256,256]{1,0:T(8,128)}, f32[256,256]{1,0:T(8,128)S(1)}, u32[]{:S(2)}) copy-start(f32[256,256]{1,0:T(8,128)S(1)} %get-tuple-element.97.refs_1_) | copy-start | bytes 786436
  19.0 1.8 %copy-start.4 = (f32[256,256]{1,0:T(8,128)}, f32[256,256]{1,0:T(8,128)S(1)}, u32[]{:S(2)}) copy-start(f32[256,256]{1,0:T(8,128)S(1)} %get-tuple-element.94.refs_0_) | copy-start | bytes 786436
  19.0 1.8 %copy-start.5 = (f32[256,256]{1,0:T(8,128)}, f32[256,256]{1,0:T(8,128)S(1)}, u32[]{:S(2)}) copy-start(f32[256,256]{1,0:T(8,128)S(1)} %get-tuple-element.95.refs_1_) | copy-start | bytes 786436
  19.0 1.8 %copy-start.12 = (f32[256,256]{1,0:T(8,128)}, f32[256,256]{1,0:T(8,128)S(1)}, u32[]{:S(2)}) copy-start(f32[256,256]{1,0:T(8,128)S(1)} %get-tuple-element.96.refs_0_) | copy-start | bytes 786436
  20.8 6.2 %collective-permute-start.3 = (f32[2,128,128]{2,1,0:T(8,128)S(1)}, f32[2,128,128]{2,1,0:T(8,128)S(1)}, u32[]{:S(2)}, u32[]{:S(2)}) collective-permute-start(f32[2,128,128]{2,1,0:T(8,128)S(1)} %get-tuple-element.162), channel_id=1, source_target_pairs={{0,6},{1,65},{2,4},{3,67},{4,2},{5,69},{6,0},{7,71},{8,14},{9,73},... | collective-permute-start | bytes 393224 | tf_op jit(solution)/shard_map/ppermute | solution.py:384
  23.8 0.7 %copy-start.14 = (f32[256,256]{1,0:T(8,128)}, f32[256,256]{1,0:T(8,128)S(1)}, u32[]{:S(2)}) copy-start(f32[256,256]{1,0:T(8,128)S(1)} %get-tuple-element.108.refs_2_) | copy-start | bytes 786436
  24.6 0.7 %copy-start.15 = (f32[256,256]{1,0:T(8,128)}, f32[256,256]{1,0:T(8,128)S(1)}, u32[]{:S(2)}) copy-start(f32[256,256]{1,0:T(8,128)S(1)} %get-tuple-element.109.refs_3_) | copy-start | bytes 786436
  25.3 1.8 %copy-start.6 = (f32[256,256]{1,0:T(8,128)}, f32[256,256]{1,0:T(8,128)S(1)}, u32[]{:S(2)}) copy-start(f32[256,256]{1,0:T(8,128)S(1)} %get-tuple-element.106.refs_2_) | copy-start | bytes 786436
  25.3 1.8 %copy-start.7 = (f32[256,256]{1,0:T(8,128)}, f32[256,256]{1,0:T(8,128)S(1)}, u32[]{:S(2)}) copy-start(f32[256,256]{1,0:T(8,128)S(1)} %get-tuple-element.107.refs_3_) | copy-start | bytes 786436
  27.1 3.9 %collective-permute-start.4 = (f32[2,128,128]{2,1,0:T(8,128)S(1)}, f32[2,128,128]{2,1,0:T(8,128)S(1)}, u32[]{:S(2)}, u32[]{:S(2)}) collective-permute-start(f32[2,128,128]{2,1,0:T(8,128)S(1)} %get-tuple-element.160), channel_id=1, source_target_pairs={{0,8},{1,33},{2,10},{3,35},{4,12},{5,37},{6,14},{7,39},{8,0},{9,41... | collective-permute-start | bytes 393224 | tf_op jit(solution)/shard_map/ppermute | solution.py:384
  28.8 0.7 %copy-start.16 = (f32[256,256]{1,0:T(8,128)}, f32[256,256]{1,0:T(8,128)S(1)}, u32[]{:S(2)}) copy-start(f32[256,256]{1,0:T(8,128)S(1)} %get-tuple-element.120.refs_4_) | copy-start | bytes 786436
  29.5 0.7 %copy-start.17 = (f32[256,256]{1,0:T(8,128)}, f32[256,256]{1,0:T(8,128)S(1)}, u32[]{:S(2)}) copy-start(f32[256,256]{1,0:T(8,128)S(1)} %get-tuple-element.121.refs_5_) | copy-start | bytes 786436
  30.3 0.7 %copy-start.8 = (f32[256,256]{1,0:T(8,128)}, f32[256,256]{1,0:T(8,128)S(1)}, u32[]{:S(2)}) copy-start(f32[256,256]{1,0:T(8,128)S(1)} %get-tuple-element.118.refs_4_) | copy-start | bytes 786436
  30.3 0.8 %copy-start.9 = (f32[256,256]{1,0:T(8,128)}, f32[256,256]{1,0:T(8,128)S(1)}, u32[]{:S(2)}) copy-start(f32[256,256]{1,0:T(8,128)S(1)} %get-tuple-element.119.refs_5_) | copy-start | bytes 786436
  31.1 5.5 %collective-permute-start.5 = (f32[2,128,128]{2,1,0:T(8,128)S(1)}, f32[2,128,128]{2,1,0:T(8,128)S(1)}, u32[]{:S(2)}, u32[]{:S(2)}) collective-permute-start(f32[2,128,128]{2,1,0:T(8,128)S(1)} %get-tuple-element.158), channel_id=1, source_target_pairs={{0,24},{1,25},{2,26},{3,27},{4,28},{5,29},{6,30},{7,31},{8,16},{9,... | collective-permute-start | bytes 393224 | tf_op jit(solution)/shard_map/ppermute | solution.py:384
  35.9 0.7 %copy-start.19 = (f32[256,256]{1,0:T(8,128)}, f32[256,256]{1,0:T(8,128)S(1)}, u32[]{:S(2)}) copy-start(f32[256,256]{1,0:T(8,128)S(1)} %get-tuple-element.133.refs_7_) | copy-start | bytes 786436
  36.6 0.7 %copy-start.10 = (f32[256,256]{1,0:T(8,128)}, f32[256,256]{1,0:T(8,128)S(1)}, u32[]{:S(2)}) copy-start(f32[256,256]{1,0:T(8,128)S(1)} %get-tuple-element.130.refs_6_) | copy-start | bytes 786436
  36.6 0.8 %copy-start.11 = (f32[256,256]{1,0:T(8,128)}, f32[256,256]{1,0:T(8,128)S(1)}, u32[]{:S(2)}) copy-start(f32[256,256]{1,0:T(8,128)S(1)} %get-tuple-element.131.refs_7_) | copy-start | bytes 786436
  36.6 0.9 %copy-start.18 = (f32[256,256]{1,0:T(8,128)}, f32[256,256]{1,0:T(8,128)S(1)}, u32[]{:S(2)}) copy-start(f32[256,256]{1,0:T(8,128)S(1)} %get-tuple-element.132.refs_6_) | copy-start | bytes 786436
  37.5 4.2 %collective-permute-start.7 = (f32[4,2,128,128]{3,2,1,0:T(8,128)S(1)}, f32[4,2,128,128]{3,2,1,0:T(8,128)S(1)}, u32[]{:S(2)}, u32[]{:S(2)}) collective-permute-start(f32[4,2,128,128]{3,2,1,0:T(8,128)S(1)} %pad_maximum_fusion.stacked), channel_id=1, source_target_pairs={{0,1},{1,0},{2,3},{3,2},{4,5},{5,4},{6,7},{7,6},{8,9},{9,8},{10,11... | collective-permute-start | bytes 1572872 | tf_op jit(solution)/shard_map/ppermute | solution.py:395
  37.5 4.2 %collective-permute-start.6 = (f32[2,128,128]{2,1,0:T(8,128)S(1)}, f32[2,128,128]{2,1,0:T(8,128)S(1)}, u32[]{:S(2)}, u32[]{:S(2)}) collective-permute-start(f32[2,128,128]{2,1,0:T(8,128)S(1)} %get-tuple-element.156), channel_id=1, source_target_pairs={{0,32},{1,9},{2,34},{3,11},{4,36},{5,13},{6,38},{7,15},{8,40},{9,1... | collective-permute-start | bytes 393224 | tf_op jit(solution)/shard_map/ppermute | solution.py:384
  41.8 7.2 %collective-permute-start.8 = (f32[2,128,128]{2,1,0:T(8,128)S(1)}, f32[2,128,128]{2,1,0:T(8,128)S(1)}, u32[]{:S(2)}, u32[]{:S(2)}) collective-permute-start(f32[2,128,128]{2,1,0:T(8,128)S(1)} %get-tuple-element.154), channel_id=1, source_target_pairs={{0,64},{1,7},{2,66},{3,5},{4,68},{5,3},{6,70},{7,1},{8,72},{9,15},... | collective-permute-start | bytes 393224 | tf_op jit(solution)/shard_map/ppermute | solution.py:384
  44.3 4.6 %collective-permute-start.9 = (f32[2,128,128]{2,1,0:T(8,128)S(1)}, f32[2,128,128]{2,1,0:T(8,128)S(1)}, u32[]{:S(2)}, u32[]{:S(2)}) collective-permute-start(f32[2,128,128]{2,1,0:T(8,128)S(1)} %collective-permute-done.6.here), channel_id=1, source_target_pairs={{0,1},{1,0},{2,3},{3,2},{4,5},{5,4},{6,7},{7,6},{8,9},{9,8},{10,11... | collective-permute-start | bytes 393224 | tf_op jit(solution)/shard_map/ppermute | solution.py:399
  49.0 4.2 %collective-permute-start.10 = (f32[2,128,128]{2,1,0:T(8,128)S(1)}, f32[2,128,128]{2,1,0:T(8,128)S(1)}, u32[]{:S(2)}, u32[]{:S(2)}) collective-permute-start(f32[2,128,128]{2,1,0:T(8,128)S(1)} %get-tuple-element.152), channel_id=1, source_target_pairs={{0,192},{1,3},{2,194},{3,1},{4,196},{5,7},{6,198},{7,5},{8,200},{9... | collective-permute-start | bytes 393224 | tf_op jit(solution)/shard_map/ppermute | solution.py:384
  50.3 3.4 %collective-permute-start.11 = (f32[2,128,128]{2,1,0:T(8,128)S(1)}, f32[2,128,128]{2,1,0:T(8,128)S(1)}, u32[]{:S(2)}, u32[]{:S(2)}) collective-permute-start(f32[2,128,128]{2,1,0:T(8,128)S(1)} %collective-permute-done.8.alone), channel_id=1, source_target_pairs={{0,1},{1,0},{2,3},{3,2},{4,5},{5,4},{6,7},{7,6},{8,9},{9,8},{10,11... | collective-permute-start | bytes 393224 | tf_op jit(solution)/shard_map/ppermute | solution.py:416
  53.8 5.1 %collective-permute-start.12 = (f32[2,128,128]{2,1,0:T(8,128)S(1)}, f32[2,128,128]{2,1,0:T(8,128)S(1)}, u32[]{:S(2)}, u32[]{:S(2)}) collective-permute-start(f32[2,128,128]{2,1,0:T(8,128)S(1)} %get-tuple-element.150), channel_id=1, source_target_pairs={{0,1},{1,0},{2,3},{3,2},{4,5},{5,4},{6,7},{7,6},{8,9},{9,8},{10,11... | collective-permute-start | bytes 393224 | tf_op jit(solution)/shard_map/ppermute | solution.py:438

commit v2 on v1

--- a/solution.py
+++ b/solution.py
@@ -183,12 +183,10 @@
         dv[:, lanes] = e
 
 
-def far_kernel(
-    width, heads, count, first_far, place, w, q, g, stacked, handed, *refs
-):
+def far_kernel(width, heads, count, first_far, axis, place, w, x, stacked, handed, *refs):
     own = place[0]
     on_first = (own & 1) == 0
-    local, (out, dq, near, arrived) = refs[:-4], refs[-4:]
+    local, (total, near, arrived) = refs[:-3], refs[-3:]
     fetches = [pltpu.make_async_copy(part, near.at[n], arrived.at[n]) for n, part in enumerate(local)]
     for fetch in fetches:
         fetch.start()
@@ -198,42 +196,40 @@
         for j in range(1, count + 1):
             state = jnp.where(on_first, stacked[j - 1, h], handed[j - 1, h])
             of_head.append(jnp.where((own >> j & 1) == 1, state, 0.0).astype(BF16))
-        states.append((jnp.concatenate(of_head, axis=0), jnp.concatenate(of_head, axis=1)))
-    for i in range(q.shape[0] // BLOCK):
+        states.append(jnp.concatenate(of_head, axis=axis))
+    for i in range(x.shape[0] // BLOCK):
         rows = slice(i * BLOCK, (i + 1) * BLOCK)
-        fetches[2 * i].wait()
-        fetches[2 * i + 1].wait()
+        fetches[i].wait()
         for h in range(heads):
             lanes = slice(h * width, (h + 1) * width)
-            scaled_q = [weighted(q[rows, lanes], w[rows, :], h, first_far + j) for j in range(1, count + 1)]
-            scaled_g = [weighted(g[rows, lanes], w[rows, :], h, first_far + j) for j in range(1, count + 1)]
-            tall, broad = states[h]
-            o = contract(jnp.concatenate(scaled_q, axis=1), tall, 1, 0)
-            d = contract(jnp.concatenate(scaled_g, axis=1), broad, 1, 1)
-            out[rows, lanes] = near[2 * i, :, lanes] + o
-            dq[rows, lanes] = near[2 * i + 1, :, lanes] + d
-
-
-def more_kernel(width, heads, level, first_far, place, w, q, g, here, there, f_out, f_dq, out, dq):
+            scaled = [weighted(x[rows, lanes], w[rows, :], h, first_far + j) for j in range(1, count + 1)]
+            total[rows, lanes] = near[i, :, lanes] + contract(
+                jnp.concatenate(scaled, axis=1), states[h], 1, axis
+            )
+
+
+def more_kernel(width, heads, first, first_far, place, w, q, g, fifth, fifth_in, alone, alone_in, f_out, f_dq, out, dq):
     own = place[0]
     on_first = (own & 1) == 0
     for h in range(heads):
         lanes = slice(h * width, (h + 1) * width)
-        state = jnp.where(on_first, here[h], there[h])
-        state = jnp.where((own >> level & 1) == 1, state, 0.0).astype(BF16)
-        scaled_q = weighted(q[:, lanes], w, h, first_far + level)
-        scaled_g = weighted(g[:, lanes], w, h, first_far + level)
-        out[:, lanes] = f_out[:, lanes] + contract(scaled_q, state, 1, 0)
-        dq[:, lanes] = f_dq[:, lanes] + contract(scaled_g, state, 1, 1)
+        pair, scaled_q, scaled_g = [], [], []
+        for j, here, there in ((first, fifth, fifth_in), (first + 1, alone, alone_in)):
+            state = jnp.where(on_first, here[h], there[h])
+            pair.append(jnp.where((own >> j & 1) == 1, state, 0.0).astype(BF16))
+            scaled_q.append(weighted(q[:, lanes], w, h, first_far + j))
+            scaled_g.append(weighted(g[:, lanes], w, h, first_far + j))
+        o = contract(jnp.concatenate(scaled_q, axis=1), jnp.concatenate(pair, axis=0), 1, 0)
+        d = contract(jnp.concatenate(scaled_g, axis=1), jnp.concatenate(pair, axis=1), 1, 1)
+        out[:, lanes] = f_out[:, lanes] + o
+        dq[:, lanes] = f_dq[:, lanes] + d
 
 
 def last_kernel(
-    width, heads, far, first_far, place, w, q, k, v, g, alone, top, alone_in, final, carried,
-    far_out, far_dq, *refs,
+    width, heads, far, first_far, place, w, q, k, v, g, top, final, carried, far_out, far_dq, *refs
 ):
     own = place[0]
-    on_first = (own & 1) == 0
-    local, (out, dq, dk, dv, near, arrived) = refs[:-6], refs[-6:]
+    local, (out, dq, dk, dv, near, arrived, state, pulled) = refs[:-8], refs[-8:]
     step = pl.program_id(0)
     fetches = [pltpu.make_async_copy(part, near.at[n], arrived.at[n]) for n, part in enumerate(local)]
 
@@ -241,33 +237,27 @@
     def _():
         for fetch in fetches:
             fetch.start()
+        on_first = (own & 1) == 0
+        for h in range(heads):
+            highest = jnp.where(on_first, top[h], final[h])
+            state[h] = jnp.where((own >> far - 1 & 1) == 1, highest, 0.0).astype(BF16)
+            pulled[h] = jnp.where(on_first, final[h], carried[h]).astype(BF16)
 
     for i in range(q.shape[0] // BLOCK):
 
         @pl.when(step == i)
         def _(i=i):
             rows = slice(i * BLOCK, (i + 1) * BLOCK)
-            sums = []
-            for h in range(heads):
-                lanes = slice(h * width, (h + 1) * width)
-                pair = []
-                for j, here, there in ((far - 2, alone, alone_in), (far - 1, top, final)):
-                    state = jnp.where(on_first, here[h], there[h])
-                    pair.append(jnp.where((own >> j & 1) == 1, state, 0.0).astype(BF16))
-                pulled = jnp.where(on_first, final[h], carried[h]).astype(BF16)
-                scaled_q = [weighted(q[rows, lanes], w[rows, :], h, first_far + j) for j in (far - 2, far - 1)]
-                scaled_g = [weighted(g[rows, lanes], w[rows, :], h, first_far + j) for j in (far - 2, far - 1)]
-                o = contract(jnp.concatenate(scaled_q, axis=1), jnp.concatenate(pair, axis=0), 1, 0)
-                d = contract(jnp.concatenate(scaled_g, axis=1), jnp.concatenate(pair, axis=1), 1, 1)
-                out[:, lanes] = far_out[rows, lanes] + o
-                dq[:, lanes] = far_dq[rows, lanes] + d
-                sums.append((contract(v[rows, lanes], pulled, 1, 0), contract(k[rows, lanes], pulled, 1, 1)))
             fetches[2 * i].wait()
             fetches[2 * i + 1].wait()
             for h in range(heads):
                 lanes = slice(h * width, (h + 1) * width)
-                dk[:, lanes] = near[2 * i, :, lanes] + sums[h][0]
-                dv[:, lanes] = near[2 * i + 1, :, lanes] + sums[h][1]
+                at = h * STRIDE + first_far + far - 1
+                scale = w[rows, at : at + 1]
+                out[:, lanes] = far_out[rows, lanes] + scale * contract(q[rows, lanes], state[h], 1, 0)
+                dq[:, lanes] = far_dq[rows, lanes] + scale * contract(g[rows, lanes], state[h], 1, 1)
+                dk[:, lanes] = near[2 * i, :, lanes] + contract(v[rows, lanes], pulled[h], 1, 0)
+                dv[:, lanes] = near[2 * i + 1, :, lanes] + contract(k[rows, lanes], pulled[h], 1, 1)
 
 
 def links(row_bits, col_bits):
@@ -363,6 +353,21 @@
             in_specs=[smem] + [pl.BlockSpec()] * 2,
             out_specs=[VMEM] * (far - 2),
         )(place, own_part, from_other)
+
+    def add_far(axis, x, stacked, handed):
+        parts = outside(*[local[4 * i + axis] for i in range(blocks)])
+        return call(
+            functools.partial(far_kernel, width, heads, far - 4, first_far, axis),
+            full((tokens, columns)),
+            (far - 4) * unit,
+            4 * array,
+            in_specs=[smem] + [VMEM] * 2 + [pl.BlockSpec()] * 2 + [HBM] * blocks,
+            out_specs=VMEM,
+            scratch_shapes=[
+                pltpu.VMEM((blocks, BLOCK, columns), F32),
+                pltpu.SemaphoreType.DMA((blocks,)),
+            ],
+        )(place, weights, x, stacked, handed, *parts)
 
     steps = links(row_bits, col_bits)
     rounds = len(steps)
@@ -397,38 +402,30 @@
         elif r == rounds - 1:
             fifth = received[-1]
             fifth_in = lax.ppermute(fifth, AXES, exchange)
-            firsts = outside(*[part for i in range(blocks) for part in local[4 * i : 4 * i + 2]])
-            far_sums = call(
-                functools.partial(far_kernel, width, heads, far - 4, first_far),
-                [full((tokens, columns))] * 2,
-                2 * (far - 4) * unit,
-                8 * array,
-                in_specs=[smem] + [VMEM] * 3 + [pl.BlockSpec()] * 2 + [HBM] * len(firsts),
-                out_specs=[VMEM] * 2,
-                scratch_shapes=[
-                    pltpu.VMEM((len(firsts), BLOCK, columns), F32),
-                    pltpu.SemaphoreType.DMA((len(firsts),)),
-                ],
-            )(place, weights, queries, out_grad, stacked, handed, *firsts)
-            after += (fifth_in, far_sums)
+            far_out = add_far(0, queries, stacked, handed)
+            after += (fifth_in, far_out)
         else:
             alone = received[-1]
             alone_in = lax.ppermute(alone, AXES, exchange)
+            far_dq = add_far(1, out_grad, stacked, handed)
             far_out, far_dq = call(
                 functools.partial(more_kernel, width, heads, far - 3, first_far),
                 [full((tokens, columns))] * 2,
-                2 * unit,
+                4 * unit,
                 8 * array,
-                in_specs=[smem] + [VMEM] * 7,
+                in_specs=[smem] + [VMEM] * 9,
                 out_specs=[VMEM] * 2,
-            )(place, weights, queries, out_grad, fifth, fifth_in, *far_sums)
+            )(
+                place, weights, queries, out_grad, fifth, fifth_in, alone, alone_in,
+                far_out, far_dq,
+            )
             after += (alone_in, far_out, far_dq)
         after = tie(*after)
         got = after[0]
         if r == 1:
             sums = after[1]
         if r == rounds - 1:
-            far_sums = after[2]
+            far_out = after[2]
         if r == rounds:
             far_out, far_dq = after[2:]
         received.append(got)
@@ -445,14 +442,16 @@
         6 * unit,
         16 * array,
         grid=(blocks,),
-        in_specs=[smem] + [VMEM] * 5 + [pl.BlockSpec()] * 5 + [VMEM] * 2 + [HBM] * len(seconds),
+        in_specs=[smem] + [VMEM] * 5 + [pl.BlockSpec()] * 3 + [VMEM] * 2 + [HBM] * len(seconds),
         out_specs=[wide] * 4,
         scratch_shapes=[
             pltpu.VMEM((len(seconds), BLOCK, columns), F32),
             pltpu.SemaphoreType.DMA((len(seconds),)),
+            pltpu.VMEM(square, BF16),
+            pltpu.VMEM(square, BF16),
         ],
     )(
-        place, weights, queries, keys, values, out_grad, alone, top, alone_in, final, carried,
+        place, weights, queries, keys, values, out_grad, top, final, carried,
         far_out, far_dq, *seconds,
     )
 

time: 63.7 us -> 65.6 us (1.030)
  local copies, waits for them, and re-layouts: 5.21 us -> 7.8 us
  starting transfers between devices: 23.3 us -> 20.8 us
  Pallas kernels: 23.2 us -> 25.4 us
    unnamed x40, local copies, waits for them, and re-layouts: 5.21 us -> 7.8 us
    pallas_call x1 -> x2, Pallas kernels: 3.79 us -> 6.24 us  [add_far(): call(functools.partial(far_kernel, width, heads, far - 4, first_far, axis...]
    ppermute x1, starting transfers between devices: 4.16 us -> 1.97 us  [shards(): lax.ppermute(jnp.where(on_first, top, carried + low_grads), AXES, exchange)]
  transfers between devices with their start and end apart: 13 -> 13, of which waited for: 6 -> 5; matrix products, arithmetic and copies ran while one was open for 0% -> 0% of each run, Pallas kernels for 20% -> 24%
where the time goes in v2:
time: 65.6 us; the launch traced here: 65.5 us
  Pallas kernels  25.4 us (39%)
  starting transfers between devices  20.8 us (32%)
  waiting for transfers between devices  10.1 us (15%)
  local copies, waits for them, and re-layouts  7.8 us (12%)
  between operations  1.06 us (2%)
    ppermute x7, starting transfers between devices, shards(): got = lax.ppermute(send, AXES, pairs)  12.7 us
    unnamed x40, local copies, waits for them, and re-layouts  7.8 us
    pallas_call x4, Pallas kernels, tile(): call(functools.partial(tile_kernel, i, width, heads, depth, first_far), [...  6.93 us
    ppermute x7, waiting for transfers between devices, shards(): got = lax.ppermute(send, AXES, pairs)  6.61 us
    pallas_call x2, Pallas kernels, add_far(): call(functools.partial(far_kernel, width, heads, far - 4, first_far, axis...  6.24 us
    pallas_call x1, Pallas kernels, shards(): call(functools.partial(last_kernel, width, heads, far, first_far), [full(...  3.97 us
    pallas_call x1, Pallas kernels, second(): call(functools.partial(second_kernel, first_far, width, heads, far), (ful...  3.21 us
    ppermute x1, starting transfers between devices, shards(): other_middle = lax.ppermute(middle, AXES, exchange)  3.2 us
  transfers between devices with their start and end apart: 13, of which 5 were waited for; matrix products, arithmetic and copies ran while one was open for 0% of the time, Pallas kernels for 24%

profile of v2, /device:TPU:1, one launch (start us, length us, event | category | flops | bytes accessed | tf_op | source)
XLA Modules:
  0.0 65.5 jit_solution(12658621395992877839)
XLA Ops:
  0.7 2.5 %shard_map.93 = (f32[1024,128]{1,0:T(8,128)S(1)}, f32[2,2,128,128]{3,2,1,0:T(8,128)S(1)}) custom-call(s32[1,1024]{1,0:T(1,128)} %bitcast.19, f32[21,2,64]{2,1,0:T(2,128)} %bitcast.18, bf16[1024,256]{1,0:T(8,128)(2,1)} %q.9, bf16[1024,256]{1,0:T(8,128)(2,1)} %k.5, bf16[1024,256]{1,0:T(8,128)(2,1)} %v.5, bf16[1024,256]{1,0:T(8,128)(2,1)} %g.9), custom_call_target="tpu_custom_call" | custom-call | flops 201326592 | bytes 2097152 | tf_op jit(solution)/shard_map/pallas_call | solution.py:306
  3.2 0.0 copy-start.3
  3.2 3.2 %shard_map.94 = (f32[2,128,128]{2,1,0:T(8,128)S(1)}, f32[6,2,128,128]{3,2,1,0:T(8,128)}) custom-call(f32[1024,128]{1,0:T(8,128)S(1)} %get-tuple-element.121.w, bf16[1024,256]{1,0:T(8,128)(2,1)S(1)} %copy-done, bf16[1024,256]{1,0:T(8,128)(2,1)S(1)} %copy-done.1), custom_call_target="tpu_custom_call" | custom-call | flops 536870912 | bytes 2097152 | tf_op jit(solution)/shard_map/pallas_call | solution.py:323
  6.4 3.2 %collective-permute-start.2 = (f32[6,2,128,128]{3,2,1,0:T(8,128)}, f32[6,2,128,128]{3,2,1,0:T(8,128)}, u32[]{:S(2)}, u32[]{:S(2)}) collective-permute-start(f32[6,2,128,128]{3,2,1,0:T(8,128)} %get-tuple-element.78.own_part), channel_id=1, source_target_pairs={{0,1},{1,0},{2,3},{3,2},{4,5},{5,4},{6,7},{7,6},{8,9},{9,8},{10,11... | collective-permute-start | bytes 2359304 | tf_op jit(solution)/shard_map/ppermute | solution.py:345
  9.6 0.0 collective-permute-start
  9.6 2.5 %collective-permute-done.ends = f32[2,2,128,128]{3,2,1,0:T(8,128)S(1)} collective-permute-done((f32[2,2,128,128]{3,2,1,0:T(8,128)S(1)}, f32[2,2,128,128]{3,2,1,0:T(8,128)S(1)}, u32[]{:S(2)}, u32[]{:S(2)}) %collective-permute-start) | collective-permute-done | bytes 262176 | tf_op jit(solution)/shard_map/ppermute | solution.py:320
  12.2 4.4 %collective-permute-start.1 = (f32[2,128,128]{2,1,0:T(8,128)S(1)}, f32[2,128,128]{2,1,0:T(8,128)S(1)}, u32[]{:S(2)}, u32[]{:S(2)}) collective-permute-start(f32[2,128,128]{2,1,0:T(8,128)S(1)} %get-tuple-element.77), channel_id=1, source_target_pairs={{0,2},{1,193},{2,0},{3,195},{4,6},{5,197},{6,4},{7,199},{8,10},{9,... | collective-permute-start | bytes 393224 | tf_op jit(solution)/shard_map/ppermute | solution.py:389
  16.6 1.7 %shard_map.96 = (f32[256,256]{1,0:T(8,128)S(1)}, f32[256,256]{1,0:T(8,128)S(1)}, f32[256,256]{1,0:T(8,128)S(1)}, f32[256,256]{1,0:T(8,128)S(1)}) custom-call(s32[1]{0:T(128)} %bitcast.place, f32[1024,128]{1,0:T(8,128)S(1)} %get-tuple-element.121.w, bf16[1024,256]{1,0:T(8,128)(2,1)S(1)} %copy-done, bf16[1024,256]{1,0:T(8,128)(2,1)S(1)} %copy-done.2, ...), custom_call_target="tpu_custom_call" | custom-call | flops 335544320 | bytes 3145728 | tf_op jit(solution)/shard_map/pallas_call | solution.py:336
  18.3 0.7 %copy-done.5 = f32[256,256]{1,0:T(8,128)} copy-done((f32[256,256]{1,0:T(8,128)}, f32[256,256]{1,0:T(8,128)S(1)}, u32[]{:S(2)}) %copy-start.5) | copy-done | bytes 262168
  19.0 0.7 %copy-done.12 = f32[256,256]{1,0:T(8,128)} copy-done((f32[256,256]{1,0:T(8,128)}, f32[256,256]{1,0:T(8,128)S(1)}, u32[]{:S(2)}) %copy-start.12) | copy-done | bytes 262168
  19.7 0.7 %copy-done.13 = f32[256,256]{1,0:T(8,128)} copy-done((f32[256,256]{1,0:T(8,128)}, f32[256,256]{1,0:T(8,128)S(1)}, u32[]{:S(2)}) %copy-start.13) | copy-done | bytes 262168
  20.4 0.0 collective-permute-done.2.from_other
  20.4 1.5 %shard_map.95 = (f32[2,128,128]{2,1,0:T(8,128)S(1)}, f32[2,128,128]{2,1,0:T(8,128)S(1)}, f32[2,128,128]{2,1,0:T(8,128)S(1)}, f32[2,128,128]{2,1,0:T(8,128)S(1)},...) custom-call(s32[1]{0:T(128)} %bitcast.place, f32[6,2,128,128]{3,2,1,0:T(8,128)} %get-tuple-element.78.own_part, ...), custom_call_target="tpu_custom_call" | custom-call | flops 131072 | bytes 524288 | tf_op jit(solution)/shard_map/pallas_call | solution.py:348
  22.0 0.0 collective-permute-done.1
  22.0 1.3 %collective-permute-start.3 = (f32[2,128,128]{2,1,0:T(8,128)S(1)}, f32[2,128,128]{2,1,0:T(8,128)S(1)}, u32[]{:S(2)}, u32[]{:S(2)}) collective-permute-start(f32[2,128,128]{2,1,0:T(8,128)S(1)} %get-tuple-element.156), channel_id=1, source_target_pairs={{0,6},{1,65},{2,4},{3,67},{4,2},{5,69},{6,0},{7,71},{8,14},{9,73},... | collective-permute-start | bytes 393224 | tf_op jit(solution)/shard_map/ppermute | solution.py:389
  23.3 1.8 %shard_map.97 = (f32[256,256]{1,0:T(8,128)S(1)}, f32[256,256]{1,0:T(8,128)S(1)}, f32[256,256]{1,0:T(8,128)S(1)}, f32[256,256]{1,0:T(8,128)S(1)}) custom-call(s32[1]{0:T(128)} %bitcast.place, f32[1024,128]{1,0:T(8,128)S(1)} %get-tuple-element.121.w, bf16[1024,256]{1,0:T(8,128)(2,1)S(1)} %copy-done, bf16[1024,256]{1,0:T(8,128)(2,1)S(1)} %copy-done.2, ...), custom_call_target="tpu_custom_call" | custom-call | flops 335544320 | bytes 3145728 | tf_op jit(solution)/shard_map/pallas_call | solution.py:336
  25.1 0.7 %copy-done.14 = f32[256,256]{1,0:T(8,128)} copy-done((f32[256,256]{1,0:T(8,128)}, f32[256,256]{1,0:T(8,128)S(1)}, u32[]{:S(2)}) %copy-start.14) | copy-done | bytes 262168
  25.8 0.7 %copy-done.16 = f32[256,256]{1,0:T(8,128)} copy-done((f32[256,256]{1,0:T(8,128)}, f32[256,256]{1,0:T(8,128)S(1)}, u32[]{:S(2)}) %copy-start.16) | copy-done | bytes 262168
  26.5 1.7 %collective-permute-done.3 = f32[2,128,128]{2,1,0:T(8,128)S(1)} collective-permute-done((f32[2,128,128]{2,1,0:T(8,128)S(1)}, f32[2,128,128]{2,1,0:T(8,128)S(1)}, u32[]{:S(2)}, u32[]{:S(2)}) %collective-permute-start.3) | collective-permute-done | bytes 131104 | tf_op jit(solution)/shard_map/ppermute | solution.py:389
  28.3 0.1 collective-permute-start.4
  28.4 1.6 %shard_map.98 = (f32[256,256]{1,0:T(8,128)S(1)}, f32[256,256]{1,0:T(8,128)S(1)}, f32[256,256]{1,0:T(8,128)S(1)}, f32[256,256]{1,0:T(8,128)S(1)}) custom-call(s32[1]{0:T(128)} %bitcast.place, f32[1024,128]{1,0:T(8,128)S(1)} %get-tuple-element.121.w, bf16[1024,256]{1,0:T(8,128)(2,1)S(1)} %copy-done, bf16[1024,256]{1,0:T(8,128)(2,1)S(1)} %copy-done.2, ...), custom_call_target="tpu_custom_call" | custom-call | flops 335544320 | bytes 3145728 | tf_op jit(solution)/shard_map/pallas_call | solution.py:336
  30.0 0.7 %copy-done.15 = f32[256,256]{1,0:T(8,128)} copy-done((f32[256,256]{1,0:T(8,128)}, f32[256,256]{1,0:T(8,128)S(1)}, u32[]{:S(2)}) %copy-start.15) | copy-done | bytes 262168
  30.7 0.7 %copy-done.18 = f32[256,256]{1,0:T(8,128)} copy-done((f32[256,256]{1,0:T(8,128)}, f32[256,256]{1,0:T(8,128)S(1)}, u32[]{:S(2)}) %copy-start.18) | copy-done | bytes 262168
  31.4 0.8 %collective-permute-done.4 = f32[2,128,128]{2,1,0:T(8,128)S(1)} collective-permute-done((f32[2,128,128]{2,1,0:T(8,128)S(1)}, f32[2,128,128]{2,1,0:T(8,128)S(1)}, u32[]{:S(2)}, u32[]{:S(2)}) %collective-permute-start.4) | collective-permute-done | bytes 131104 | tf_op jit(solution)/shard_map/ppermute | solution.py:389
  32.2 0.1 copy-done.9
  32.3 2.9 %collective-permute-start.5 = (f32[2,128,128]{2,1,0:T(8,128)S(1)}, f32[2,128,128]{2,1,0:T(8,128)S(1)}, u32[]{:S(2)}, u32[]{:S(2)}) collective-permute-start(f32[2,128,128]{2,1,0:T(8,128)S(1)} %get-tuple-element.152), channel_id=1, source_target_pairs={{0,24},{1,25},{2,26},{3,27},{4,28},{5,29},{6,30},{7,31},{8,16},{9,... | collective-permute-start | bytes 393224 | tf_op jit(solution)/shard_map/ppermute | solution.py:389
  35.2 1.8 %shard_map.99 = (f32[256,256]{1,0:T(8,128)S(1)}, f32[256,256]{1,0:T(8,128)S(1)}, f32[256,256]{1,0:T(8,128)S(1)}, f32[256,256]{1,0:T(8,128)S(1)}) custom-call(s32[1]{0:T(128)} %bitcast.place, f32[1024,128]{1,0:T(8,128)S(1)} %get-tuple-element.121.w, bf16[1024,256]{1,0:T(8,128)(2,1)S(1)} %copy-done, bf16[1024,256]{1,0:T(8,128)(2,1)S(1)} %copy-done.2, ...), custom_call_target="tpu_custom_call" | custom-call | flops 335544320 | bytes 3145728 | tf_op jit(solution)/shard_map/pallas_call | solution.py:336
  37.1 0.7 %copy-done.11 = f32[256,256]{1,0:T(8,128)} copy-done((f32[256,256]{1,0:T(8,128)}, f32[256,256]{1,0:T(8,128)S(1)}, u32[]{:S(2)}) %copy-start.11) | copy-done | bytes 262168
  37.8 0.7 %copy-done.17 = f32[256,256]{1,0:T(8,128)} copy-done((f32[256,256]{1,0:T(8,128)}, f32[256,256]{1,0:T(8,128)S(1)}, u32[]{:S(2)}) %copy-start.17) | copy-done | bytes 262168
  38.5 0.7 %copy-done.19 = f32[256,256]{1,0:T(8,128)} copy-done((f32[256,256]{1,0:T(8,128)}, f32[256,256]{1,0:T(8,128)S(1)}, u32[]{:S(2)}) %copy-start.19) | copy-done | bytes 262168
  39.2 0.0 collective-permute-done.5
  39.3 0.7 %copy-done.10 = f32[256,256]{1,0:T(8,128)} copy-done((f32[256,256]{1,0:T(8,128)}, f32[256,256]{1,0:T(8,128)S(1)}, u32[]{:S(2)}) %copy-start.10) | copy-done | bytes 262168
  39.9 0.0 collective-permute-start.7
  40.0 0.1 collective-permute-start.6
  40.1 4.1 %collective-permute-done.6.fifth = f32[2,128,128]{2,1,0:T(8,128)S(1)} collective-permute-done((f32[2,128,128]{2,1,0:T(8,128)S(1)}, f32[2,128,128]{2,1,0:T(8,128)S(1)}, u32[]{:S(2)}, u32[]{:S(2)}) %collective-permute-start.6) | collective-permute-done | bytes 131104 | tf_op jit(solution)/shard_map/ppermute | solution.py:389
  44.2 2.6 %collective-permute-start.8 = (f32[2,128,128]{2,1,0:T(8,128)S(1)}, f32[2,128,128]{2,1,0:T(8,128)S(1)}, u32[]{:S(2)}, u32[]{:S(2)}) collective-permute-start(f32[2,128,128]{2,1,0:T(8,128)S(1)} %get-tuple-element.148), channel_id=1, source_target_pairs={{0,64},{1,7},{2,66},{3,5},{4,68},{5,3},{6,70},{7,1},{8,72},{9,15},... | collective-permute-start | bytes 393224 | tf_op jit(solution)/shard_map/ppermute | solution.py:389
  46.8 0.8 %collective-permute-start.9 = (f32[2,128,128]{2,1,0:T(8,128)S(1)}, f32[2,128,128]{2,1,0:T(8,128)S(1)}, u32[]{:S(2)}, u32[]{:S(2)}) collective-permute-start(f32[2,128,128]{2,1,0:T(8,128)S(1)} %collective-permute-done.6.fifth), channel_id=1, source_target_pairs={{0,1},{1,0},{2,3},{3,2},{4,5},{5,4},{6,7},{7,6},{8,9},{9,8},{10,11... | collective-permute-start | bytes 393224 | tf_op jit(solution)/shard_map/ppermute | solution.py:404
  47.6 3.1 %shard_map.100.f_out = f32[1024,256]{1,0:T(8,128)S(1)} custom-call(s32[1]{0:T(128)} %bitcast.place, f32[1024,128]{1,0:T(8,128)S(1)} %get-tuple-element.121.w, bf16[1024,256]{1,0:T(8,128)(2,1)S(1)} %copy-done, f32[4,2,128,128]{3,2,1,0:T(8,128)S(1)} %pad_maximum_fusion.stacked, f32[4,2,128,128]{3,2,1,0:T(8,128)S(1)} %collective-permute-done.7.handed, ...), custom_call_target="tpu_custom_call" | custom-call | flops 268435456 | bytes 2097152 | tf_op jit(solution)/shard_map/pallas_call | solution.py:359
  50.7 0.0 collective-permute-done.8.alone
  50.8 0.0 collective-permute-done.9.fifth_in
  50.8 2.2 %collective-permute-start.11 = (f32[2,128,128]{2,1,0:T(8,128)S(1)}, f32[2,128,128]{2,1,0:T(8,128)S(1)}, u32[]{:S(2)}, u32[]{:S(2)}) collective-permute-start(f32[2,128,128]{2,1,0:T(8,128)S(1)} %collective-permute-done.8.alone), channel_id=1, source_target_pairs={{0,1},{1,0},{2,3},{3,2},{4,5},{5,4},{6,7},{7,6},{8,9},{9,8},{10,11... | collective-permute-start | bytes 393224 | tf_op jit(solution)/shard_map/ppermute | solution.py:409
  52.9 1.3 %collective-permute-start.10 = (f32[2,128,128]{2,1,0:T(8,128)S(1)}, f32[2,128,128]{2,1,0:T(8,128)S(1)}, u32[]{:S(2)}, u32[]{:S(2)}) collective-permute-start(f32[2,128,128]{2,1,0:T(8,128)S(1)} %get-tuple-element.146), channel_id=1, source_target_pairs={{0,192},{1,3},{2,194},{3,1},{4,196},{5,7},{6,198},{7,5},{8,200},{9... | collective-permute-start | bytes 393224 | tf_op jit(solution)/shard_map/ppermute | solution.py:389
  54.2 3.1 %shard_map.101.f_dq = f32[1024,256]{1,0:T(8,128)S(1)} custom-call(s32[1]{0:T(128)} %bitcast.place, f32[1024,128]{1,0:T(8,128)S(1)} %get-tuple-element.121.w, bf16[1024,256]{1,0:T(8,128)(2,1)S(1)} %copy-done.1, f32[4,2,128,128]{3,2,1,0:T(8,128)S(1)} %pad_maximum_fusion.stacked, f32[4,2,128,128]{3,2,1,0:T(8,128)S(1)} %collective-permute-done.7.handed, ...), custom_call_target="tpu_custom_call" | custom-call | flops 268435456 | bytes 2097152 | tf_op jit(solution)/shard_map/pallas_call | solution.py:359
  57.4 0.0 collective-permute-done.11.alone_in
  57.4 0.9 %shard_map.102 = (f32[1024,256]{1,0:T(8,128)S(1)}, f32[1024,256]{1,0:T(8,128)S(1)}) custom-call(s32[1]{0:T(128)} %bitcast.place, f32[1024,128]{1,0:T(8,128)S(1)} %get-tuple-element.121.w, bf16[1024,256]{1,0:T(8,128)(2,1)S(1)} %copy-done, bf16[1024,256]{1,0:T(8,128)(2,1)S(1)} %copy-done.1, f32[2,128,128]{2,1,0:T(8,128)S(1)} %collective-permute-done.6.fifth, ...), custom_call_target="tpu_custom_call" | custom-call | flops 268435456 | bytes 4194304 | tf_op jit(solution)/shard_map/pallas_call | solution.py:411
  58.4 2.0 %collective-permute-start.12 = (f32[2,128,128]{2,1,0:T(8,128)S(1)}, f32[2,128,128]{2,1,0:T(8,128)S(1)}, u32[]{:S(2)}, u32[]{:S(2)}) collective-permute-start(f32[2,128,128]{2,1,0:T(8,128)S(1)} %get-tuple-element.144), channel_id=1, source_target_pairs={{0,1},{1,0},{2,3},{3,2},{4,5},{5,4},{6,7},{7,6},{8,9},{9,8},{10,11... | collective-permute-start | bytes 393224 | tf_op jit(solution)/shard_map/ppermute | solution.py:435
  60.3 1.0 %collective-permute-done.12.final = f32[2,128,128]{2,1,0:T(8,128)S(1)} collective-permute-done((f32[2,128,128]{2,1,0:T(8,128)S(1)}, f32[2,128,128]{2,1,0:T(8,128)S(1)}, u32[]{:S(2)}, u32[]{:S(2)}) %collective-permute-start.12) | collective-permute-done | bytes 131104 | tf_op jit(solution)/shard_map/ppermute | solution.py:435
  61.3 4.0 %shard_map.103 = (f32[1024,256]{1,0:T(8,128)}, f32[1024,256]{1,0:T(8,128)}, f32[1024,256]{1,0:T(8,128)}, f32[1024,256]{1,0:T(8,128)}) custom-call(s32[1]{0:T(128)} %bitcast.place, f32[1024,128]{1,0:T(8,128)S(1)} %get-tuple-element.121.w, bf16[1024,256]{1,0:T(8,128)(2,1)S(1)} %copy-done, bf16[1024,256]{1,0:T(8,128)(2,1)S(1)} %copy-done.2, ...), custom_call_target="tpu_custom_call" | custom-call | flops 402653184 | bytes 8388608 | tf_op jit(solution)/shard_map/pallas_call | solution.py:439
  (38 shorter events, 0.3 us)
Async XLA Ops:
  0.6 2.6 %copy-start = (bf16[1024,256]{1,0:T(8,128)(2,1)S(1)}, bf16[1024,256]{1,0:T(8,128)(2,1)}, u32[]{:S(2)}) copy-start(bf16[1024,256]{1,0:T(8,128)(2,1)} %q.9) | copy-start | bytes 1572868
  0.6 2.6 %copy-start.1 = (bf16[1024,256]{1,0:T(8,128)(2,1)S(1)}, bf16[1024,256]{1,0:T(8,128)(2,1)}, u32[]{:S(2)}) copy-start(bf16[1024,256]{1,0:T(8,128)(2,1)} %g.9) | copy-start | bytes 1572868
  3.2 13.4 %copy-start.3 = (bf16[1024,256]{1,0:T(8,128)(2,1)S(1)}, bf16[1024,256]{1,0:T(8,128)(2,1)}, u32[]{:S(2)}) copy-start(bf16[1024,256]{1,0:T(8,128)(2,1)} %v.5) | copy-start | bytes 1572868
  6.4 10.1 %copy-start.2 = (bf16[1024,256]{1,0:T(8,128)(2,1)S(1)}, bf16[1024,256]{1,0:T(8,128)(2,1)}, u32[]{:S(2)}) copy-start(bf16[1024,256]{1,0:T(8,128)(2,1)} %k.5) | copy-start | bytes 1572868
  6.4 14.0 %collective-permute-start.2 = (f32[6,2,128,128]{3,2,1,0:T(8,128)}, f32[6,2,128,128]{3,2,1,0:T(8,128)}, u32[]{:S(2)}, u32[]{:S(2)}) collective-permute-start(f32[6,2,128,128]{3,2,1,0:T(8,128)} %get-tuple-element.78.own_part), channel_id=1, source_target_pairs={{0,1},{1,0},{2,3},{3,2},{4,5},{5,4},{6,7},{7,6},{8,9},{9,8},{10,11... | collective-permute-start | bytes 2359304 | tf_op jit(solution)/shard_map/ppermute | solution.py:345
  9.6 2.5 %collective-permute-start = (f32[2,2,128,128]{3,2,1,0:T(8,128)S(1)}, f32[2,2,128,128]{3,2,1,0:T(8,128)S(1)}, u32[]{:S(2)}, u32[]{:S(2)}) collective-permute-start(f32[2,2,128,128]{3,2,1,0:T(8,128)S(1)} %get-tuple-element.75), channel_id=1, source_target_pairs={{0,1},{1,0},{2,3},{3,2},{4,5},{5,4},{6,7},{7,6},{8,9},{9,8},{10,11... | collective-permute-start | bytes 786440 | tf_op jit(solution)/shard_map/ppermute | solution.py:320
  12.2 9.8 %collective-permute-start.1 = (f32[2,128,128]{2,1,0:T(8,128)S(1)}, f32[2,128,128]{2,1,0:T(8,128)S(1)}, u32[]{:S(2)}, u32[]{:S(2)}) collective-permute-start(f32[2,128,128]{2,1,0:T(8,128)S(1)} %get-tuple-element.77), channel_id=1, source_target_pairs={{0,2},{1,193},{2,0},{3,195},{4,6},{5,197},{6,4},{7,199},{8,10},{9,... | collective-permute-start | bytes 393224 | tf_op jit(solution)/shard_map/ppermute | solution.py:389
  18.3 0.7 %copy-start.5 = (f32[256,256]{1,0:T(8,128)}, f32[256,256]{1,0:T(8,128)S(1)}, u32[]{:S(2)}) copy-start(f32[256,256]{1,0:T(8,128)S(1)} %get-tuple-element.94.refs_1_) | copy-start | bytes 786436
  19.0 0.7 %copy-start.12 = (f32[256,256]{1,0:T(8,128)}, f32[256,256]{1,0:T(8,128)S(1)}, u32[]{:S(2)}) copy-start(f32[256,256]{1,0:T(8,128)S(1)} %get-tuple-element.92.refs_0_) | copy-start | bytes 786436
  19.7 0.7 %copy-start.13 = (f32[256,256]{1,0:T(8,128)}, f32[256,256]{1,0:T(8,128)S(1)}, u32[]{:S(2)}) copy-start(f32[256,256]{1,0:T(8,128)S(1)} %get-tuple-element.91.refs_0_) | copy-start | bytes 786436
  20.4 1.6 %copy-start.4 = (f32[256,256]{1,0:T(8,128)}, f32[256,256]{1,0:T(8,128)S(1)}, u32[]{:S(2)}) copy-start(f32[256,256]{1,0:T(8,128)S(1)} %get-tuple-element.93.refs_0_) | copy-start | bytes 786436
  22.0 6.2 %collective-permute-start.3 = (f32[2,128,128]{2,1,0:T(8,128)S(1)}, f32[2,128,128]{2,1,0:T(8,128)S(1)}, u32[]{:S(2)}, u32[]{:S(2)}) collective-permute-start(f32[2,128,128]{2,1,0:T(8,128)S(1)} %get-tuple-element.156), channel_id=1, source_target_pairs={{0,6},{1,65},{2,4},{3,67},{4,2},{5,69},{6,0},{7,71},{8,14},{9,73},... | collective-permute-start | bytes 393224 | tf_op jit(solution)/shard_map/ppermute | solution.py:389
  25.1 0.7 %copy-start.14 = (f32[256,256]{1,0:T(8,128)}, f32[256,256]{1,0:T(8,128)S(1)}, u32[]{:S(2)}) copy-start(f32[256,256]{1,0:T(8,128)S(1)} %get-tuple-element.104.refs_1_) | copy-start | bytes 786436
  25.8 0.7 %copy-start.16 = (f32[256,256]{1,0:T(8,128)}, f32[256,256]{1,0:T(8,128)S(1)}, u32[]{:S(2)}) copy-start(f32[256,256]{1,0:T(8,128)S(1)} %get-tuple-element.103.refs_1_) | copy-start | bytes 786436
  26.5 1.8 %copy-start.6 = (f32[256,256]{1,0:T(8,128)}, f32[256,256]{1,0:T(8,128)S(1)}, u32[]{:S(2)}) copy-start(f32[256,256]{1,0:T(8,128)S(1)} %get-tuple-element.105.refs_2_) | copy-start | bytes 786436
  26.5 1.8 %copy-start.7 = (f32[256,256]{1,0:T(8,128)}, f32[256,256]{1,0:T(8,128)S(1)}, u32[]{:S(2)}) copy-start(f32[256,256]{1,0:T(8,128)S(1)} %get-tuple-element.106.refs_3_) | copy-start | bytes 786436
  28.3 3.9 %collective-permute-start.4 = (f32[2,128,128]{2,1,0:T(8,128)S(1)}, f32[2,128,128]{2,1,0:T(8,128)S(1)}, u32[]{:S(2)}, u32[]{:S(2)}) collective-permute-start(f32[2,128,128]{2,1,0:T(8,128)S(1)} %get-tuple-element.154), channel_id=1, source_target_pairs={{0,8},{1,33},{2,10},{3,35},{4,12},{5,37},{6,14},{7,39},{8,0},{9,41... | collective-permute-start | bytes 393224 | tf_op jit(solution)/shard_map/ppermute | solution.py:389
  30.0 0.7 %copy-start.15 = (f32[256,256]{1,0:T(8,128)}, f32[256,256]{1,0:T(8,128)S(1)}, u32[]{:S(2)}) copy-start(f32[256,256]{1,0:T(8,128)S(1)} %get-tuple-element.116.refs_2_) | copy-start | bytes 786436
  30.7 0.7 %copy-start.18 = (f32[256,256]{1,0:T(8,128)}, f32[256,256]{1,0:T(8,128)S(1)}, u32[]{:S(2)}) copy-start(f32[256,256]{1,0:T(8,128)S(1)} %get-tuple-element.115.refs_2_) | copy-start | bytes 786436
  31.4 0.8 %copy-start.8 = (f32[256,256]{1,0:T(8,128)}, f32[256,256]{1,0:T(8,128)S(1)}, u32[]{:S(2)}) copy-start(f32[256,256]{1,0:T(8,128)S(1)} %get-tuple-element.117.refs_4_) | copy-start | bytes 786436
  31.4 0.9 %copy-start.9 = (f32[256,256]{1,0:T(8,128)}, f32[256,256]{1,0:T(8,128)S(1)}, u32[]{:S(2)}) copy-start(f32[256,256]{1,0:T(8,128)S(1)} %get-tuple-element.118.refs_5_) | copy-start | bytes 786436
  32.3 6.9 %collective-permute-start.5 = (f32[2,128,128]{2,1,0:T(8,128)S(1)}, f32[2,128,128]{2,1,0:T(8,128)S(1)}, u32[]{:S(2)}, u32[]{:S(2)}) collective-permute-start(f32[2,128,128]{2,1,0:T(8,128)S(1)} %get-tuple-element.152), channel_id=1, source_target_pairs={{0,24},{1,25},{2,26},{3,27},{4,28},{5,29},{6,30},{7,31},{8,16},{9,... | collective-permute-start | bytes 393224 | tf_op jit(solution)/shard_map/ppermute | solution.py:389
  37.1 0.7 %copy-start.11 = (f32[256,256]{1,0:T(8,128)}, f32[256,256]{1,0:T(8,128)S(1)}, u32[]{:S(2)}) copy-start(f32[256,256]{1,0:T(8,128)S(1)} %get-tuple-element.130.refs_7_) | copy-start | bytes 786436
  37.8 0.7 %copy-start.17 = (f32[256,256]{1,0:T(8,128)}, f32[256,256]{1,0:T(8,128)S(1)}, u32[]{:S(2)}) copy-start(f32[256,256]{1,0:T(8,128)S(1)} %get-tuple-element.128.refs_3_) | copy-start | bytes 786436
  38.5 0.7 %copy-start.19 = (f32[256,256]{1,0:T(8,128)}, f32[256,256]{1,0:T(8,128)S(1)}, u32[]{:S(2)}) copy-start(f32[256,256]{1,0:T(8,128)S(1)} %get-tuple-element.127.refs_3_) | copy-start | bytes 786436
  39.2 0.7 %copy-start.10 = (f32[256,256]{1,0:T(8,128)}, f32[256,256]{1,0:T(8,128)S(1)}, u32[]{:S(2)}) copy-start(f32[256,256]{1,0:T(8,128)S(1)} %get-tuple-element.129.refs_6_) | copy-start | bytes 786436
  39.9 4.2 %collective-permute-start.7 = (f32[4,2,128,128]{3,2,1,0:T(8,128)S(1)}, f32[4,2,128,128]{3,2,1,0:T(8,128)S(1)}, u32[]{:S(2)}, u32[]{:S(2)}) collective-permute-start(f32[4,2,128,128]{3,2,1,0:T(8,128)S(1)} %pad_maximum_fusion.stacked), channel_id=1, source_target_pairs={{0,1},{1,0},{2,3},{3,2},{4,5},{5,4},{6,7},{7,6},{8,9},{9,8},{10,11... | collective-permute-start | bytes 1572872 | tf_op jit(solution)/shard_map/ppermute | solution.py:400
  40.0 4.2 %collective-permute-start.6 = (f32[2,128,128]{2,1,0:T(8,128)S(1)}, f32[2,128,128]{2,1,0:T(8,128)S(1)}, u32[]{:S(2)}, u32[]{:S(2)}) collective-permute-start(f32[2,128,128]{2,1,0:T(8,128)S(1)} %get-tuple-element.150), channel_id=1, source_target_pairs={{0,32},{1,9},{2,34},{3,11},{4,36},{5,13},{6,38},{7,15},{8,40},{9,1... | collective-permute-start | bytes 393224 | tf_op jit(solution)/shard_map/ppermute | solution.py:389
  44.2 6.5 %collective-permute-start.8 = (f32[2,128,128]{2,1,0:T(8,128)S(1)}, f32[2,128,128]{2,1,0:T(8,128)S(1)}, u32[]{:S(2)}, u32[]{:S(2)}) collective-permute-start(f32[2,128,128]{2,1,0:T(8,128)S(1)} %get-tuple-element.148), channel_id=1, source_target_pairs={{0,64},{1,7},{2,66},{3,5},{4,68},{5,3},{6,70},{7,1},{8,72},{9,15},... | collective-permute-start | bytes 393224 | tf_op jit(solution)/shard_map/ppermute | solution.py:389
  46.8 4.0 %collective-permute-start.9 = (f32[2,128,128]{2,1,0:T(8,128)S(1)}, f32[2,128,128]{2,1,0:T(8,128)S(1)}, u32[]{:S(2)}, u32[]{:S(2)}) collective-permute-start(f32[2,128,128]{2,1,0:T(8,128)S(1)} %collective-permute-done.6.fifth), channel_id=1, source_target_pairs={{0,1},{1,0},{2,3},{3,2},{4,5},{5,4},{6,7},{7,6},{8,9},{9,8},{10,11... | collective-permute-start | bytes 393224 | tf_op jit(solution)/shard_map/ppermute | solution.py:404
  50.8 6.6 %collective-permute-start.11 = (f32[2,128,128]{2,1,0:T(8,128)S(1)}, f32[2,128,128]{2,1,0:T(8,128)S(1)}, u32[]{:S(2)}, u32[]{:S(2)}) collective-permute-start(f32[2,128,128]{2,1,0:T(8,128)S(1)} %collective-permute-done.8.alone), channel_id=1, source_target_pairs={{0,1},{1,0},{2,3},{3,2},{4,5},{5,4},{6,7},{7,6},{8,9},{9,8},{10,11... | collective-permute-start | bytes 393224 | tf_op jit(solution)/shard_map/ppermute | solution.py:409
  52.9 5.4 %collective-permute-start.10 = (f32[2,128,128]{2,1,0:T(8,128)S(1)}, f32[2,128,128]{2,1,0:T(8,128)S(1)}, u32[]{:S(2)}, u32[]{:S(2)}) collective-permute-start(f32[2,128,128]{2,1,0:T(8,128)S(1)} %get-tuple-element.146), channel_id=1, source_target_pairs={{0,192},{1,3},{2,194},{3,1},{4,196},{5,7},{6,198},{7,5},{8,200},{9... | collective-permute-start | bytes 393224 | tf_op jit(solution)/shard_map/ppermute | solution.py:389
  58.4 3.0 %collective-permute-start.12 = (f32[2,128,128]{2,1,0:T(8,128)S(1)}, f32[2,128,128]{2,1,0:T(8,128)S(1)}, u32[]{:S(2)}, u32[]{:S(2)}) collective-permute-start(f32[2,128,128]{2,1,0:T(8,128)S(1)} %get-tuple-element.144), channel_id=1, source_target_pairs={{0,1},{1,0},{2,3},{3,2},{4,5},{5,4},{6,7},{7,6},{8,9},{9,8},{10,11... | collective-permute-start | bytes 393224 | tf_op jit(solution)/shard_map/ppermute | solution.py:435

commit v3 on v2

--- a/solution.py
+++ b/solution.py
@@ -183,10 +183,12 @@
         dv[:, lanes] = e
 
 
-def far_kernel(width, heads, count, first_far, axis, place, w, x, stacked, handed, *refs):
+def far_kernel(
+    width, heads, count, first_far, place, w, q, g, stacked, handed, *refs
+):
     own = place[0]
     on_first = (own & 1) == 0
-    local, (total, near, arrived) = refs[:-3], refs[-3:]
+    local, (out, dq, near, arrived) = refs[:-4], refs[-4:]
     fetches = [pltpu.make_async_copy(part, near.at[n], arrived.at[n]) for n, part in enumerate(local)]
     for fetch in fetches:
         fetch.start()
@@ -196,16 +198,20 @@
         for j in range(1, count + 1):
             state = jnp.where(on_first, stacked[j - 1, h], handed[j - 1, h])
             of_head.append(jnp.where((own >> j & 1) == 1, state, 0.0).astype(BF16))
-        states.append(jnp.concatenate(of_head, axis=axis))
-    for i in range(x.shape[0] // BLOCK):
+        states.append((jnp.concatenate(of_head, axis=0), jnp.concatenate(of_head, axis=1)))
+    for i in range(q.shape[0] // BLOCK):
         rows = slice(i * BLOCK, (i + 1) * BLOCK)
-        fetches[i].wait()
+        fetches[2 * i].wait()
+        fetches[2 * i + 1].wait()
         for h in range(heads):
             lanes = slice(h * width, (h + 1) * width)
-            scaled = [weighted(x[rows, lanes], w[rows, :], h, first_far + j) for j in range(1, count + 1)]
-            total[rows, lanes] = near[i, :, lanes] + contract(
-                jnp.concatenate(scaled, axis=1), states[h], 1, axis
-            )
+            scaled_q = [weighted(q[rows, lanes], w[rows, :], h, first_far + j) for j in range(1, count + 1)]
+            scaled_g = [weighted(g[rows, lanes], w[rows, :], h, first_far + j) for j in range(1, count + 1)]
+            tall, broad = states[h]
+            o = contract(jnp.concatenate(scaled_q, axis=1), tall, 1, 0)
+            d = contract(jnp.concatenate(scaled_g, axis=1), broad, 1, 1)
+            out[rows, lanes] = near[2 * i, :, lanes] + o
+            dq[rows, lanes] = near[2 * i + 1, :, lanes] + d
 
 
 def more_kernel(width, heads, first, first_far, place, w, q, g, fifth, fifth_in, alone, alone_in, f_out, f_dq, out, dq):
@@ -354,20 +360,20 @@
             out_specs=[VMEM] * (far - 2),
         )(place, own_part, from_other)
 
-    def add_far(axis, x, stacked, handed):
-        parts = outside(*[local[4 * i + axis] for i in range(blocks)])
+    def add_far(stacked, handed):
+        parts = outside(*[part for i in range(blocks) for part in local[4 * i : 4 * i + 2]])
         return call(
-            functools.partial(far_kernel, width, heads, far - 4, first_far, axis),
-            full((tokens, columns)),
-            (far - 4) * unit,
-            4 * array,
-            in_specs=[smem] + [VMEM] * 2 + [pl.BlockSpec()] * 2 + [HBM] * blocks,
-            out_specs=VMEM,
+            functools.partial(far_kernel, width, heads, far - 4, first_far),
+            [full((tokens, columns))] * 2,
+            2 * (far - 4) * unit,
+            8 * array,
+            in_specs=[smem] + [VMEM] * 3 + [pl.BlockSpec()] * 2 + [HBM] * len(parts),
+            out_specs=[VMEM] * 2,
             scratch_shapes=[
-                pltpu.VMEM((blocks, BLOCK, columns), F32),
-                pltpu.SemaphoreType.DMA((blocks,)),
+                pltpu.VMEM((len(parts), BLOCK, columns), F32),
+                pltpu.SemaphoreType.DMA((len(parts),)),
             ],
-        )(place, weights, x, stacked, handed, *parts)
+        )(place, weights, queries, out_grad, stacked, handed, *parts)
 
     steps = links(row_bits, col_bits)
     rounds = len(steps)
@@ -400,14 +406,12 @@
             handed = lax.ppermute(stacked, AXES, exchange)
             after += (stacked, handed)
         elif r == rounds - 1:
-            fifth = received[-1]
+            far_sums = add_far(stacked, handed)
+            after += (far_sums,)
+        else:
+            fifth, alone = received[-2:]
             fifth_in = lax.ppermute(fifth, AXES, exchange)
-            far_out = add_far(0, queries, stacked, handed)
-            after += (fifth_in, far_out)
-        else:
-            alone = received[-1]
             alone_in = lax.ppermute(alone, AXES, exchange)
-            far_dq = add_far(1, out_grad, stacked, handed)
             far_out, far_dq = call(
                 functools.partial(more_kernel, width, heads, far - 3, first_far),
                 [full((tokens, columns))] * 2,
@@ -417,17 +421,17 @@
                 out_specs=[VMEM] * 2,
             )(
                 place, weights, queries, out_grad, fifth, fifth_in, alone, alone_in,
-                far_out, far_dq,
+                *far_sums,
             )
-            after += (alone_in, far_out, far_dq)
+            after += (far_out, far_dq)
         after = tie(*after)
         got = after[0]
         if r == 1:
             sums = after[1]
         if r == rounds - 1:
-            far_out = after[2]
+            far_sums = after[1]
         if r == rounds:
-            far_out, far_dq = after[2:]
+            far_out, far_dq = after[1:]
         received.append(got)
         carried = carried + got
 

time: 65.6 us -> 64.4 us (0.982)
  Pallas kernels: 25.4 us -> 23 us
  waiting for transfers between devices: 10.1 us -> 11.8 us
  local copies, waits for them, and re-layouts: 7.8 us -> 6.49 us
  starting transfers between devices: 20.8 us -> 21.7 us
    pallas_call x2 -> x1, Pallas kernels: 6.24 us -> 3.78 us  [add_far(): call(functools.partial(far_kernel, width, heads, far - 4, first_far), [fu...]
    ppermute x7, waiting for transfers between devices: 6.61 us -> 8.27 us  [shards(): got = lax.ppermute(send, AXES, pairs)]
    ppermute x1, starting transfers between devices: 1.97 us -> 3.45 us  [shards(): lax.ppermute(jnp.where(on_first, top, carried + low_grads), AXES, exchange)]
    unnamed x40, local copies, waits for them, and re-layouts: 7.8 us -> 6.49 us
  transfers between devices with their start and end apart: 13 -> 13, of which waited for: 5 -> 6; matrix products, arithmetic and copies ran while one was open for 0% -> 0% of each run, Pallas kernels for 24% -> 21%
where the time goes in v3:
time: 64.4 us; the launch traced here: 64.2 us
  Pallas kernels  23 us (36%)
  starting transfers between devices  21.7 us (34%)
  waiting for transfers between devices  11.8 us (18%)
  local copies, waits for them, and re-layouts  6.49 us (10%)
  between operations  1.04 us (2%)
    ppermute x7, starting transfers between devices, shards(): got = lax.ppermute(send, AXES, pairs)  12.7 us
    ppermute x7, waiting for transfers between devices, shards(): got = lax.ppermute(send, AXES, pairs)  8.27 us
    pallas_call x4, Pallas kernels, tile(): call(functools.partial(tile_kernel, i, width, heads, depth, first_far), [...  6.93 us
    unnamed x40, local copies, waits for them, and re-layouts  6.49 us
    pallas_call x1, Pallas kernels, shards(): call(functools.partial(last_kernel, width, heads, far, first_far), [full(...  3.96 us
    pallas_call x1, Pallas kernels, add_far(): call(functools.partial(far_kernel, width, heads, far - 4, first_far), [fu...  3.78 us
    ppermute x1, starting transfers between devices, shards(): lax.ppermute(jnp.where(on_first, top, carried + low_grads), AXES, exchange)  3.45 us
    pallas_call x1, Pallas kernels, second(): call(functools.partial(second_kernel, first_far, width, heads, far), (ful...  3.21 us
  transfers between devices with their start and end apart: 13, of which 6 were waited for; matrix products, arithmetic and copies ran while one was open for 0% of the time, Pallas kernels for 21%

profile of v3, /device:TPU:1, one launch (start us, length us, event | category | flops | bytes accessed | tf_op | source)
XLA Modules:
  0.0 64.2 jit_solution(7733776592525911400)
XLA Ops:
  0.7 2.5 %shard_map.93 = (f32[1024,128]{1,0:T(8,128)S(1)}, f32[2,2,128,128]{3,2,1,0:T(8,128)S(1)}) custom-call(s32[1,1024]{1,0:T(1,128)} %bitcast.19, f32[21,2,64]{2,1,0:T(2,128)} %bitcast.18, bf16[1024,256]{1,0:T(8,128)(2,1)} %q.11, bf16[1024,256]{1,0:T(8,128)(2,1)} %k.5, bf16[1024,256]{1,0:T(8,128)(2,1)} %v.5, bf16[1024,256]{1,0:T(8,128)(2,1)} %g.11), custom_call_target="tpu_custom_call" | custom-call | flops 201326592 | bytes 2097152 | tf_op jit(solution)/shard_map/pallas_call | solution.py:312
  3.2 0.0 copy-start.3
  3.2 3.2 %shard_map.94 = (f32[2,128,128]{2,1,0:T(8,128)S(1)}, f32[6,2,128,128]{3,2,1,0:T(8,128)}) custom-call(f32[1024,128]{1,0:T(8,128)S(1)} %get-tuple-element.124.w, bf16[1024,256]{1,0:T(8,128)(2,1)S(1)} %copy-done, bf16[1024,256]{1,0:T(8,128)(2,1)S(1)} %copy-done.1), custom_call_target="tpu_custom_call" | custom-call | flops 536870912 | bytes 2097152 | tf_op jit(solution)/shard_map/pallas_call | solution.py:329
  6.4 3.2 %collective-permute-start.2 = (f32[6,2,128,128]{3,2,1,0:T(8,128)}, f32[6,2,128,128]{3,2,1,0:T(8,128)}, u32[]{:S(2)}, u32[]{:S(2)}) collective-permute-start(f32[6,2,128,128]{3,2,1,0:T(8,128)} %get-tuple-element.81.own_part), channel_id=1, source_target_pairs={{0,1},{1,0},{2,3},{3,2},{4,5},{5,4},{6,7},{7,6},{8,9},{9,8},{10,11... | collective-permute-start | bytes 2359304 | tf_op jit(solution)/shard_map/ppermute | solution.py:351
  9.6 0.0 collective-permute-start
  9.6 2.5 %collective-permute-done.ends = f32[2,2,128,128]{3,2,1,0:T(8,128)S(1)} collective-permute-done((f32[2,2,128,128]{3,2,1,0:T(8,128)S(1)}, f32[2,2,128,128]{3,2,1,0:T(8,128)S(1)}, u32[]{:S(2)}, u32[]{:S(2)}) %collective-permute-start) | collective-permute-done | bytes 262176 | tf_op jit(solution)/shard_map/ppermute | solution.py:326
  12.2 4.4 %collective-permute-start.1 = (f32[2,128,128]{2,1,0:T(8,128)S(1)}, f32[2,128,128]{2,1,0:T(8,128)S(1)}, u32[]{:S(2)}, u32[]{:S(2)}) collective-permute-start(f32[2,128,128]{2,1,0:T(8,128)S(1)} %get-tuple-element.80), channel_id=1, source_target_pairs={{0,2},{1,193},{2,0},{3,195},{4,6},{5,197},{6,4},{7,199},{8,10},{9,... | collective-permute-start | bytes 393224 | tf_op jit(solution)/shard_map/ppermute | solution.py:395
  16.6 1.7 %shard_map.96 = (f32[256,256]{1,0:T(8,128)S(1)}, f32[256,256]{1,0:T(8,128)S(1)}, f32[256,256]{1,0:T(8,128)S(1)}, f32[256,256]{1,0:T(8,128)S(1)}) custom-call(s32[1]{0:T(128)} %bitcast.place, f32[1024,128]{1,0:T(8,128)S(1)} %get-tuple-element.124.w, bf16[1024,256]{1,0:T(8,128)(2,1)S(1)} %copy-done, bf16[1024,256]{1,0:T(8,128)(2,1)S(1)} %copy-done.2, ...), custom_call_target="tpu_custom_call" | custom-call | flops 335544320 | bytes 3145728 | tf_op jit(solution)/shard_map/pallas_call | solution.py:342
  18.3 0.7 %copy-done.5 = f32[256,256]{1,0:T(8,128)} copy-done((f32[256,256]{1,0:T(8,128)}, f32[256,256]{1,0:T(8,128)S(1)}, u32[]{:S(2)}) %copy-start.5) | copy-done | bytes 262168
  19.0 0.7 %copy-done.13 = f32[256,256]{1,0:T(8,128)} copy-done((f32[256,256]{1,0:T(8,128)}, f32[256,256]{1,0:T(8,128)S(1)}, u32[]{:S(2)}) %copy-start.13) | copy-done | bytes 262168
  19.7 0.0 collective-permute-done.2.from_other
  19.7 1.6 %shard_map.95 = (f32[2,128,128]{2,1,0:T(8,128)S(1)}, f32[2,128,128]{2,1,0:T(8,128)S(1)}, f32[2,128,128]{2,1,0:T(8,128)S(1)}, f32[2,128,128]{2,1,0:T(8,128)S(1)},...) custom-call(s32[1]{0:T(128)} %bitcast.place, f32[6,2,128,128]{3,2,1,0:T(8,128)} %get-tuple-element.81.own_part, ...), custom_call_target="tpu_custom_call" | custom-call | flops 131072 | bytes 524288 | tf_op jit(solution)/shard_map/pallas_call | solution.py:354
  21.4 0.0 collective-permute-done.1
  21.4 1.3 %collective-permute-start.3 = (f32[2,128,128]{2,1,0:T(8,128)S(1)}, f32[2,128,128]{2,1,0:T(8,128)S(1)}, u32[]{:S(2)}, u32[]{:S(2)}) collective-permute-start(f32[2,128,128]{2,1,0:T(8,128)S(1)} %get-tuple-element.162), channel_id=1, source_target_pairs={{0,6},{1,65},{2,4},{3,67},{4,2},{5,69},{6,0},{7,71},{8,14},{9,73},... | collective-permute-start | bytes 393224 | tf_op jit(solution)/shard_map/ppermute | solution.py:395
  22.7 1.8 %shard_map.97 = (f32[256,256]{1,0:T(8,128)S(1)}, f32[256,256]{1,0:T(8,128)S(1)}, f32[256,256]{1,0:T(8,128)S(1)}, f32[256,256]{1,0:T(8,128)S(1)}) custom-call(s32[1]{0:T(128)} %bitcast.place, f32[1024,128]{1,0:T(8,128)S(1)} %get-tuple-element.124.w, bf16[1024,256]{1,0:T(8,128)(2,1)S(1)} %copy-done, bf16[1024,256]{1,0:T(8,128)(2,1)S(1)} %copy-done.2, ...), custom_call_target="tpu_custom_call" | custom-call | flops 335544320 | bytes 3145728 | tf_op jit(solution)/shard_map/pallas_call | solution.py:342
  24.4 0.0 copy-start.14
  24.5 0.7 %copy-done.14 = f32[256,256]{1,0:T(8,128)} copy-done((f32[256,256]{1,0:T(8,128)}, f32[256,256]{1,0:T(8,128)S(1)}, u32[]{:S(2)}) %copy-start.14) | copy-done | bytes 262168
  25.1 0.7 %copy-done.15 = f32[256,256]{1,0:T(8,128)} copy-done((f32[256,256]{1,0:T(8,128)}, f32[256,256]{1,0:T(8,128)S(1)}, u32[]{:S(2)}) %copy-start.15) | copy-done | bytes 262168
  25.9 1.8 %collective-permute-done.3 = f32[2,128,128]{2,1,0:T(8,128)S(1)} collective-permute-done((f32[2,128,128]{2,1,0:T(8,128)S(1)}, f32[2,128,128]{2,1,0:T(8,128)S(1)}, u32[]{:S(2)}, u32[]{:S(2)}) %collective-permute-start.3) | collective-permute-done | bytes 131104 | tf_op jit(solution)/shard_map/ppermute | solution.py:395
  27.7 0.1 collective-permute-start.4
  27.8 1.6 %shard_map.98 = (f32[256,256]{1,0:T(8,128)S(1)}, f32[256,256]{1,0:T(8,128)S(1)}, f32[256,256]{1,0:T(8,128)S(1)}, f32[256,256]{1,0:T(8,128)S(1)}) custom-call(s32[1]{0:T(128)} %bitcast.place, f32[1024,128]{1,0:T(8,128)S(1)} %get-tuple-element.124.w, bf16[1024,256]{1,0:T(8,128)(2,1)S(1)} %copy-done, bf16[1024,256]{1,0:T(8,128)(2,1)S(1)} %copy-done.2, ...), custom_call_target="tpu_custom_call" | custom-call | flops 335544320 | bytes 3145728 | tf_op jit(solution)/shard_map/pallas_call | solution.py:342
  29.4 0.7 %copy-done.16 = f32[256,256]{1,0:T(8,128)} copy-done((f32[256,256]{1,0:T(8,128)}, f32[256,256]{1,0:T(8,128)S(1)}, u32[]{:S(2)}) %copy-start.16) | copy-done | bytes 262168
  30.1 0.7 %copy-done.17 = f32[256,256]{1,0:T(8,128)} copy-done((f32[256,256]{1,0:T(8,128)}, f32[256,256]{1,0:T(8,128)S(1)}, u32[]{:S(2)}) %copy-start.17) | copy-done | bytes 262168
  30.8 0.7 %collective-permute-done.4 = f32[2,128,128]{2,1,0:T(8,128)S(1)} collective-permute-done((f32[2,128,128]{2,1,0:T(8,128)S(1)}, f32[2,128,128]{2,1,0:T(8,128)S(1)}, u32[]{:S(2)}, u32[]{:S(2)}) %collective-permute-start.4) | collective-permute-done | bytes 131104 | tf_op jit(solution)/shard_map/ppermute | solution.py:395
  31.6 0.1 copy-done.9
  31.7 2.9 %collective-permute-start.5 = (f32[2,128,128]{2,1,0:T(8,128)S(1)}, f32[2,128,128]{2,1,0:T(8,128)S(1)}, u32[]{:S(2)}, u32[]{:S(2)}) collective-permute-start(f32[2,128,128]{2,1,0:T(8,128)S(1)} %get-tuple-element.158), channel_id=1, source_target_pairs={{0,24},{1,25},{2,26},{3,27},{4,28},{5,29},{6,30},{7,31},{8,16},{9,... | collective-permute-start | bytes 393224 | tf_op jit(solution)/shard_map/ppermute | solution.py:395
  34.6 1.8 %shard_map.99 = (f32[256,256]{1,0:T(8,128)S(1)}, f32[256,256]{1,0:T(8,128)S(1)}, f32[256,256]{1,0:T(8,128)S(1)}, f32[256,256]{1,0:T(8,128)S(1)}) custom-call(s32[1]{0:T(128)} %bitcast.place, f32[1024,128]{1,0:T(8,128)S(1)} %get-tuple-element.124.w, bf16[1024,256]{1,0:T(8,128)(2,1)S(1)} %copy-done, bf16[1024,256]{1,0:T(8,128)(2,1)S(1)} %copy-done.2, ...), custom_call_target="tpu_custom_call" | custom-call | flops 335544320 | bytes 3145728 | tf_op jit(solution)/shard_map/pallas_call | solution.py:342
  36.5 0.7 %copy-done.11 = f32[256,256]{1,0:T(8,128)} copy-done((f32[256,256]{1,0:T(8,128)}, f32[256,256]{1,0:T(8,128)S(1)}, u32[]{:S(2)}) %copy-start.11) | copy-done | bytes 262168
  37.2 0.7 %copy-done.19 = f32[256,256]{1,0:T(8,128)} copy-done((f32[256,256]{1,0:T(8,128)}, f32[256,256]{1,0:T(8,128)S(1)}, u32[]{:S(2)}) %copy-start.19) | copy-done | bytes 262168
  37.9 0.0 collective-permute-done.5
  37.9 0.7 %copy-done.10 = f32[256,256]{1,0:T(8,128)} copy-done((f32[256,256]{1,0:T(8,128)}, f32[256,256]{1,0:T(8,128)S(1)}, u32[]{:S(2)}) %copy-start.10) | copy-done | bytes 262168
  38.6 0.1 copy-done.18
  38.7 0.0 collective-permute-start.7
  38.7 0.1 collective-permute-start.6
  38.8 4.1 %collective-permute-done.6.fifth = f32[2,128,128]{2,1,0:T(8,128)S(1)} collective-permute-done((f32[2,128,128]{2,1,0:T(8,128)S(1)}, f32[2,128,128]{2,1,0:T(8,128)S(1)}, u32[]{:S(2)}, u32[]{:S(2)}) %collective-permute-start.6) | collective-permute-done | bytes 131104 | tf_op jit(solution)/shard_map/ppermute | solution.py:395
  42.9 0.0 collective-permute-done.7.handed
  43.0 2.6 %collective-permute-start.8 = (f32[2,128,128]{2,1,0:T(8,128)S(1)}, f32[2,128,128]{2,1,0:T(8,128)S(1)}, u32[]{:S(2)}, u32[]{:S(2)}) collective-permute-start(f32[2,128,128]{2,1,0:T(8,128)S(1)} %get-tuple-element.154), channel_id=1, source_target_pairs={{0,64},{1,7},{2,66},{3,5},{4,68},{5,3},{6,70},{7,1},{8,72},{9,15},... | collective-permute-start | bytes 393224 | tf_op jit(solution)/shard_map/ppermute | solution.py:395
  45.5 0.8 %collective-permute-start.10 = (f32[2,128,128]{2,1,0:T(8,128)S(1)}, f32[2,128,128]{2,1,0:T(8,128)S(1)}, u32[]{:S(2)}, u32[]{:S(2)}) collective-permute-start(f32[2,128,128]{2,1,0:T(8,128)S(1)} %collective-permute-done.6.fifth), channel_id=1, source_target_pairs={{0,1},{1,0},{2,3},{3,2},{4,5},{5,4},{6,7},{7,6},{8,9},{9,8},{10,11... | collective-permute-start | bytes 393224 | tf_op jit(solution)/shard_map/ppermute | solution.py:413
  46.4 3.8 %shard_map.100 = (f32[1024,256]{1,0:T(8,128)S(1)}, f32[1024,256]{1,0:T(8,128)S(1)}) custom-call(s32[1]{0:T(128)} %bitcast.place, f32[1024,128]{1,0:T(8,128)S(1)} %get-tuple-element.124.w, bf16[1024,256]{1,0:T(8,128)(2,1)S(1)} %copy-done, bf16[1024,256]{1,0:T(8,128)(2,1)S(1)} %copy-done.1, f32[4,2,128,128]{3,2,1,0:T(8,128)S(1)} %pad_maximum_fusion.stacked, ...), custom_call_target="tpu_custom_call" | custom-call | flops 536870912 | bytes 4194304 | tf_op jit(solution)/shard_map/pallas_call | solution.py:365
  50.2 0.0 collective-permute-done.8.alone
  50.2 1.5 %collective-permute-start.11 = (f32[2,128,128]{2,1,0:T(8,128)S(1)}, f32[2,128,128]{2,1,0:T(8,128)S(1)}, u32[]{:S(2)}, u32[]{:S(2)}) collective-permute-start(f32[2,128,128]{2,1,0:T(8,128)S(1)} %collective-permute-done.8.alone), channel_id=1, source_target_pairs={{0,1},{1,0},{2,3},{3,2},{4,5},{5,4},{6,7},{7,6},{8,9},{9,8},{10,11... | collective-permute-start | bytes 393224 | tf_op jit(solution)/shard_map/ppermute | solution.py:414
  51.7 1.3 %collective-permute-start.9 = (f32[2,128,128]{2,1,0:T(8,128)S(1)}, f32[2,128,128]{2,1,0:T(8,128)S(1)}, u32[]{:S(2)}, u32[]{:S(2)}) collective-permute-start(f32[2,128,128]{2,1,0:T(8,128)S(1)} %get-tuple-element.152), channel_id=1, source_target_pairs={{0,192},{1,3},{2,194},{3,1},{4,196},{5,7},{6,198},{7,5},{8,200},{9... | collective-permute-start | bytes 393224 | tf_op jit(solution)/shard_map/ppermute | solution.py:395
  53.0 0.0 collective-permute-done.10.fifth_in
  53.0 0.9 %shard_map.101 = (f32[1024,256]{1,0:T(8,128)S(1)}, f32[1024,256]{1,0:T(8,128)S(1)}) custom-call(s32[1]{0:T(128)} %bitcast.place, f32[1024,128]{1,0:T(8,128)S(1)} %get-tuple-element.124.w, bf16[1024,256]{1,0:T(8,128)(2,1)S(1)} %copy-done, bf16[1024,256]{1,0:T(8,128)(2,1)S(1)} %copy-done.1, f32[2,128,128]{2,1,0:T(8,128)S(1)} %collective-permute-done.6.fifth, ...), custom_call_target="tpu_custom_call" | custom-call | flops 268435456 | bytes 4194304 | tf_op jit(solution)/shard_map/pallas_call | solution.py:415
  54.0 1.7 %collective-permute-done.9.top = f32[2,128,128]{2,1,0:T(8,128)S(1)} collective-permute-done((f32[2,128,128]{2,1,0:T(8,128)S(1)}, f32[2,128,128]{2,1,0:T(8,128)S(1)}, u32[]{:S(2)}, u32[]{:S(2)}) %collective-permute-start.9) | collective-permute-done | bytes 131104 | tf_op jit(solution)/shard_map/ppermute | solution.py:395
  55.6 3.4 %collective-permute-start.12 = (f32[2,128,128]{2,1,0:T(8,128)S(1)}, f32[2,128,128]{2,1,0:T(8,128)S(1)}, u32[]{:S(2)}, u32[]{:S(2)}) collective-permute-start(f32[2,128,128]{2,1,0:T(8,128)S(1)} %get-tuple-element.150), channel_id=1, source_target_pairs={{0,1},{1,0},{2,3},{3,2},{4,5},{5,4},{6,7},{7,6},{8,9},{9,8},{10,11... | collective-permute-start | bytes 393224 | tf_op jit(solution)/shard_map/ppermute | solution.py:439
  59.1 1.0 %collective-permute-done.12.final = f32[2,128,128]{2,1,0:T(8,128)S(1)} collective-permute-done((f32[2,128,128]{2,1,0:T(8,128)S(1)}, f32[2,128,128]{2,1,0:T(8,128)S(1)}, u32[]{:S(2)}, u32[]{:S(2)}) %collective-permute-start.12) | collective-permute-done | bytes 131104 | tf_op jit(solution)/shard_map/ppermute | solution.py:439
  60.1 4.0 %shard_map.102 = (f32[1024,256]{1,0:T(8,128)}, f32[1024,256]{1,0:T(8,128)}, f32[1024,256]{1,0:T(8,128)}, f32[1024,256]{1,0:T(8,128)}) custom-call(s32[1]{0:T(128)} %bitcast.place, f32[1024,128]{1,0:T(8,128)S(1)} %get-tuple-element.124.w, bf16[1024,256]{1,0:T(8,128)(2,1)S(1)} %copy-done, bf16[1024,256]{1,0:T(8,128)(2,1)S(1)} %copy-done.2, ...), custom_call_target="tpu_custom_call" | custom-call | flops 402653184 | bytes 8388608 | tf_op jit(solution)/shard_map/pallas_call | solution.py:443
  (37 shorter events, 0.3 us)
Async XLA Ops:
  0.6 2.6 %copy-start = (bf16[1024,256]{1,0:T(8,128)(2,1)S(1)}, bf16[1024,256]{1,0:T(8,128)(2,1)}, u32[]{:S(2)}) copy-start(bf16[1024,256]{1,0:T(8,128)(2,1)} %q.11) | copy-start | bytes 1572868
  0.6 2.6 %copy-start.1 = (bf16[1024,256]{1,0:T(8,128)(2,1)S(1)}, bf16[1024,256]{1,0:T(8,128)(2,1)}, u32[]{:S(2)}) copy-start(bf16[1024,256]{1,0:T(8,128)(2,1)} %g.11) | copy-start | bytes 1572868
  3.2 13.4 %copy-start.3 = (bf16[1024,256]{1,0:T(8,128)(2,1)S(1)}, bf16[1024,256]{1,0:T(8,128)(2,1)}, u32[]{:S(2)}) copy-start(bf16[1024,256]{1,0:T(8,128)(2,1)} %v.5) | copy-start | bytes 1572868
  6.4 10.1 %copy-start.2 = (bf16[1024,256]{1,0:T(8,128)(2,1)S(1)}, bf16[1024,256]{1,0:T(8,128)(2,1)}, u32[]{:S(2)}) copy-start(bf16[1024,256]{1,0:T(8,128)(2,1)} %k.5) | copy-start | bytes 1572868
  6.4 13.3 %collective-permute-start.2 = (f32[6,2,128,128]{3,2,1,0:T(8,128)}, f32[6,2,128,128]{3,2,1,0:T(8,128)}, u32[]{:S(2)}, u32[]{:S(2)}) collective-permute-start(f32[6,2,128,128]{3,2,1,0:T(8,128)} %get-tuple-element.81.own_part), channel_id=1, source_target_pairs={{0,1},{1,0},{2,3},{3,2},{4,5},{5,4},{6,7},{7,6},{8,9},{9,8},{10,11... | collective-permute-start | bytes 2359304 | tf_op jit(solution)/shard_map/ppermute | solution.py:351
  9.6 2.5 %collective-permute-start = (f32[2,2,128,128]{3,2,1,0:T(8,128)S(1)}, f32[2,2,128,128]{3,2,1,0:T(8,128)S(1)}, u32[]{:S(2)}, u32[]{:S(2)}) collective-permute-start(f32[2,2,128,128]{3,2,1,0:T(8,128)S(1)} %get-tuple-element.78), channel_id=1, source_target_pairs={{0,1},{1,0},{2,3},{3,2},{4,5},{5,4},{6,7},{7,6},{8,9},{9,8},{10,11... | collective-permute-start | bytes 786440 | tf_op jit(solution)/shard_map/ppermute | solution.py:326
  12.2 9.2 %collective-permute-start.1 = (f32[2,128,128]{2,1,0:T(8,128)S(1)}, f32[2,128,128]{2,1,0:T(8,128)S(1)}, u32[]{:S(2)}, u32[]{:S(2)}) collective-permute-start(f32[2,128,128]{2,1,0:T(8,128)S(1)} %get-tuple-element.80), channel_id=1, source_target_pairs={{0,2},{1,193},{2,0},{3,195},{4,6},{5,197},{6,4},{7,199},{8,10},{9,... | collective-permute-start | bytes 393224 | tf_op jit(solution)/shard_map/ppermute | solution.py:395
  18.3 0.7 %copy-start.5 = (f32[256,256]{1,0:T(8,128)}, f32[256,256]{1,0:T(8,128)S(1)}, u32[]{:S(2)}) copy-start(f32[256,256]{1,0:T(8,128)S(1)} %get-tuple-element.97.refs_1_) | copy-start | bytes 786436
  19.0 0.7 %copy-start.13 = (f32[256,256]{1,0:T(8,128)}, f32[256,256]{1,0:T(8,128)S(1)}, u32[]{:S(2)}) copy-start(f32[256,256]{1,0:T(8,128)S(1)} %get-tuple-element.95.refs_1_) | copy-start | bytes 786436
  19.7 1.7 %copy-start.4 = (f32[256,256]{1,0:T(8,128)}, f32[256,256]{1,0:T(8,128)S(1)}, u32[]{:S(2)}) copy-start(f32[256,256]{1,0:T(8,128)S(1)} %get-tuple-element.96.refs_0_) | copy-start | bytes 786436
  19.7 1.7 %copy-start.12 = (f32[256,256]{1,0:T(8,128)}, f32[256,256]{1,0:T(8,128)S(1)}, u32[]{:S(2)}) copy-start(f32[256,256]{1,0:T(8,128)S(1)} %get-tuple-element.94.refs_0_) | copy-start | bytes 786436
  21.4 6.2 %collective-permute-start.3 = (f32[2,128,128]{2,1,0:T(8,128)S(1)}, f32[2,128,128]{2,1,0:T(8,128)S(1)}, u32[]{:S(2)}, u32[]{:S(2)}) collective-permute-start(f32[2,128,128]{2,1,0:T(8,128)S(1)} %get-tuple-element.162), channel_id=1, source_target_pairs={{0,6},{1,65},{2,4},{3,67},{4,2},{5,69},{6,0},{7,71},{8,14},{9,73},... | collective-permute-start | bytes 393224 | tf_op jit(solution)/shard_map/ppermute | solution.py:395
  24.4 0.7 %copy-start.14 = (f32[256,256]{1,0:T(8,128)}, f32[256,256]{1,0:T(8,128)S(1)}, u32[]{:S(2)}) copy-start(f32[256,256]{1,0:T(8,128)S(1)} %get-tuple-element.106.refs_2_) | copy-start | bytes 786436
  25.1 0.7 %copy-start.15 = (f32[256,256]{1,0:T(8,128)}, f32[256,256]{1,0:T(8,128)S(1)}, u32[]{:S(2)}) copy-start(f32[256,256]{1,0:T(8,128)S(1)} %get-tuple-element.107.refs_3_) | copy-start | bytes 786436
  25.8 1.8 %copy-start.6 = (f32[256,256]{1,0:T(8,128)}, f32[256,256]{1,0:T(8,128)S(1)}, u32[]{:S(2)}) copy-start(f32[256,256]{1,0:T(8,128)S(1)} %get-tuple-element.108.refs_2_) | copy-start | bytes 786436
  25.8 1.8 %copy-start.7 = (f32[256,256]{1,0:T(8,128)}, f32[256,256]{1,0:T(8,128)S(1)}, u32[]{:S(2)}) copy-start(f32[256,256]{1,0:T(8,128)S(1)} %get-tuple-element.109.refs_3_) | copy-start | bytes 786436
  27.7 3.9 %collective-permute-start.4 = (f32[2,128,128]{2,1,0:T(8,128)S(1)}, f32[2,128,128]{2,1,0:T(8,128)S(1)}, u32[]{:S(2)}, u32[]{:S(2)}) collective-permute-start(f32[2,128,128]{2,1,0:T(8,128)S(1)} %get-tuple-element.160), channel_id=1, source_target_pairs={{0,8},{1,33},{2,10},{3,35},{4,12},{5,37},{6,14},{7,39},{8,0},{9,41... | collective-permute-start | bytes 393224 | tf_op jit(solution)/shard_map/ppermute | solution.py:395
  29.4 0.7 %copy-start.16 = (f32[256,256]{1,0:T(8,128)}, f32[256,256]{1,0:T(8,128)S(1)}, u32[]{:S(2)}) copy-start(f32[256,256]{1,0:T(8,128)S(1)} %get-tuple-element.118.refs_4_) | copy-start | bytes 786436
  30.1 0.7 %copy-start.17 = (f32[256,256]{1,0:T(8,128)}, f32[256,256]{1,0:T(8,128)S(1)}, u32[]{:S(2)}) copy-start(f32[256,256]{1,0:T(8,128)S(1)} %get-tuple-element.119.refs_5_) | copy-start | bytes 786436
  30.8 0.8 %copy-start.8 = (f32[256,256]{1,0:T(8,128)}, f32[256,256]{1,0:T(8,128)S(1)}, u32[]{:S(2)}) copy-start(f32[256,256]{1,0:T(8,128)S(1)} %get-tuple-element.120.refs_4_) | copy-start | bytes 786436
  30.8 0.8 %copy-start.9 = (f32[256,256]{1,0:T(8,128)}, f32[256,256]{1,0:T(8,128)S(1)}, u32[]{:S(2)}) copy-start(f32[256,256]{1,0:T(8,128)S(1)} %get-tuple-element.121.refs_5_) | copy-start | bytes 786436
  31.7 6.2 %collective-permute-start.5 = (f32[2,128,128]{2,1,0:T(8,128)S(1)}, f32[2,128,128]{2,1,0:T(8,128)S(1)}, u32[]{:S(2)}, u32[]{:S(2)}) collective-permute-start(f32[2,128,128]{2,1,0:T(8,128)S(1)} %get-tuple-element.158), channel_id=1, source_target_pairs={{0,24},{1,25},{2,26},{3,27},{4,28},{5,29},{6,30},{7,31},{8,16},{9,... | collective-permute-start | bytes 393224 | tf_op jit(solution)/shard_map/ppermute | solution.py:395
  36.5 0.7 %copy-start.11 = (f32[256,256]{1,0:T(8,128)}, f32[256,256]{1,0:T(8,128)S(1)}, u32[]{:S(2)}) copy-start(f32[256,256]{1,0:T(8,128)S(1)} %get-tuple-element.133.refs_7_) | copy-start | bytes 786436
  37.2 0.7 %copy-start.19 = (f32[256,256]{1,0:T(8,128)}, f32[256,256]{1,0:T(8,128)S(1)}, u32[]{:S(2)}) copy-start(f32[256,256]{1,0:T(8,128)S(1)} %get-tuple-element.131.refs_7_) | copy-start | bytes 786436
  37.9 0.7 %copy-start.10 = (f32[256,256]{1,0:T(8,128)}, f32[256,256]{1,0:T(8,128)S(1)}, u32[]{:S(2)}) copy-start(f32[256,256]{1,0:T(8,128)S(1)} %get-tuple-element.132.refs_6_) | copy-start | bytes 786436
  37.9 0.8 %copy-start.18 = (f32[256,256]{1,0:T(8,128)}, f32[256,256]{1,0:T(8,128)S(1)}, u32[]{:S(2)}) copy-start(f32[256,256]{1,0:T(8,128)S(1)} %get-tuple-element.130.refs_6_) | copy-start | bytes 786436
  38.7 4.2 %collective-permute-start.7 = (f32[4,2,128,128]{3,2,1,0:T(8,128)S(1)}, f32[4,2,128,128]{3,2,1,0:T(8,128)S(1)}, u32[]{:S(2)}, u32[]{:S(2)}) collective-permute-start(f32[4,2,128,128]{3,2,1,0:T(8,128)S(1)} %pad_maximum_fusion.stacked), channel_id=1, source_target_pairs={{0,1},{1,0},{2,3},{3,2},{4,5},{5,4},{6,7},{7,6},{8,9},{9,8},{10,11... | collective-permute-start | bytes 1572872 | tf_op jit(solution)/shard_map/ppermute | solution.py:406
  38.7 4.2 %collective-permute-start.6 = (f32[2,128,128]{2,1,0:T(8,128)S(1)}, f32[2,128,128]{2,1,0:T(8,128)S(1)}, u32[]{:S(2)}, u32[]{:S(2)}) collective-permute-start(f32[2,128,128]{2,1,0:T(8,128)S(1)} %get-tuple-element.156), channel_id=1, source_target_pairs={{0,32},{1,9},{2,34},{3,11},{4,36},{5,13},{6,38},{7,15},{8,40},{9,1... | collective-permute-start | bytes 393224 | tf_op jit(solution)/shard_map/ppermute | solution.py:395
  43.0 7.2 %collective-permute-start.8 = (f32[2,128,128]{2,1,0:T(8,128)S(1)}, f32[2,128,128]{2,1,0:T(8,128)S(1)}, u32[]{:S(2)}, u32[]{:S(2)}) collective-permute-start(f32[2,128,128]{2,1,0:T(8,128)S(1)} %get-tuple-element.154), channel_id=1, source_target_pairs={{0,64},{1,7},{2,66},{3,5},{4,68},{5,3},{6,70},{7,1},{8,72},{9,15},... | collective-permute-start | bytes 393224 | tf_op jit(solution)/shard_map/ppermute | solution.py:395
  45.5 7.5 %collective-permute-start.10 = (f32[2,128,128]{2,1,0:T(8,128)S(1)}, f32[2,128,128]{2,1,0:T(8,128)S(1)}, u32[]{:S(2)}, u32[]{:S(2)}) collective-permute-start(f32[2,128,128]{2,1,0:T(8,128)S(1)} %collective-permute-done.6.fifth), channel_id=1, source_target_pairs={{0,1},{1,0},{2,3},{3,2},{4,5},{5,4},{6,7},{7,6},{8,9},{9,8},{10,11... | collective-permute-start | bytes 393224 | tf_op jit(solution)/shard_map/ppermute | solution.py:413
  50.2 2.8 %collective-permute-start.11 = (f32[2,128,128]{2,1,0:T(8,128)S(1)}, f32[2,128,128]{2,1,0:T(8,128)S(1)}, u32[]{:S(2)}, u32[]{:S(2)}) collective-permute-start(f32[2,128,128]{2,1,0:T(8,128)S(1)} %collective-permute-done.8.alone), channel_id=1, source_target_pairs={{0,1},{1,0},{2,3},{3,2},{4,5},{5,4},{6,7},{7,6},{8,9},{9,8},{10,11... | collective-permute-start | bytes 393224 | tf_op jit(solution)/shard_map/ppermute | solution.py:414
  51.7 3.9 %collective-permute-start.9 = (f32[2,128,128]{2,1,0:T(8,128)S(1)}, f32[2,128,128]{2,1,0:T(8,128)S(1)}, u32[]{:S(2)}, u32[]{:S(2)}) collective-permute-start(f32[2,128,128]{2,1,0:T(8,128)S(1)} %get-tuple-element.152), channel_id=1, source_target_pairs={{0,192},{1,3},{2,194},{3,1},{4,196},{5,7},{6,198},{7,5},{8,200},{9... | collective-permute-start | bytes 393224 | tf_op jit(solution)/shard_map/ppermute | solution.py:395
  55.6 4.4 %collective-permute-start.12 = (f32[2,128,128]{2,1,0:T(8,128)S(1)}, f32[2,128,128]{2,1,0:T(8,128)S(1)}, u32[]{:S(2)}, u32[]{:S(2)}) collective-permute-start(f32[2,128,128]{2,1,0:T(8,128)S(1)} %get-tuple-element.150), channel_id=1, source_target_pairs={{0,1},{1,0},{2,3},{3,2},{4,5},{5,4},{6,7},{7,6},{8,9},{9,8},{10,11... | collective-permute-start | bytes 393224 | tf_op jit(solution)/shard_map/ppermute | solution.py:439

commit v4 on v3

--- a/solution.py
+++ b/solution.py
@@ -249,21 +249,23 @@
             state[h] = jnp.where((own >> far - 1 & 1) == 1, highest, 0.0).astype(BF16)
             pulled[h] = jnp.where(on_first, final[h], carried[h]).astype(BF16)
 
-    for i in range(q.shape[0] // BLOCK):
-
-        @pl.when(step == i)
-        def _(i=i):
-            rows = slice(i * BLOCK, (i + 1) * BLOCK)
-            fetches[2 * i].wait()
-            fetches[2 * i + 1].wait()
+    for n in range(q.shape[0] // SMALL):
+
+        @pl.when(step == n)
+        def _(n=n):
+            i, start = n * SMALL // BLOCK, n * SMALL % BLOCK
+            rows, part = slice(n * SMALL, (n + 1) * SMALL), slice(start, start + SMALL)
+            if start == 0:
+                fetches[2 * i].wait()
+                fetches[2 * i + 1].wait()
             for h in range(heads):
                 lanes = slice(h * width, (h + 1) * width)
                 at = h * STRIDE + first_far + far - 1
                 scale = w[rows, at : at + 1]
                 out[:, lanes] = far_out[rows, lanes] + scale * contract(q[rows, lanes], state[h], 1, 0)
                 dq[:, lanes] = far_dq[rows, lanes] + scale * contract(g[rows, lanes], state[h], 1, 1)
-                dk[:, lanes] = near[2 * i, :, lanes] + contract(v[rows, lanes], pulled[h], 1, 0)
-                dv[:, lanes] = near[2 * i + 1, :, lanes] + contract(k[rows, lanes], pulled[h], 1, 1)
+                dk[:, lanes] = near[2 * i, part, lanes] + contract(v[rows, lanes], pulled[h], 1, 0)
+                dv[:, lanes] = near[2 * i + 1, part, lanes] + contract(k[rows, lanes], pulled[h], 1, 1)
 
 
 def links(row_bits, col_bits):
@@ -438,14 +440,14 @@
     top = received[-1]
     final = lax.ppermute(jnp.where(on_first, top, carried + low_grads), AXES, exchange)
 
-    wide = pl.BlockSpec((BLOCK, columns), lambda i: (i, 0))
+    wide = pl.BlockSpec((SMALL, columns), lambda i: (i, 0))
     seconds = outside(*[part for i in range(blocks) for part in local[4 * i + 2 : 4 * i + 4]])
     return call(
         functools.partial(last_kernel, width, heads, far, first_far),
         [full((tokens, columns))] * 4,
         6 * unit,
         16 * array,
-        grid=(blocks,),
+        grid=(tokens // SMALL,),
         in_specs=[smem] + [VMEM] * 5 + [pl.BlockSpec()] * 3 + [VMEM] * 2 + [HBM] * len(seconds),
         out_specs=[wide] * 4,
         scratch_shapes=[

time: 64.4 us -> 66.2 us (1.028)
  Pallas kernels: 23 us -> 24.8 us
    pallas_call x1, Pallas kernels: 3.96 us -> 5.78 us  [shards(): call(functools.partial(last_kernel, width, heads, far, first_far), [full(...]
  transfers between devices with their start and end apart: 13 -> 13, of which waited for: 6 -> 6; matrix products, arithmetic and copies ran while one was open for 0% -> 0% of each run, Pallas kernels for 21% -> 20%
where the time goes in v4:
time: 66.2 us; the launch traced here: 66 us
  Pallas kernels  24.8 us (37%)
  starting transfers between devices  21.7 us (33%)
  waiting for transfers between devices  11.8 us (18%)
  local copies, waits for them, and re-layouts  6.49 us (10%)
  between operations  1.04 us (2%)
    ppermute x7, starting transfers between devices, shards(): got = lax.ppermute(send, AXES, pairs)  12.7 us
    ppermute x7, waiting for transfers between devices, shards(): got = lax.ppermute(send, AXES, pairs)  8.27 us
    pallas_call x4, Pallas kernels, tile(): call(functools.partial(tile_kernel, i, width, heads, depth, first_far), [...  6.93 us
    unnamed x40, local copies, waits for them, and re-layouts  6.49 us
    pallas_call x1, Pallas kernels, shards(): call(functools.partial(last_kernel, width, heads, far, first_far), [full(...  5.78 us
    pallas_call x1, Pallas kernels, add_far(): call(functools.partial(far_kernel, width, heads, far - 4, first_far), [fu...  3.78 us
    ppermute x1, starting transfers between devices, shards(): lax.ppermute(jnp.where(on_first, top, carried + low_grads), AXES, exchange)  3.45 us
    pallas_call x1, Pallas kernels, second(): call(functools.partial(second_kernel, first_far, width, heads, far), (ful...  3.21 us
  transfers between devices with their start and end apart: 13, of which 6 were waited for; matrix products, arithmetic and copies ran while one was open for 0% of the time, Pallas kernels for 20%

profile of v4, /device:TPU:1, one launch (start us, length us, event | category | flops | bytes accessed | tf_op | source)
XLA Modules:
  0.0 66.0 jit_solution(17550287950643738054)
XLA Ops:
  0.7 2.5 %shard_map.93 = (f32[1024,128]{1,0:T(8,128)S(1)}, f32[2,2,128,128]{3,2,1,0:T(8,128)S(1)}) custom-call(s32[1,1024]{1,0:T(1,128)} %bitcast.19, f32[21,2,64]{2,1,0:T(2,128)} %bitcast.18, bf16[1024,256]{1,0:T(8,128)(2,1)} %q.11, bf16[1024,256]{1,0:T(8,128)(2,1)} %k.5, bf16[1024,256]{1,0:T(8,128)(2,1)} %v.5, bf16[1024,256]{1,0:T(8,128)(2,1)} %g.11), custom_call_target="tpu_custom_call" | custom-call | flops 201326592 | bytes 2097152 | tf_op jit(solution)/shard_map/pallas_call | solution.py:314
  3.2 0.0 copy-start.3
  3.2 3.2 %shard_map.94 = (f32[2,128,128]{2,1,0:T(8,128)S(1)}, f32[6,2,128,128]{3,2,1,0:T(8,128)}) custom-call(f32[1024,128]{1,0:T(8,128)S(1)} %get-tuple-element.124.w, bf16[1024,256]{1,0:T(8,128)(2,1)S(1)} %copy-done, bf16[1024,256]{1,0:T(8,128)(2,1)S(1)} %copy-done.1), custom_call_target="tpu_custom_call" | custom-call | flops 536870912 | bytes 2097152 | tf_op jit(solution)/shard_map/pallas_call | solution.py:331
  6.4 3.2 %collective-permute-start.2 = (f32[6,2,128,128]{3,2,1,0:T(8,128)}, f32[6,2,128,128]{3,2,1,0:T(8,128)}, u32[]{:S(2)}, u32[]{:S(2)}) collective-permute-start(f32[6,2,128,128]{3,2,1,0:T(8,128)} %get-tuple-element.81.own_part), channel_id=1, source_target_pairs={{0,1},{1,0},{2,3},{3,2},{4,5},{5,4},{6,7},{7,6},{8,9},{9,8},{10,11... | collective-permute-start | bytes 2359304 | tf_op jit(solution)/shard_map/ppermute | solution.py:353
  9.6 0.0 collective-permute-start
  9.6 2.5 %collective-permute-done.ends = f32[2,2,128,128]{3,2,1,0:T(8,128)S(1)} collective-permute-done((f32[2,2,128,128]{3,2,1,0:T(8,128)S(1)}, f32[2,2,128,128]{3,2,1,0:T(8,128)S(1)}, u32[]{:S(2)}, u32[]{:S(2)}) %collective-permute-start) | collective-permute-done | bytes 262176 | tf_op jit(solution)/shard_map/ppermute | solution.py:328
  12.2 4.4 %collective-permute-start.1 = (f32[2,128,128]{2,1,0:T(8,128)S(1)}, f32[2,128,128]{2,1,0:T(8,128)S(1)}, u32[]{:S(2)}, u32[]{:S(2)}) collective-permute-start(f32[2,128,128]{2,1,0:T(8,128)S(1)} %get-tuple-element.80), channel_id=1, source_target_pairs={{0,2},{1,193},{2,0},{3,195},{4,6},{5,197},{6,4},{7,199},{8,10},{9,... | collective-permute-start | bytes 393224 | tf_op jit(solution)/shard_map/ppermute | solution.py:397
  16.6 1.7 %shard_map.96 = (f32[256,256]{1,0:T(8,128)S(1)}, f32[256,256]{1,0:T(8,128)S(1)}, f32[256,256]{1,0:T(8,128)S(1)}, f32[256,256]{1,0:T(8,128)S(1)}) custom-call(s32[1]{0:T(128)} %bitcast.place, f32[1024,128]{1,0:T(8,128)S(1)} %get-tuple-element.124.w, bf16[1024,256]{1,0:T(8,128)(2,1)S(1)} %copy-done, bf16[1024,256]{1,0:T(8,128)(2,1)S(1)} %copy-done.2, ...), custom_call_target="tpu_custom_call" | custom-call | flops 335544320 | bytes 3145728 | tf_op jit(solution)/shard_map/pallas_call | solution.py:344
  18.3 0.7 %copy-done.5 = f32[256,256]{1,0:T(8,128)} copy-done((f32[256,256]{1,0:T(8,128)}, f32[256,256]{1,0:T(8,128)S(1)}, u32[]{:S(2)}) %copy-start.5) | copy-done | bytes 262168
  19.0 0.7 %copy-done.13 = f32[256,256]{1,0:T(8,128)} copy-done((f32[256,256]{1,0:T(8,128)}, f32[256,256]{1,0:T(8,128)S(1)}, u32[]{:S(2)}) %copy-start.13) | copy-done | bytes 262168
  19.7 0.0 collective-permute-done.2.from_other
  19.7 1.6 %shard_map.95 = (f32[2,128,128]{2,1,0:T(8,128)S(1)}, f32[2,128,128]{2,1,0:T(8,128)S(1)}, f32[2,128,128]{2,1,0:T(8,128)S(1)}, f32[2,128,128]{2,1,0:T(8,128)S(1)},...) custom-call(s32[1]{0:T(128)} %bitcast.place, f32[6,2,128,128]{3,2,1,0:T(8,128)} %get-tuple-element.81.own_part, ...), custom_call_target="tpu_custom_call" | custom-call | flops 131072 | bytes 524288 | tf_op jit(solution)/shard_map/pallas_call | solution.py:356
  21.4 0.0 collective-permute-done.1
  21.4 1.3 %collective-permute-start.3 = (f32[2,128,128]{2,1,0:T(8,128)S(1)}, f32[2,128,128]{2,1,0:T(8,128)S(1)}, u32[]{:S(2)}, u32[]{:S(2)}) collective-permute-start(f32[2,128,128]{2,1,0:T(8,128)S(1)} %get-tuple-element.162), channel_id=1, source_target_pairs={{0,6},{1,65},{2,4},{3,67},{4,2},{5,69},{6,0},{7,71},{8,14},{9,73},... | collective-permute-start | bytes 393224 | tf_op jit(solution)/shard_map/ppermute | solution.py:397
  22.7 1.8 %shard_map.97 = (f32[256,256]{1,0:T(8,128)S(1)}, f32[256,256]{1,0:T(8,128)S(1)}, f32[256,256]{1,0:T(8,128)S(1)}, f32[256,256]{1,0:T(8,128)S(1)}) custom-call(s32[1]{0:T(128)} %bitcast.place, f32[1024,128]{1,0:T(8,128)S(1)} %get-tuple-element.124.w, bf16[1024,256]{1,0:T(8,128)(2,1)S(1)} %copy-done, bf16[1024,256]{1,0:T(8,128)(2,1)S(1)} %copy-done.2, ...), custom_call_target="tpu_custom_call" | custom-call | flops 335544320 | bytes 3145728 | tf_op jit(solution)/shard_map/pallas_call | solution.py:344
  24.4 0.0 copy-start.14
  24.5 0.7 %copy-done.14 = f32[256,256]{1,0:T(8,128)} copy-done((f32[256,256]{1,0:T(8,128)}, f32[256,256]{1,0:T(8,128)S(1)}, u32[]{:S(2)}) %copy-start.14) | copy-done | bytes 262168
  25.1 0.7 %copy-done.15 = f32[256,256]{1,0:T(8,128)} copy-done((f32[256,256]{1,0:T(8,128)}, f32[256,256]{1,0:T(8,128)S(1)}, u32[]{:S(2)}) %copy-start.15) | copy-done | bytes 262168
  25.9 1.8 %collective-permute-done.3 = f32[2,128,128]{2,1,0:T(8,128)S(1)} collective-permute-done((f32[2,128,128]{2,1,0:T(8,128)S(1)}, f32[2,128,128]{2,1,0:T(8,128)S(1)}, u32[]{:S(2)}, u32[]{:S(2)}) %collective-permute-start.3) | collective-permute-done | bytes 131104 | tf_op jit(solution)/shard_map/ppermute | solution.py:397
  27.7 0.1 collective-permute-start.4
  27.8 1.6 %shard_map.98 = (f32[256,256]{1,0:T(8,128)S(1)}, f32[256,256]{1,0:T(8,128)S(1)}, f32[256,256]{1,0:T(8,128)S(1)}, f32[256,256]{1,0:T(8,128)S(1)}) custom-call(s32[1]{0:T(128)} %bitcast.place, f32[1024,128]{1,0:T(8,128)S(1)} %get-tuple-element.124.w, bf16[1024,256]{1,0:T(8,128)(2,1)S(1)} %copy-done, bf16[1024,256]{1,0:T(8,128)(2,1)S(1)} %copy-done.2, ...), custom_call_target="tpu_custom_call" | custom-call | flops 335544320 | bytes 3145728 | tf_op jit(solution)/shard_map/pallas_call | solution.py:344
  29.4 0.7 %copy-done.16 = f32[256,256]{1,0:T(8,128)} copy-done((f32[256,256]{1,0:T(8,128)}, f32[256,256]{1,0:T(8,128)S(1)}, u32[]{:S(2)}) %copy-start.16) | copy-done | bytes 262168
  30.1 0.7 %copy-done.17 = f32[256,256]{1,0:T(8,128)} copy-done((f32[256,256]{1,0:T(8,128)}, f32[256,256]{1,0:T(8,128)S(1)}, u32[]{:S(2)}) %copy-start.17) | copy-done | bytes 262168
  30.8 0.7 %collective-permute-done.4 = f32[2,128,128]{2,1,0:T(8,128)S(1)} collective-permute-done((f32[2,128,128]{2,1,0:T(8,128)S(1)}, f32[2,128,128]{2,1,0:T(8,128)S(1)}, u32[]{:S(2)}, u32[]{:S(2)}) %collective-permute-start.4) | collective-permute-done | bytes 131104 | tf_op jit(solution)/shard_map/ppermute | solution.py:397
  31.6 0.1 copy-done.9
  31.7 2.9 %collective-permute-start.5 = (f32[2,128,128]{2,1,0:T(8,128)S(1)}, f32[2,128,128]{2,1,0:T(8,128)S(1)}, u32[]{:S(2)}, u32[]{:S(2)}) collective-permute-start(f32[2,128,128]{2,1,0:T(8,128)S(1)} %get-tuple-element.158), channel_id=1, source_target_pairs={{0,24},{1,25},{2,26},{3,27},{4,28},{5,29},{6,30},{7,31},{8,16},{9,... | collective-permute-start | bytes 393224 | tf_op jit(solution)/shard_map/ppermute | solution.py:397
  34.6 1.8 %shard_map.99 = (f32[256,256]{1,0:T(8,128)S(1)}, f32[256,256]{1,0:T(8,128)S(1)}, f32[256,256]{1,0:T(8,128)S(1)}, f32[256,256]{1,0:T(8,128)S(1)}) custom-call(s32[1]{0:T(128)} %bitcast.place, f32[1024,128]{1,0:T(8,128)S(1)} %get-tuple-element.124.w, bf16[1024,256]{1,0:T(8,128)(2,1)S(1)} %copy-done, bf16[1024,256]{1,0:T(8,128)(2,1)S(1)} %copy-done.2, ...), custom_call_target="tpu_custom_call" | custom-call | flops 335544320 | bytes 3145728 | tf_op jit(solution)/shard_map/pallas_call | solution.py:344
  36.5 0.7 %copy-done.11 = f32[256,256]{1,0:T(8,128)} copy-done((f32[256,256]{1,0:T(8,128)}, f32[256,256]{1,0:T(8,128)S(1)}, u32[]{:S(2)}) %copy-start.11) | copy-done | bytes 262168
  37.2 0.7 %copy-done.19 = f32[256,256]{1,0:T(8,128)} copy-done((f32[256,256]{1,0:T(8,128)}, f32[256,256]{1,0:T(8,128)S(1)}, u32[]{:S(2)}) %copy-start.19) | copy-done | bytes 262168
  37.9 0.0 collective-permute-done.5
  37.9 0.7 %copy-done.10 = f32[256,256]{1,0:T(8,128)} copy-done((f32[256,256]{1,0:T(8,128)}, f32[256,256]{1,0:T(8,128)S(1)}, u32[]{:S(2)}) %copy-start.10) | copy-done | bytes 262168
  38.6 0.1 copy-done.18
  38.7 0.0 collective-permute-start.7
  38.7 0.1 collective-permute-start.6
  38.8 4.1 %collective-permute-done.6.fifth = f32[2,128,128]{2,1,0:T(8,128)S(1)} collective-permute-done((f32[2,128,128]{2,1,0:T(8,128)S(1)}, f32[2,128,128]{2,1,0:T(8,128)S(1)}, u32[]{:S(2)}, u32[]{:S(2)}) %collective-permute-start.6) | collective-permute-done | bytes 131104 | tf_op jit(solution)/shard_map/ppermute | solution.py:397
  42.9 0.0 collective-permute-done.7.handed
  43.0 2.6 %collective-permute-start.8 = (f32[2,128,128]{2,1,0:T(8,128)S(1)}, f32[2,128,128]{2,1,0:T(8,128)S(1)}, u32[]{:S(2)}, u32[]{:S(2)}) collective-permute-start(f32[2,128,128]{2,1,0:T(8,128)S(1)} %get-tuple-element.154), channel_id=1, source_target_pairs={{0,64},{1,7},{2,66},{3,5},{4,68},{5,3},{6,70},{7,1},{8,72},{9,15},... | collective-permute-start | bytes 393224 | tf_op jit(solution)/shard_map/ppermute | solution.py:397
  45.5 0.8 %collective-permute-start.10 = (f32[2,128,128]{2,1,0:T(8,128)S(1)}, f32[2,128,128]{2,1,0:T(8,128)S(1)}, u32[]{:S(2)}, u32[]{:S(2)}) collective-permute-start(f32[2,128,128]{2,1,0:T(8,128)S(1)} %collective-permute-done.6.fifth), channel_id=1, source_target_pairs={{0,1},{1,0},{2,3},{3,2},{4,5},{5,4},{6,7},{7,6},{8,9},{9,8},{10,11... | collective-permute-start | bytes 393224 | tf_op jit(solution)/shard_map/ppermute | solution.py:415
  46.4 3.8 %shard_map.100 = (f32[1024,256]{1,0:T(8,128)S(1)}, f32[1024,256]{1,0:T(8,128)S(1)}) custom-call(s32[1]{0:T(128)} %bitcast.place, f32[1024,128]{1,0:T(8,128)S(1)} %get-tuple-element.124.w, bf16[1024,256]{1,0:T(8,128)(2,1)S(1)} %copy-done, bf16[1024,256]{1,0:T(8,128)(2,1)S(1)} %copy-done.1, f32[4,2,128,128]{3,2,1,0:T(8,128)S(1)} %pad_maximum_fusion.stacked, ...), custom_call_target="tpu_custom_call" | custom-call | flops 536870912 | bytes 4194304 | tf_op jit(solution)/shard_map/pallas_call | solution.py:367
  50.2 0.0 collective-permute-done.8.alone
  50.2 1.5 %collective-permute-start.11 = (f32[2,128,128]{2,1,0:T(8,128)S(1)}, f32[2,128,128]{2,1,0:T(8,128)S(1)}, u32[]{:S(2)}, u32[]{:S(2)}) collective-permute-start(f32[2,128,128]{2,1,0:T(8,128)S(1)} %collective-permute-done.8.alone), channel_id=1, source_target_pairs={{0,1},{1,0},{2,3},{3,2},{4,5},{5,4},{6,7},{7,6},{8,9},{9,8},{10,11... | collective-permute-start | bytes 393224 | tf_op jit(solution)/shard_map/ppermute | solution.py:416
  51.7 1.3 %collective-permute-start.9 = (f32[2,128,128]{2,1,0:T(8,128)S(1)}, f32[2,128,128]{2,1,0:T(8,128)S(1)}, u32[]{:S(2)}, u32[]{:S(2)}) collective-permute-start(f32[2,128,128]{2,1,0:T(8,128)S(1)} %get-tuple-element.152), channel_id=1, source_target_pairs={{0,192},{1,3},{2,194},{3,1},{4,196},{5,7},{6,198},{7,5},{8,200},{9... | collective-permute-start | bytes 393224 | tf_op jit(solution)/shard_map/ppermute | solution.py:397
  53.0 0.0 collective-permute-done.10.fifth_in
  53.0 0.9 %shard_map.101 = (f32[1024,256]{1,0:T(8,128)S(1)}, f32[1024,256]{1,0:T(8,128)S(1)}) custom-call(s32[1]{0:T(128)} %bitcast.place, f32[1024,128]{1,0:T(8,128)S(1)} %get-tuple-element.124.w, bf16[1024,256]{1,0:T(8,128)(2,1)S(1)} %copy-done, bf16[1024,256]{1,0:T(8,128)(2,1)S(1)} %copy-done.1, f32[2,128,128]{2,1,0:T(8,128)S(1)} %collective-permute-done.6.fifth, ...), custom_call_target="tpu_custom_call" | custom-call | flops 268435456 | bytes 4194304 | tf_op jit(solution)/shard_map/pallas_call | solution.py:417
  54.0 1.7 %collective-permute-done.9.top = f32[2,128,128]{2,1,0:T(8,128)S(1)} collective-permute-done((f32[2,128,128]{2,1,0:T(8,128)S(1)}, f32[2,128,128]{2,1,0:T(8,128)S(1)}, u32[]{:S(2)}, u32[]{:S(2)}) %collective-permute-start.9) | collective-permute-done | bytes 131104 | tf_op jit(solution)/shard_map/ppermute | solution.py:397
  55.6 3.4 %collective-permute-start.12 = (f32[2,128,128]{2,1,0:T(8,128)S(1)}, f32[2,128,128]{2,1,0:T(8,128)S(1)}, u32[]{:S(2)}, u32[]{:S(2)}) collective-permute-start(f32[2,128,128]{2,1,0:T(8,128)S(1)} %get-tuple-element.150), channel_id=1, source_target_pairs={{0,1},{1,0},{2,3},{3,2},{4,5},{5,4},{6,7},{7,6},{8,9},{9,8},{10,11... | collective-permute-start | bytes 393224 | tf_op jit(solution)/shard_map/ppermute | solution.py:441
  59.1 1.0 %collective-permute-done.12.final = f32[2,128,128]{2,1,0:T(8,128)S(1)} collective-permute-done((f32[2,128,128]{2,1,0:T(8,128)S(1)}, f32[2,128,128]{2,1,0:T(8,128)S(1)}, u32[]{:S(2)}, u32[]{:S(2)}) %collective-permute-start.12) | collective-permute-done | bytes 131104 | tf_op jit(solution)/shard_map/ppermute | solution.py:441
  60.1 5.8 %shard_map.102 = (f32[1024,256]{1,0:T(8,128)}, f32[1024,256]{1,0:T(8,128)}, f32[1024,256]{1,0:T(8,128)}, f32[1024,256]{1,0:T(8,128)}) custom-call(s32[1]{0:T(128)} %bitcast.place, f32[1024,128]{1,0:T(8,128)S(1)} %get-tuple-element.124.w, bf16[1024,256]{1,0:T(8,128)(2,1)S(1)} %copy-done, bf16[1024,256]{1,0:T(8,128)(2,1)S(1)} %copy-done.2, ...), custom_call_target="tpu_custom_call" | custom-call | flops 402653184 | bytes 8388608 | tf_op jit(solution)/shard_map/pallas_call | solution.py:445
  (37 shorter events, 0.3 us)
Async XLA Ops:
  0.6 2.6 %copy-start = (bf16[1024,256]{1,0:T(8,128)(2,1)S(1)}, bf16[1024,256]{1,0:T(8,128)(2,1)}, u32[]{:S(2)}) copy-start(bf16[1024,256]{1,0:T(8,128)(2,1)} %q.11) | copy-start | bytes 1572868
  0.6 2.6 %copy-start.1 = (bf16[1024,256]{1,0:T(8,128)(2,1)S(1)}, bf16[1024,256]{1,0:T(8,128)(2,1)}, u32[]{:S(2)}) copy-start(bf16[1024,256]{1,0:T(8,128)(2,1)} %g.11) | copy-start | bytes 1572868
  3.2 13.4 %copy-start.3 = (bf16[1024,256]{1,0:T(8,128)(2,1)S(1)}, bf16[1024,256]{1,0:T(8,128)(2,1)}, u32[]{:S(2)}) copy-start(bf16[1024,256]{1,0:T(8,128)(2,1)} %v.5) | copy-start | bytes 1572868
  6.4 10.1 %copy-start.2 = (bf16[1024,256]{1,0:T(8,128)(2,1)S(1)}, bf16[1024,256]{1,0:T(8,128)(2,1)}, u32[]{:S(2)}) copy-start(bf16[1024,256]{1,0:T(8,128)(2,1)} %k.5) | copy-start | bytes 1572868
  6.4 13.3 %collective-permute-start.2 = (f32[6,2,128,128]{3,2,1,0:T(8,128)}, f32[6,2,128,128]{3,2,1,0:T(8,128)}, u32[]{:S(2)}, u32[]{:S(2)}) collective-permute-start(f32[6,2,128,128]{3,2,1,0:T(8,128)} %get-tuple-element.81.own_part), channel_id=1, source_target_pairs={{0,1},{1,0},{2,3},{3,2},{4,5},{5,4},{6,7},{7,6},{8,9},{9,8},{10,11... | collective-permute-start | bytes 2359304 | tf_op jit(solution)/shard_map/ppermute | solution.py:353
  9.6 2.5 %collective-permute-start = (f32[2,2,128,128]{3,2,1,0:T(8,128)S(1)}, f32[2,2,128,128]{3,2,1,0:T(8,128)S(1)}, u32[]{:S(2)}, u32[]{:S(2)}) collective-permute-start(f32[2,2,128,128]{3,2,1,0:T(8,128)S(1)} %get-tuple-element.78), channel_id=1, source_target_pairs={{0,1},{1,0},{2,3},{3,2},{4,5},{5,4},{6,7},{7,6},{8,9},{9,8},{10,11... | collective-permute-start | bytes 786440 | tf_op jit(solution)/shard_map/ppermute | solution.py:328
  12.2 9.2 %collective-permute-start.1 = (f32[2,128,128]{2,1,0:T(8,128)S(1)}, f32[2,128,128]{2,1,0:T(8,128)S(1)}, u32[]{:S(2)}, u32[]{:S(2)}) collective-permute-start(f32[2,128,128]{2,1,0:T(8,128)S(1)} %get-tuple-element.80), channel_id=1, source_target_pairs={{0,2},{1,193},{2,0},{3,195},{4,6},{5,197},{6,4},{7,199},{8,10},{9,... | collective-permute-start | bytes 393224 | tf_op jit(solution)/shard_map/ppermute | solution.py:397
  18.3 0.7 %copy-start.5 = (f32[256,256]{1,0:T(8,128)}, f32[256,256]{1,0:T(8,128)S(1)}, u32[]{:S(2)}) copy-start(f32[256,256]{1,0:T(8,128)S(1)} %get-tuple-element.97.refs_1_) | copy-start | bytes 786436
  19.0 0.7 %copy-start.13 = (f32[256,256]{1,0:T(8,128)}, f32[256,256]{1,0:T(8,128)S(1)}, u32[]{:S(2)}) copy-start(f32[256,256]{1,0:T(8,128)S(1)} %get-tuple-element.95.refs_1_) | copy-start | bytes 786436
  19.7 1.7 %copy-start.4 = (f32[256,256]{1,0:T(8,128)}, f32[256,256]{1,0:T(8,128)S(1)}, u32[]{:S(2)}) copy-start(f32[256,256]{1,0:T(8,128)S(1)} %get-tuple-element.96.refs_0_) | copy-start | bytes 786436
  19.7 1.7 %copy-start.12 = (f32[256,256]{1,0:T(8,128)}, f32[256,256]{1,0:T(8,128)S(1)}, u32[]{:S(2)}) copy-start(f32[256,256]{1,0:T(8,128)S(1)} %get-tuple-element.94.refs_0_) | copy-start | bytes 786436
  21.4 6.2 %collective-permute-start.3 = (f32[2,128,128]{2,1,0:T(8,128)S(1)}, f32[2,128,128]{2,1,0:T(8,128)S(1)}, u32[]{:S(2)}, u32[]{:S(2)}) collective-permute-start(f32[2,128,128]{2,1,0:T(8,128)S(1)} %get-tuple-element.162), channel_id=1, source_target_pairs={{0,6},{1,65},{2,4},{3,67},{4,2},{5,69},{6,0},{7,71},{8,14},{9,73},... | collective-permute-start | bytes 393224 | tf_op jit(solution)/shard_map/ppermute | solution.py:397
  24.4 0.7 %copy-start.14 = (f32[256,256]{1,0:T(8,128)}, f32[256,256]{1,0:T(8,128)S(1)}, u32[]{:S(2)}) copy-start(f32[256,256]{1,0:T(8,128)S(1)} %get-tuple-element.106.refs_2_) | copy-start | bytes 786436
  25.1 0.7 %copy-start.15 = (f32[256,256]{1,0:T(8,128)}, f32[256,256]{1,0:T(8,128)S(1)}, u32[]{:S(2)}) copy-start(f32[256,256]{1,0:T(8,128)S(1)} %get-tuple-element.107.refs_3_) | copy-start | bytes 786436
  25.8 1.8 %copy-start.6 = (f32[256,256]{1,0:T(8,128)}, f32[256,256]{1,0:T(8,128)S(1)}, u32[]{:S(2)}) copy-start(f32[256,256]{1,0:T(8,128)S(1)} %get-tuple-element.108.refs_2_) | copy-start | bytes 786436
  25.8 1.8 %copy-start.7 = (f32[256,256]{1,0:T(8,128)}, f32[256,256]{1,0:T(8,128)S(1)}, u32[]{:S(2)}) copy-start(f32[256,256]{1,0:T(8,128)S(1)} %get-tuple-element.109.refs_3_) | copy-start | bytes 786436
  27.7 3.9 %collective-permute-start.4 = (f32[2,128,128]{2,1,0:T(8,128)S(1)}, f32[2,128,128]{2,1,0:T(8,128)S(1)}, u32[]{:S(2)}, u32[]{:S(2)}) collective-permute-start(f32[2,128,128]{2,1,0:T(8,128)S(1)} %get-tuple-element.160), channel_id=1, source_target_pairs={{0,8},{1,33},{2,10},{3,35},{4,12},{5,37},{6,14},{7,39},{8,0},{9,41... | collective-permute-start | bytes 393224 | tf_op jit(solution)/shard_map/ppermute | solution.py:397
  29.4 0.7 %copy-start.16 = (f32[256,256]{1,0:T(8,128)}, f32[256,256]{1,0:T(8,128)S(1)}, u32[]{:S(2)}) copy-start(f32[256,256]{1,0:T(8,128)S(1)} %get-tuple-element.118.refs_4_) | copy-start | bytes 786436
  30.1 0.7 %copy-start.17 = (f32[256,256]{1,0:T(8,128)}, f32[256,256]{1,0:T(8,128)S(1)}, u32[]{:S(2)}) copy-start(f32[256,256]{1,0:T(8,128)S(1)} %get-tuple-element.119.refs_5_) | copy-start | bytes 786436
  30.8 0.8 %copy-start.8 = (f32[256,256]{1,0:T(8,128)}, f32[256,256]{1,0:T(8,128)S(1)}, u32[]{:S(2)}) copy-start(f32[256,256]{1,0:T(8,128)S(1)} %get-tuple-element.120.refs_4_) | copy-start | bytes 786436
  30.8 0.8 %copy-start.9 = (f32[256,256]{1,0:T(8,128)}, f32[256,256]{1,0:T(8,128)S(1)}, u32[]{:S(2)}) copy-start(f32[256,256]{1,0:T(8,128)S(1)} %get-tuple-element.121.refs_5_) | copy-start | bytes 786436
  31.7 6.2 %collective-permute-start.5 = (f32[2,128,128]{2,1,0:T(8,128)S(1)}, f32[2,128,128]{2,1,0:T(8,128)S(1)}, u32[]{:S(2)}, u32[]{:S(2)}) collective-permute-start(f32[2,128,128]{2,1,0:T(8,128)S(1)} %get-tuple-element.158), channel_id=1, source_target_pairs={{0,24},{1,25},{2,26},{3,27},{4,28},{5,29},{6,30},{7,31},{8,16},{9,... | collective-permute-start | bytes 393224 | tf_op jit(solution)/shard_map/ppermute | solution.py:397
  36.5 0.7 %copy-start.11 = (f32[256,256]{1,0:T(8,128)}, f32[256,256]{1,0:T(8,128)S(1)}, u32[]{:S(2)}) copy-start(f32[256,256]{1,0:T(8,128)S(1)} %get-tuple-element.133.refs_7_) | copy-start | bytes 786436
  37.2 0.7 %copy-start.19 = (f32[256,256]{1,0:T(8,128)}, f32[256,256]{1,0:T(8,128)S(1)}, u32[]{:S(2)}) copy-start(f32[256,256]{1,0:T(8,128)S(1)} %get-tuple-element.131.refs_7_) | copy-start | bytes 786436
  37.9 0.7 %copy-start.10 = (f32[256,256]{1,0:T(8,128)}, f32[256,256]{1,0:T(8,128)S(1)}, u32[]{:S(2)}) copy-start(f32[256,256]{1,0:T(8,128)S(1)} %get-tuple-element.132.refs_6_) | copy-start | bytes 786436
  37.9 0.8 %copy-start.18 = (f32[256,256]{1,0:T(8,128)}, f32[256,256]{1,0:T(8,128)S(1)}, u32[]{:S(2)}) copy-start(f32[256,256]{1,0:T(8,128)S(1)} %get-tuple-element.130.refs_6_) | copy-start | bytes 786436
  38.7 4.2 %collective-permute-start.7 = (f32[4,2,128,128]{3,2,1,0:T(8,128)S(1)}, f32[4,2,128,128]{3,2,1,0:T(8,128)S(1)}, u32[]{:S(2)}, u32[]{:S(2)}) collective-permute-start(f32[4,2,128,128]{3,2,1,0:T(8,128)S(1)} %pad_maximum_fusion.stacked), channel_id=1, source_target_pairs={{0,1},{1,0},{2,3},{3,2},{4,5},{5,4},{6,7},{7,6},{8,9},{9,8},{10,11... | collective-permute-start | bytes 1572872 | tf_op jit(solution)/shard_map/ppermute | solution.py:408
  38.7 4.2 %collective-permute-start.6 = (f32[2,128,128]{2,1,0:T(8,128)S(1)}, f32[2,128,128]{2,1,0:T(8,128)S(1)}, u32[]{:S(2)}, u32[]{:S(2)}) collective-permute-start(f32[2,128,128]{2,1,0:T(8,128)S(1)} %get-tuple-element.156), channel_id=1, source_target_pairs={{0,32},{1,9},{2,34},{3,11},{4,36},{5,13},{6,38},{7,15},{8,40},{9,1... | collective-permute-start | bytes 393224 | tf_op jit(solution)/shard_map/ppermute | solution.py:397
  43.0 7.2 %collective-permute-start.8 = (f32[2,128,128]{2,1,0:T(8,128)S(1)}, f32[2,128,128]{2,1,0:T(8,128)S(1)}, u32[]{:S(2)}, u32[]{:S(2)}) collective-permute-start(f32[2,128,128]{2,1,0:T(8,128)S(1)} %get-tuple-element.154), channel_id=1, source_target_pairs={{0,64},{1,7},{2,66},{3,5},{4,68},{5,3},{6,70},{7,1},{8,72},{9,15},... | collective-permute-start | bytes 393224 | tf_op jit(solution)/shard_map/ppermute | solution.py:397
  45.5 7.5 %collective-permute-start.10 = (f32[2,128,128]{2,1,0:T(8,128)S(1)}, f32[2,128,128]{2,1,0:T(8,128)S(1)}, u32[]{:S(2)}, u32[]{:S(2)}) collective-permute-start(f32[2,128,128]{2,1,0:T(8,128)S(1)} %collective-permute-done.6.fifth), channel_id=1, source_target_pairs={{0,1},{1,0},{2,3},{3,2},{4,5},{5,4},{6,7},{7,6},{8,9},{9,8},{10,11... | collective-permute-start | bytes 393224 | tf_op jit(solution)/shard_map/ppermute | solution.py:415
  50.2 2.8 %collective-permute-start.11 = (f32[2,128,128]{2,1,0:T(8,128)S(1)}, f32[2,128,128]{2,1,0:T(8,128)S(1)}, u32[]{:S(2)}, u32[]{:S(2)}) collective-permute-start(f32[2,128,128]{2,1,0:T(8,128)S(1)} %collective-permute-done.8.alone), channel_id=1, source_target_pairs={{0,1},{1,0},{2,3},{3,2},{4,5},{5,4},{6,7},{7,6},{8,9},{9,8},{10,11... | collective-permute-start | bytes 393224 | tf_op jit(solution)/shard_map/ppermute | solution.py:416
  51.7 3.9 %collective-permute-start.9 = (f32[2,128,128]{2,1,0:T(8,128)S(1)}, f32[2,128,128]{2,1,0:T(8,128)S(1)}, u32[]{:S(2)}, u32[]{:S(2)}) collective-permute-start(f32[2,128,128]{2,1,0:T(8,128)S(1)} %get-tuple-element.152), channel_id=1, source_target_pairs={{0,192},{1,3},{2,194},{3,1},{4,196},{5,7},{6,198},{7,5},{8,200},{9... | collective-permute-start | bytes 393224 | tf_op jit(solution)/shard_map/ppermute | solution.py:397
  55.6 4.4 %collective-permute-start.12 = (f32[2,128,128]{2,1,0:T(8,128)S(1)}, f32[2,128,128]{2,1,0:T(8,128)S(1)}, u32[]{:S(2)}, u32[]{:S(2)}) collective-permute-start(f32[2,128,128]{2,1,0:T(8,128)S(1)} %get-tuple-element.150), channel_id=1, source_target_pairs={{0,1},{1,0},{2,3},{3,2},{4,5},{5,4},{6,7},{7,6},{8,9},{9,8},{10,11... | collective-permute-start | bytes 393224 | tf_op jit(solution)/shard_map/ppermute | solution.py:441
